TPU v7x, 32 devices: a whole 2x2x4 slice. The times are simulated.
32 devices in a mesh: ctx: 16 (over z, y, core), wsh: 2 (over x).
Axes of the slice: x: 2, y: 2, z: 4, core: 2. Of those that a mesh axis runs over, the one named last changes fastest.
Arguments:
- tokens: bfloat16 [2, 4096, 1472], P('wsh', 'ctx'), may hold values from -6 to 6
- lengths: int32 [2, 1], P('wsh'), may hold values from 1024 to 4096, as said below
- buckets: int32 [255], replicated, may hold values from 0 to 31, as said below
- attention_gain: bfloat16 [1472], P('wsh'), may hold values from 0.5 to 1.5
- query_weight: bfloat16 [1472, 384], P('wsh'), may hold values from -0.078125 to 0.078125
- key_weight: bfloat16 [1472, 384], P('wsh'), may hold values from -0.078125 to 0.078125
- value_weight: bfloat16 [1472, 384], P('wsh'), may hold values from -0.15625 to 0.15625
- output_weight: bfloat16 [384, 1472], P(None, 'wsh'), may hold values from -2.5 to 2.5
- bias_table: bfloat16 [32, 6], P('wsh'), may hold values from -3 to 3
- feed_gain: bfloat16 [1472], P('wsh'), may hold values from 0.5 to 1.5
- gate_weight: bfloat16 [1472, 3584], P(None, 'wsh'), may hold values from -0.15625 to 0.15625
- up_weight: bfloat16 [1472, 3584], P(None, 'wsh'), may hold values from -0.15625 to 0.15625
- down_weight: bfloat16 [3584, 1472], P('wsh'), may hold values from -0.09375 to 0.09375
- cotangent: bfloat16 [2, 4096, 1472], P('wsh', 'ctx'), may hold values from -6 to 6
Outputs:
- result: bfloat16 [2, 4096, 1472], P('wsh', 'ctx')
- input_gradient: bfloat16 [2, 4096, 1472], P('wsh', 'ctx')
- attention_gain_gradient: float32 [1472], P('wsh')
- query_gradient: float32 [1472, 384], P('wsh', 'ctx')
- key_gradient: float32 [1472, 384], P('wsh', 'ctx')
- value_gradient: float32 [1472, 384], P('wsh', 'ctx')
- output_gradient: float32 [384, 1472], P('ctx', 'wsh')
- bias_gradient: float32 [32, 6], P('wsh')
- feed_gain_gradient: float32 [1472], P('wsh')
- gate_gradient: float32 [1472, 3584], P(None, ('ctx', 'wsh'))
- up_gradient: float32 [1472, 3584], P(None, ('ctx', 'wsh'))
- down_gradient: float32 [3584, 1472], P(('ctx', 'wsh'))
Inputs may be any that keep to these rules, and one draw needn't show every extreme that they name: `lengths`: every sequence has 1024 or more live tokens; in every draw one sequence has all 4096. Offsets j - i <= 0 map into buckets below 16, offsets above 0 into the upper half.
All inputs are finite; a program needn't handle non-finite values.
Results may differ from a plain program's by a relative error of at most 0.02.
Values may be sent and summed in bfloat16 or wider, within the bound.
No kernel may reach another device: no remote copies, remote signals or barrier semaphores. Data moves between devices by JAX's collectives and lax.ppermute only.
A program may use at most 256 MiB of HBM per device.

v0:
```python
import jax
import jax.numpy as jnp
from jax import lax
from jax.sharding import PartitionSpec as P

EPSILON = 1e-06
MASKED = -1e30
HIGH = lax.Precision.HIGHEST


def shifted(block, axis, distance):
    devices = range(lax.axis_size(axis))
    route = [((i - distance) % len(devices), i) for i in devices]
    return lax.ppermute(block, axis, route)


def row_scale(values):
    return lax.rsqrt(jnp.mean(values * values, axis=-1, keepdims=True) + EPSILON)


def normalize(values, gain):
    return values * row_scale(values) * gain


def skew_expand(offset_bias, length):
    count = offset_bias.shape[0]
    padded = jnp.pad(offset_bias, ((0, 0), (0, 1)))
    tiled = jnp.tile(padded, (1, length))[:, : length * (2 * length - 1)]
    return tiled.reshape(count, length, 2 * length - 1)[:, :, length - 1 :]


def diagonal_sums(grid, length):
    count = grid.shape[0]
    wide = jnp.pad(grid, ((0, 0), (0, 0), (length - 1, 0))).reshape(
        count, length * (2 * length - 1)
    )
    wide = jnp.pad(wide, ((0, 0), (0, length)))
    return jnp.sum(wide.reshape(count, length, 2 * length), axis=1)[:, : 2 * length - 1]


def bucket_onehot(offset_start, length, buckets, bucket_count):
    reach = (buckets.shape[0] + 1) // 2
    offsets = offset_start + jnp.arange(2 * length - 1, dtype=jnp.int32) - (length - 1)
    spots = jnp.clip(offsets, 1 - reach, reach - 1) + (reach - 1)
    table_spots = jnp.arange(buckets.shape[0], dtype=jnp.int32)
    chosen = jnp.sum(jnp.where(spots[:, None] == table_spots[None, :], buckets[None, :], 0), axis=1)
    return chosen[:, None] == jnp.arange(bucket_count, dtype=jnp.int32)[None, :]


def block_scores(query3, keys3, table, onehot, key_live, length):
    scores = jnp.einsum("ihd,jhd->hij", query3, keys3, preferred_element_type=jnp.float32)
    offset_bias = jnp.einsum(
        "ob,bh->ho", onehot.astype(jnp.bfloat16), table, preferred_element_type=jnp.float32
    )
    scores = scores + skew_expand(offset_bias, length)
    return jnp.where(key_live[None, None, :], scores, MASKED)


def body(
    tokens,
    lengths,
    buckets,
    attention_gain,
    query_weight,
    key_weight,
    value_weight,
    output_weight,
    bias_table,
    feed_gain,
    gate_weight,
    up_weight,
    down_weight,
    cotangent,
):
    (
        gain_first,
        query_full,
        key_full,
        value_full,
        output_full,
        table_full,
        gain_second,
        gate_full,
        up_full,
        down_full,
    ) = (
        lax.all_gather(attention_gain, "wsh", axis=0, tiled=True),
        lax.all_gather(query_weight, "wsh", axis=0, tiled=True),
        lax.all_gather(key_weight, "wsh", axis=0, tiled=True),
        lax.all_gather(value_weight, "wsh", axis=0, tiled=True),
        lax.all_gather(output_weight, "wsh", axis=1, tiled=True),
        lax.all_gather(bias_table, "wsh", axis=0, tiled=True),
        lax.all_gather(feed_gain, "wsh", axis=0, tiled=True),
        lax.all_gather(gate_weight, "wsh", axis=1, tiled=True),
        lax.all_gather(up_weight, "wsh", axis=1, tiled=True),
        lax.all_gather(down_weight, "wsh", axis=0, tiled=True),
    )
    length = tokens.shape[1]
    heads = table_full.shape[1]
    bucket_count = table_full.shape[0]
    inner = query_full.shape[1]
    head_size = inner // heads
    seq_count = lengths.shape[1]
    wide_count = lax.axis_size("ctx")
    span = wide_count // seq_count
    here = lax.axis_index("ctx")
    my_seq = here % seq_count
    my_block = here // seq_count
    seq_pick = jnp.arange(seq_count, dtype=jnp.int32) == my_seq
    my_length = jnp.sum(jnp.where(seq_pick, lengths[0], 0))
    positions = jnp.arange(length, dtype=jnp.int32)
    live = (my_block * length + positions < my_length).astype(jnp.float32)[:, None]
    inputs = tokens[0].astype(jnp.float32)
    gain_one = gain_first.astype(jnp.float32)
    first = normalize(inputs, gain_one).astype(jnp.bfloat16)
    query = jnp.dot(first, query_full, preferred_element_type=jnp.float32).astype(jnp.bfloat16)
    keys = jnp.dot(first, key_full, preferred_element_type=jnp.float32).astype(jnp.bfloat16)
    values = jnp.dot(first, value_full, preferred_element_type=jnp.float32).astype(jnp.bfloat16)
    query3 = query.reshape(length, heads, head_size)

    def forward_step(carry, block_keys, block_values, key_block):
        run_max, run_total, running = carry
        onehot = bucket_onehot((key_block - my_block) * length, length, buckets, bucket_count)
        key_live = key_block * length + positions < my_length
        scores = block_scores(
            query3,
            block_keys.reshape(length, heads, head_size),
            table_full,
            onehot,
            key_live,
            length,
        )
        new_max = jnp.maximum(run_max, jnp.max(scores, axis=2))
        weights = jnp.exp(scores - new_max[:, :, None])
        factor = jnp.exp(run_max - new_max)
        run_total = run_total * factor + jnp.sum(weights, axis=2)
        update = jnp.einsum(
            "hij,jhd->ihd",
            weights.astype(jnp.bfloat16),
            block_values.reshape(length, heads, head_size),
            preferred_element_type=jnp.float32,
        )
        running = running * jnp.transpose(factor)[:, :, None] + update
        return (new_max, run_total, running)

    start_carry = (
        jnp.full((heads, length), MASKED, jnp.float32),
        jnp.zeros((heads, length), jnp.float32),
        jnp.zeros((length, heads, head_size), jnp.float32),
    )
    start_carry = forward_step(start_carry, keys, values, my_block)
    stored = ()

    def cycle_turn(turn, state):
        carry, block_keys, block_values, stored_blocks = state
        block_keys, block_values = shifted((block_keys, block_values), "ctx", seq_count)
        carry = forward_step(carry, block_keys, block_values, (my_block - turn) % span)
        return (carry, block_keys, block_values, stored_blocks)

    (run_max, run_total, running), _, _, stored = lax.fori_loop(
        1, span, cycle_turn, (start_carry, keys, values, stored)
    )
    log_total = run_max + jnp.log(run_total)
    attention = (running / jnp.transpose(run_total)[:, :, None]).reshape(length, inner)
    attention_low = attention.astype(jnp.bfloat16)
    branch = jnp.dot(attention_low, output_full, preferred_element_type=jnp.float32)
    middle = inputs + live * branch
    gain_two = gain_second.astype(jnp.float32)
    second = normalize(middle, gain_two).astype(jnp.bfloat16)
    gate = jnp.dot(second, gate_full, preferred_element_type=jnp.float32)
    up = jnp.dot(second, up_full, preferred_element_type=jnp.float32)
    hidden = (jax.nn.gelu(gate, approximate=True) * up).astype(jnp.bfloat16)
    feed = jnp.dot(hidden, down_full, preferred_element_type=jnp.float32)
    result = (middle + live * feed).astype(jnp.bfloat16)
    outer = live * cotangent[0].astype(jnp.float32)
    outer_low = outer.astype(jnp.bfloat16)
    down_grad = jnp.einsum("tf,td->fd", hidden, outer_low, preferred_element_type=jnp.float32)
    hidden_grad = jnp.einsum("td,fd->tf", outer_low, down_full, preferred_element_type=jnp.float32)

    def gated(gate_in, up_in):
        return jax.nn.gelu(gate_in, approximate=True) * up_in

    _, gate_pull = jax.vjp(gated, gate, up)
    gate_back, up_back = gate_pull(hidden_grad)
    gate_low = gate_back.astype(jnp.bfloat16)
    up_low = up_back.astype(jnp.bfloat16)
    gate_grad = jnp.einsum("td,tf->df", second, gate_low, preferred_element_type=jnp.float32)
    up_grad = jnp.einsum("td,tf->df", second, up_low, preferred_element_type=jnp.float32)
    second_grad = jnp.einsum(
        "tf,df->td", gate_low, gate_full, preferred_element_type=jnp.float32
    ) + jnp.einsum("tf,df->td", up_low, up_full, preferred_element_type=jnp.float32)
    _, norm_pull = jax.vjp(normalize, middle, gain_two)
    middle_back, gain_two_grad = norm_pull(second_grad)
    middle_grad = outer + middle_back
    branch_low = (live * middle_grad).astype(jnp.bfloat16)
    output_grad = jnp.einsum(
        "ti,td->id", attention_low, branch_low, preferred_element_type=jnp.float32
    )
    attention_grad = jnp.einsum(
        "td,id->ti", branch_low, output_full, preferred_element_type=jnp.float32
    ).astype(jnp.bfloat16)
    attention_grad3 = attention_grad.reshape(length, heads, head_size)
    delta = jnp.transpose(
        jnp.sum(
            (attention_grad.astype(jnp.float32) * attention).reshape(length, heads, head_size),
            axis=2,
        )
    )

    def backward_step(block_keys, block_values, key_block):
        keys3 = block_keys.reshape(length, heads, head_size)
        values3 = block_values.reshape(length, heads, head_size)
        onehot = bucket_onehot((key_block - my_block) * length, length, buckets, bucket_count)
        key_live = key_block * length + positions < my_length
        scores = block_scores(query3, keys3, table_full, onehot, key_live, length)
        probs = jnp.exp(scores - log_total[:, :, None])
        prob_grad = jnp.einsum(
            "ihd,jhd->hij", attention_grad3, values3, preferred_element_type=jnp.float32
        )
        score_grad = (probs * (prob_grad - delta[:, :, None])).astype(jnp.bfloat16)
        part_query = jnp.einsum(
            "hij,jhd->ihd", score_grad, keys3, preferred_element_type=jnp.float32
        )
        part_keys = jnp.einsum(
            "hij,ihd->jhd", score_grad, query3, preferred_element_type=jnp.float32
        )
        part_values = jnp.einsum(
            "hij,ihd->jhd",
            probs.astype(jnp.bfloat16),
            attention_grad3,
            preferred_element_type=jnp.float32,
        )
        part_table = jnp.einsum(
            "ho,ob->bh",
            diagonal_sums(score_grad.astype(jnp.float32), length),
            onehot.astype(jnp.float32),
            precision=HIGH,
        )
        return (
            part_query.reshape(length, inner),
            part_keys.reshape(length, inner),
            part_values.reshape(length, inner),
            part_table,
        )

    def back_turn(turn, state):
        block_keys, block_values, keys_sum, values_sum, query_sum, table_sum = state
        part_query, part_keys, part_values, part_table = backward_step(
            block_keys, block_values, (my_block - turn) % span
        )
        keys_next = keys_sum + part_keys
        values_next = values_sum + part_values
        keys_sum, values_sum = (
            shifted(keys_next.astype(jnp.bfloat16), "ctx", seq_count).astype(keys_next.dtype),
            shifted(values_next.astype(jnp.bfloat16), "ctx", seq_count).astype(values_next.dtype),
        )
        block_keys, block_values = shifted((block_keys, block_values), "ctx", seq_count)
        return (
            block_keys,
            block_values,
            keys_sum,
            values_sum,
            query_sum + part_query,
            table_sum + part_table,
        )

    zeros_rows = jnp.zeros((length, inner), jnp.float32)
    back_state = (
        keys,
        values,
        zeros_rows,
        zeros_rows,
        zeros_rows,
        jnp.zeros((bucket_count, heads), jnp.float32),
    )
    _, _, keys_sum, values_sum, query_sum, table_grad = lax.fori_loop(
        0, span, back_turn, back_state
    )
    query_low = query_sum.astype(jnp.bfloat16)
    keys_low = keys_sum.astype(jnp.bfloat16)
    values_low = values_sum.astype(jnp.bfloat16)
    query_grad = jnp.einsum("td,ti->di", first, query_low, preferred_element_type=jnp.float32)
    key_grad = jnp.einsum("td,ti->di", first, keys_low, preferred_element_type=jnp.float32)
    value_grad = jnp.einsum("td,ti->di", first, values_low, preferred_element_type=jnp.float32)
    first_grad = (
        jnp.einsum("ti,di->td", query_low, query_full, preferred_element_type=jnp.float32)
        + jnp.einsum("ti,di->td", keys_low, key_full, preferred_element_type=jnp.float32)
        + jnp.einsum("ti,di->td", values_low, value_full, preferred_element_type=jnp.float32)
    )
    _, first_pull = jax.vjp(normalize, inputs, gain_one)
    inputs_back, gain_one_grad = first_pull(first_grad)
    input_gradient = (middle_grad + inputs_back).astype(jnp.bfloat16)
    small = lax.psum((gain_one_grad, table_grad, gain_two_grad), "ctx")
    wide = (
        lax.psum_scatter(query_grad, "ctx", scatter_dimension=1, tiled=True),
        lax.psum_scatter(key_grad, "ctx", scatter_dimension=1, tiled=True),
        lax.psum_scatter(value_grad, "ctx", scatter_dimension=1, tiled=True),
        lax.psum_scatter(output_grad, "ctx", scatter_dimension=0, tiled=True),
        lax.psum_scatter(gate_grad, "ctx", scatter_dimension=1, tiled=True),
        lax.psum_scatter(up_grad, "ctx", scatter_dimension=1, tiled=True),
        lax.psum_scatter(down_grad, "ctx", scatter_dimension=0, tiled=True),
    )
    final = (
        lax.psum_scatter(
            small[0].astype(jnp.bfloat16), "wsh", scatter_dimension=0, tiled=True
        ).astype(jnp.float32),
        lax.psum_scatter(
            small[1].astype(jnp.bfloat16), "wsh", scatter_dimension=0, tiled=True
        ).astype(jnp.float32),
        lax.psum_scatter(
            small[2].astype(jnp.bfloat16), "wsh", scatter_dimension=0, tiled=True
        ).astype(jnp.float32),
        lax.psum_scatter(
            wide[0].astype(jnp.bfloat16), "wsh", scatter_dimension=0, tiled=True
        ).astype(jnp.float32),
        lax.psum_scatter(
            wide[1].astype(jnp.bfloat16), "wsh", scatter_dimension=0, tiled=True
        ).astype(jnp.float32),
        lax.psum_scatter(
            wide[2].astype(jnp.bfloat16), "wsh", scatter_dimension=0, tiled=True
        ).astype(jnp.float32),
        lax.psum_scatter(
            wide[3].astype(jnp.bfloat16), "wsh", scatter_dimension=1, tiled=True
        ).astype(jnp.float32),
        lax.psum_scatter(
            wide[4].astype(jnp.bfloat16), "wsh", scatter_dimension=1, tiled=True
        ).astype(jnp.float32),
        lax.psum_scatter(
            wide[5].astype(jnp.bfloat16), "wsh", scatter_dimension=1, tiled=True
        ).astype(jnp.float32),
        lax.psum_scatter(
            wide[6].astype(jnp.bfloat16), "wsh", scatter_dimension=0, tiled=True
        ).astype(jnp.float32),
    )
    gain_one_out, table_out, gain_two_out = (final[0], final[1], final[2])
    query_out, key_out, value_out, output_out = (final[3], final[4], final[5], final[6])
    gate_out, up_out, down_out = (final[7], final[8], final[9])
    return (
        result[None],
        input_gradient[None],
        gain_one_out,
        query_out,
        key_out,
        value_out,
        output_out,
        table_out,
        gain_two_out,
        gate_out,
        up_out,
        down_out,
    )


def solution(mesh):
    placed = (
        P("wsh", "ctx", None),
        P("wsh", None),
        P(),
        P("wsh"),
        P("wsh", None),
        P("wsh", None),
        P("wsh", None),
        P(None, "wsh"),
        P("wsh", None),
        P("wsh"),
        P(None, "wsh"),
        P(None, "wsh"),
        P("wsh", None),
        P("wsh", "ctx", None),
    )
    return jax.shard_map(
        body,
        mesh=mesh,
        in_specs=placed,
        out_specs=(
            P("wsh", "ctx", None),
            P("wsh", "ctx", None),
            P("wsh"),
            P("wsh", "ctx"),
            P("wsh", "ctx"),
            P("wsh", "ctx"),
            P("ctx", "wsh"),
            P("wsh", None),
            P("wsh"),
            P(None, ("ctx", "wsh")),
            P(None, ("ctx", "wsh")),
            P(("ctx", "wsh"), None),
        ),
        check_vma=False,
    )
```

profile of v0, /device:TPU:0, one launch (start us, length us, event | category | flops | bytes accessed | tf_op | source)
XLA Modules:
  0.0 2166.0 jit_solution(2266062317483967884)
XLA Ops:
  12.0 5.2 all-gather
  22.4 4.8 reshape.279
  33.7 5.2 all-reduce.11
  43.6 14.7 all-gather.11.cloned.1.call-done
  65.3 16.8 all-gather.13.cloned.1.call-done
  89.0 317.9 %while.50 = (s32[]{:T(128)}, f32[6,256]{1,0:T(8,128)S(1)}, f32[6,256]{1,0:T(8,128)S(1)}, f32[256,6,64]{0,2,1:T(8,128)}, bf16[256,384]{0,1:T(8,128)(2,1)}, /*inde...) while((s32[]{:T(128)}, f32[6,256]{1,0:T(8,128)S(1)}, ...), condition=%wide.region_8.9_spmd.clone, body=%wide.region_4.8_spmd.clone.sunk | while | flops 104222576 | bytes 41623364 | solution.py:160
  95.8 4.8 reshape.332
  117.2 5.7 reshape.332
  139.4 4.8 reshape.332
  160.4 4.8 reshape.332
  181.5 4.8 reshape.332
  202.5 4.8 reshape.332
  223.6 4.8 reshape.332
  243.6 5.4 reshape.332
  265.4 4.8 reshape.332
  286.4 4.8 reshape.332
  307.5 4.8 reshape.332
  328.5 4.8 reshape.332
  349.6 4.8 reshape.332
  370.6 4.8 reshape.332
  392.2 4.8 reshape.332
  411.8 9.1 fusion.83
  421.0 9.1 fusion.84
  430.0 71.0 %all-gather.21.cloned.1.call-done = bf16[3584,1472]{0,1:T(8,128)(2,1)} async-done(((bf16[1792,1472]{0,1:T(8,128)(2,1)}), bf16[3584,1472]{0,1:T(8,128)(2,1)}) %all-gather.21.cloned.1.call-update) | async-done | bytes 10551312 | tf_op jit(solution)/shard_map/all_gather | solution.py:96
  501.1 12.1 multiply_convert_fusion.1
  513.2 7.0 fusion.85
  520.3 4.1 multiply_reduce_fusion
  528.0 569.6 %while.51 = (s32[]{:T(128)}, bf16[256,384]{0,1:T(8,128)(2,1)}, bf16[256,384]{0,1:T(8,128)(2,1)}, f32[256,384]{0,1:T(8,128)}, f32[256,384]{0,1:T(8,128)}, /*index...) while((s32[]{:T(128)}, bf16[256,384]{0,1:T(8,128)(2,1)}, ...), condition=%wide.region_15.16_spmd.clone, body=%wide.region_12.15_spmd.clone.sunk | while | flops 258763216 | bytes 65157164 | solution.py:276
  538.8 4.8 reshape.334
  550.9 4.0 reshape.335
  574.6 4.8 reshape.334
  610.4 4.8 reshape.334
  646.2 4.8 reshape.334
  681.1 4.8 reshape.334
  716.9 4.8 reshape.334
  752.7 4.8 reshape.334
  788.6 4.8 reshape.334
  823.4 4.8 reshape.334
  859.2 4.8 reshape.334
  895.0 4.8 reshape.334
  930.9 4.8 reshape.334
  965.7 4.8 reshape.334
  1001.5 4.8 reshape.334
  1037.4 4.8 reshape.334
  1073.2 4.8 reshape.334
  1111.8 10.9 fusion.86
  1122.8 10.9 fusion.87
  1134.8 10.8 fusion.49
  1151.8 61.6 %all-reduce.9 = (bf16[1472]{0:T(1024)(128)(2,1)S(1)}, bf16[32,6]{0,1:T(8,128)(2,1)S(1)}, bf16[1472]{0:T(1024)(128)(2,1)S(1)}) all-reduce(f32[1472]{0:T(1024)S(1)} %get-tuple-element.870, f32[32,6]{0,1:T(8,128)S(1)} %copy-done.47, f32[1472]{0:T(1024)S(1)} %copy-done.44), channel_id=1, replica_groups=mesh['ctx'=16,'wsh'=2] {'ctx'}, use_global_device_ids=true, to_apply=%region_18.19 | all-reduce | flops 3136 | bytes 18816 | tf_op jit(solution)/shard_map/psum | solution.py:293
  1216.2 14.2 reduce-scatter.28.cloned.1.call-done
  1232.3 63.7 %reduce-scatter.30.cloned.1.call-done = f32[1472,24]{0,1:T(8,128)} async-done(((f32[1472,384]{0,1:T(8,128)}), f32[1472,24]{0,1:T(8,128)}) %reduce-scatter.30.cloned.1.call-update) | async-done | bytes 141328 | tf_op jit(solution)/shard_map/reduce_scatter | solution.py:297
  1297.9 64.4 %reduce-scatter.32.cloned.1.call-done = f32[24,1472]{1,0:T(8,128)} async-done(((f32[384,1472]{1,0:T(8,128)}), f32[24,1472]{1,0:T(8,128)}) %reduce-scatter.32.cloned.1.call-update) | async-done | bytes 141328 | tf_op jit(solution)/shard_map/reduce_scatter | solution.py:298
  1364.2 219.8 %reduce-scatter.34.cloned.1.call-done = f32[1472,224]{0,1:T(8,128)} async-done(((f32[1472,3584]{0,1:T(8,128)}), f32[1472,224]{0,1:T(8,128)}) %reduce-scatter.34.cloned.1.call-update) | async-done | bytes 1318928 | tf_op jit(solution)/shard_map/reduce_scatter | solution.py:299
  1586.3 219.6 %reduce-scatter.38.cloned.1.call-done = f32[1472,224]{0,1:T(8,128)} async-done(((f32[1472,3584]{0,1:T(8,128)}), f32[1472,224]{0,1:T(8,128)}) %reduce-scatter.38.cloned.1.call-update) | async-done | bytes 1318928 | tf_op jit(solution)/shard_map/reduce_scatter | solution.py:300
  1808.8 218.8 %reduce-scatter.42.cloned.1.call-done = f32[224,1472]{1,0:T(8,128)} async-done(((f32[3584,1472]{1,0:T(8,128)}), f32[224,1472]{1,0:T(8,128)}) %reduce-scatter.42.cloned.1.call-update) | async-done | bytes 1318928 | tf_op jit(solution)/shard_map/reduce_scatter | solution.py:301
  2032.6 5.2 all-reduce.10
  2038.5 8.7 fusion.32
  2048.6 6.1 reduce-scatter.46.cloned.1.call-done
  2056.4 13.4 reduce-scatter.48.cloned.1.call-done
  2071.4 13.4 reduce-scatter.50.cloned.1.call-done
  2086.5 13.5 reduce-scatter.52.cloned.1.call-done
  2101.7 17.4 reduce-scatter.36.cloned.1.call-done
  2121.0 17.3 reduce-scatter.40.cloned.1.call-done
  2140.2 16.8 reduce-scatter.44.cloned.1.call-done
  (1507 shorter events, 823.8 us)
Async XLA Ops:
  7.2 33.8 %all-gather.9.cloned.1.call-start = ((), (), s32[]{:S(2)}) async-start(), calls=%async_computation.15 | async-start | bytes 1695744 | tf_op jit(solution)/shard_map/all_gather | solution.py:88
  7.9 50.4 %all-gather.11.cloned.1.call-start = ((), (), s32[]{:S(2)}) async-start(), calls=%async_computation.16 | async-start | bytes 1695744 | tf_op jit(solution)/shard_map/all_gather | solution.py:89
  8.7 73.5 %all-gather.13.cloned.1.call-start = ((), (), s32[]{:S(2)}) async-start(), calls=%async_computation.17 | async-start | bytes 1695744 | tf_op jit(solution)/shard_map/all_gather | solution.py:90
  9.4 399.5 %all-gather.15.cloned.1.call-start = ((), (), s32[]{:S(2)}) async-start(), calls=%async_computation.18 | async-start | bytes 1695744 | tf_op jit(solution)/shard_map/all_gather | solution.py:91
  10.0 401.8 %all-gather.17.cloned.1.call-start = ((), (), s32[]{:S(2)}) async-start(), calls=%async_computation.19 | async-start | bytes 15826944 | tf_op jit(solution)/shard_map/all_gather | solution.py:94
  10.6 410.4 %all-gather.19.cloned.1.call-start = ((), (), s32[]{:S(2)}) async-start(), calls=%async_computation.20 | async-start | bytes 15826944 | tf_op jit(solution)/shard_map/all_gather | solution.py:95
  11.2 489.9 %all-gather.21.cloned.1.call-start = ((), (), s32[]{:S(2)}) async-start(), calls=%async_computation.21 | async-start | bytes 15826944 | tf_op jit(solution)/shard_map/all_gather | solution.py:96
  11.9 1202.3 %reduce-scatter.26.cloned.1.call-start = ((), (), s32[]{:S(2)}) async-start(), calls=%async_computation.22 | async-start | bytes 2506752 | tf_op jit(solution)/shard_map/reduce_scatter | solution.py:295
  89.0 17.4 collective-permute-start.1
  110.1 18.8 collective-permute-start.1
  132.7 17.3 collective-permute-start.1
  174.8 17.3 collective-permute-start.1
  195.8 17.3 collective-permute-start.1
  216.9 17.3 collective-permute-start.1
  300.8 17.3 collective-permute-start.1
  342.9 17.3 collective-permute-start.1
  363.9 17.7 collective-permute-start.1
  385.5 17.4 collective-permute-start.1
  529.1 34.9 %collective-permute-start.2 = (bf16[256,384]{0,1:T(8,128)(2,1)S(1)}, bf16[256,384]{0,1:T(8,128)(2,1)}, u32[]{:S(2)}, u32[]{:S(2)}) collective-permute-start(bf16[256,384]{0,1:T(8,128)(2,1)S(1)} %copy.139), channel_id=1, source_target_pairs={{30,0},{0,2},{2,4},{4,6},{6,8},{8,10},{10,12},{12,14},{14,16},{16,... | collective-permute-start | bytes 589832 | tf_op jit(solution)/shard_map/while/body/eval_jaxpr/ppermute | solution.py:14
  530.7 33.2 %collective-permute-start.3 = (bf16[256,384]{0,1:T(8,128)(2,1)}, bf16[256,384]{0,1:T(8,128)(2,1)}, u32[]{:S(2)}, u32[]{:S(2)}) collective-permute-start(bf16[256,384]{0,1:T(8,128)(2,1)} %copy.140), channel_id=1, source_target_pairs={{30,0},{0,2},{2,4},{4,6},{6,8},{8,10},{10,12},{12,14},{14,16},{16,... | collective-permute-start | bytes 589832 | tf_op jit(solution)/shard_map/while/body/eval_jaxpr/ppermute | solution.py:14
  564.9 34.9 %collective-permute-start.2 = (bf16[256,384]{0,1:T(8,128)(2,1)S(1)}, bf16[256,384]{0,1:T(8,128)(2,1)}, u32[]{:S(2)}, u32[]{:S(2)}) collective-permute-start(bf16[256,384]{0,1:T(8,128)(2,1)S(1)} %copy.139), channel_id=1, source_target_pairs={{30,0},{0,2},{2,4},{4,6},{6,8},{8,10},{10,12},{12,14},{14,16},{16,... | collective-permute-start | bytes 589832 | tf_op jit(solution)/shard_map/while/body/eval_jaxpr/ppermute | solution.py:14
  566.5 33.2 %collective-permute-start.3 = (bf16[256,384]{0,1:T(8,128)(2,1)}, bf16[256,384]{0,1:T(8,128)(2,1)}, u32[]{:S(2)}, u32[]{:S(2)}) collective-permute-start(bf16[256,384]{0,1:T(8,128)(2,1)} %copy.140), channel_id=1, source_target_pairs={{30,0},{0,2},{2,4},{4,6},{6,8},{8,10},{10,12},{12,14},{14,16},{16,... | collective-permute-start | bytes 589832 | tf_op jit(solution)/shard_map/while/body/eval_jaxpr/ppermute | solution.py:14
  600.7 34.9 %collective-permute-start.2 = (bf16[256,384]{0,1:T(8,128)(2,1)S(1)}, bf16[256,384]{0,1:T(8,128)(2,1)}, u32[]{:S(2)}, u32[]{:S(2)}) collective-permute-start(bf16[256,384]{0,1:T(8,128)(2,1)S(1)} %copy.139), channel_id=1, source_target_pairs={{30,0},{0,2},{2,4},{4,6},{6,8},{8,10},{10,12},{12,14},{14,16},{16,... | collective-permute-start | bytes 589832 | tf_op jit(solution)/shard_map/while/body/eval_jaxpr/ppermute | solution.py:14
  602.4 33.2 %collective-permute-start.3 = (bf16[256,384]{0,1:T(8,128)(2,1)}, bf16[256,384]{0,1:T(8,128)(2,1)}, u32[]{:S(2)}, u32[]{:S(2)}) collective-permute-start(bf16[256,384]{0,1:T(8,128)(2,1)} %copy.140), channel_id=1, source_target_pairs={{30,0},{0,2},{2,4},{4,6},{6,8},{8,10},{10,12},{12,14},{14,16},{16,... | collective-permute-start | bytes 589832 | tf_op jit(solution)/shard_map/while/body/eval_jaxpr/ppermute | solution.py:14
  636.5 33.9 %collective-permute-start.2 = (bf16[256,384]{0,1:T(8,128)(2,1)S(1)}, bf16[256,384]{0,1:T(8,128)(2,1)}, u32[]{:S(2)}, u32[]{:S(2)}) collective-permute-start(bf16[256,384]{0,1:T(8,128)(2,1)S(1)} %copy.139), channel_id=1, source_target_pairs={{30,0},{0,2},{2,4},{4,6},{6,8},{8,10},{10,12},{12,14},{14,16},{16,... | collective-permute-start | bytes 589832 | tf_op jit(solution)/shard_map/while/body/eval_jaxpr/ppermute | solution.py:14
  638.2 32.2 %collective-permute-start.3 = (bf16[256,384]{0,1:T(8,128)(2,1)}, bf16[256,384]{0,1:T(8,128)(2,1)}, u32[]{:S(2)}, u32[]{:S(2)}) collective-permute-start(bf16[256,384]{0,1:T(8,128)(2,1)} %copy.140), channel_id=1, source_target_pairs={{30,0},{0,2},{2,4},{4,6},{6,8},{8,10},{10,12},{12,14},{14,16},{16,... | collective-permute-start | bytes 589832 | tf_op jit(solution)/shard_map/while/body/eval_jaxpr/ppermute | solution.py:14
  671.4 34.9 %collective-permute-start.2 = (bf16[256,384]{0,1:T(8,128)(2,1)S(1)}, bf16[256,384]{0,1:T(8,128)(2,1)}, u32[]{:S(2)}, u32[]{:S(2)}) collective-permute-start(bf16[256,384]{0,1:T(8,128)(2,1)S(1)} %copy.139), channel_id=1, source_target_pairs={{30,0},{0,2},{2,4},{4,6},{6,8},{8,10},{10,12},{12,14},{14,16},{16,... | collective-permute-start | bytes 589832 | tf_op jit(solution)/shard_map/while/body/eval_jaxpr/ppermute | solution.py:14
  673.0 33.2 %collective-permute-start.3 = (bf16[256,384]{0,1:T(8,128)(2,1)}, bf16[256,384]{0,1:T(8,128)(2,1)}, u32[]{:S(2)}, u32[]{:S(2)}) collective-permute-start(bf16[256,384]{0,1:T(8,128)(2,1)} %copy.140), channel_id=1, source_target_pairs={{30,0},{0,2},{2,4},{4,6},{6,8},{8,10},{10,12},{12,14},{14,16},{16,... | collective-permute-start | bytes 589832 | tf_op jit(solution)/shard_map/while/body/eval_jaxpr/ppermute | solution.py:14
  707.2 34.9 %collective-permute-start.2 = (bf16[256,384]{0,1:T(8,128)(2,1)S(1)}, bf16[256,384]{0,1:T(8,128)(2,1)}, u32[]{:S(2)}, u32[]{:S(2)}) collective-permute-start(bf16[256,384]{0,1:T(8,128)(2,1)S(1)} %copy.139), channel_id=1, source_target_pairs={{30,0},{0,2},{2,4},{4,6},{6,8},{8,10},{10,12},{12,14},{14,16},{16,... | collective-permute-start | bytes 589832 | tf_op jit(solution)/shard_map/while/body/eval_jaxpr/ppermute | solution.py:14
  708.9 33.2 %collective-permute-start.3 = (bf16[256,384]{0,1:T(8,128)(2,1)}, bf16[256,384]{0,1:T(8,128)(2,1)}, u32[]{:S(2)}, u32[]{:S(2)}) collective-permute-start(bf16[256,384]{0,1:T(8,128)(2,1)} %copy.140), channel_id=1, source_target_pairs={{30,0},{0,2},{2,4},{4,6},{6,8},{8,10},{10,12},{12,14},{14,16},{16,... | collective-permute-start | bytes 589832 | tf_op jit(solution)/shard_map/while/body/eval_jaxpr/ppermute | solution.py:14
  743.0 34.9 %collective-permute-start.2 = (bf16[256,384]{0,1:T(8,128)(2,1)S(1)}, bf16[256,384]{0,1:T(8,128)(2,1)}, u32[]{:S(2)}, u32[]{:S(2)}) collective-permute-start(bf16[256,384]{0,1:T(8,128)(2,1)S(1)} %copy.139), channel_id=1, source_target_pairs={{30,0},{0,2},{2,4},{4,6},{6,8},{8,10},{10,12},{12,14},{14,16},{16,... | collective-permute-start | bytes 589832 | tf_op jit(solution)/shard_map/while/body/eval_jaxpr/ppermute | solution.py:14
  744.7 33.2 %collective-permute-start.3 = (bf16[256,384]{0,1:T(8,128)(2,1)}, bf16[256,384]{0,1:T(8,128)(2,1)}, u32[]{:S(2)}, u32[]{:S(2)}) collective-permute-start(bf16[256,384]{0,1:T(8,128)(2,1)} %copy.140), channel_id=1, source_target_pairs={{30,0},{0,2},{2,4},{4,6},{6,8},{8,10},{10,12},{12,14},{14,16},{16,... | collective-permute-start | bytes 589832 | tf_op jit(solution)/shard_map/while/body/eval_jaxpr/ppermute | solution.py:14
  778.8 33.9 %collective-permute-start.2 = (bf16[256,384]{0,1:T(8,128)(2,1)S(1)}, bf16[256,384]{0,1:T(8,128)(2,1)}, u32[]{:S(2)}, u32[]{:S(2)}) collective-permute-start(bf16[256,384]{0,1:T(8,128)(2,1)S(1)} %copy.139), channel_id=1, source_target_pairs={{30,0},{0,2},{2,4},{4,6},{6,8},{8,10},{10,12},{12,14},{14,16},{16,... | collective-permute-start | bytes 589832 | tf_op jit(solution)/shard_map/while/body/eval_jaxpr/ppermute | solution.py:14
  780.5 32.2 %collective-permute-start.3 = (bf16[256,384]{0,1:T(8,128)(2,1)}, bf16[256,384]{0,1:T(8,128)(2,1)}, u32[]{:S(2)}, u32[]{:S(2)}) collective-permute-start(bf16[256,384]{0,1:T(8,128)(2,1)} %copy.140), channel_id=1, source_target_pairs={{30,0},{0,2},{2,4},{4,6},{6,8},{8,10},{10,12},{12,14},{14,16},{16,... | collective-permute-start | bytes 589832 | tf_op jit(solution)/shard_map/while/body/eval_jaxpr/ppermute | solution.py:14
  813.7 34.9 %collective-permute-start.2 = (bf16[256,384]{0,1:T(8,128)(2,1)S(1)}, bf16[256,384]{0,1:T(8,128)(2,1)}, u32[]{:S(2)}, u32[]{:S(2)}) collective-permute-start(bf16[256,384]{0,1:T(8,128)(2,1)S(1)} %copy.139), channel_id=1, source_target_pairs={{30,0},{0,2},{2,4},{4,6},{6,8},{8,10},{10,12},{12,14},{14,16},{16,... | collective-permute-start | bytes 589832 | tf_op jit(solution)/shard_map/while/body/eval_jaxpr/ppermute | solution.py:14
  815.4 33.2 %collective-permute-start.3 = (bf16[256,384]{0,1:T(8,128)(2,1)}, bf16[256,384]{0,1:T(8,128)(2,1)}, u32[]{:S(2)}, u32[]{:S(2)}) collective-permute-start(bf16[256,384]{0,1:T(8,128)(2,1)} %copy.140), channel_id=1, source_target_pairs={{30,0},{0,2},{2,4},{4,6},{6,8},{8,10},{10,12},{12,14},{14,16},{16,... | collective-permute-start | bytes 589832 | tf_op jit(solution)/shard_map/while/body/eval_jaxpr/ppermute | solution.py:14
  849.5 34.9 %collective-permute-start.2 = (bf16[256,384]{0,1:T(8,128)(2,1)S(1)}, bf16[256,384]{0,1:T(8,128)(2,1)}, u32[]{:S(2)}, u32[]{:S(2)}) collective-permute-start(bf16[256,384]{0,1:T(8,128)(2,1)S(1)} %copy.139), channel_id=1, source_target_pairs={{30,0},{0,2},{2,4},{4,6},{6,8},{8,10},{10,12},{12,14},{14,16},{16,... | collective-permute-start | bytes 589832 | tf_op jit(solution)/shard_map/while/body/eval_jaxpr/ppermute | solution.py:14
  851.2 33.2 %collective-permute-start.3 = (bf16[256,384]{0,1:T(8,128)(2,1)}, bf16[256,384]{0,1:T(8,128)(2,1)}, u32[]{:S(2)}, u32[]{:S(2)}) collective-permute-start(bf16[256,384]{0,1:T(8,128)(2,1)} %copy.140), channel_id=1, source_target_pairs={{30,0},{0,2},{2,4},{4,6},{6,8},{8,10},{10,12},{12,14},{14,16},{16,... | collective-permute-start | bytes 589832 | tf_op jit(solution)/shard_map/while/body/eval_jaxpr/ppermute | solution.py:14
  885.3 34.9 %collective-permute-start.2 = (bf16[256,384]{0,1:T(8,128)(2,1)S(1)}, bf16[256,384]{0,1:T(8,128)(2,1)}, u32[]{:S(2)}, u32[]{:S(2)}) collective-permute-start(bf16[256,384]{0,1:T(8,128)(2,1)S(1)} %copy.139), channel_id=1, source_target_pairs={{30,0},{0,2},{2,4},{4,6},{6,8},{8,10},{10,12},{12,14},{14,16},{16,... | collective-permute-start | bytes 589832 | tf_op jit(solution)/shard_map/while/body/eval_jaxpr/ppermute | solution.py:14
  887.0 33.2 %collective-permute-start.3 = (bf16[256,384]{0,1:T(8,128)(2,1)}, bf16[256,384]{0,1:T(8,128)(2,1)}, u32[]{:S(2)}, u32[]{:S(2)}) collective-permute-start(bf16[256,384]{0,1:T(8,128)(2,1)} %copy.140), channel_id=1, source_target_pairs={{30,0},{0,2},{2,4},{4,6},{6,8},{8,10},{10,12},{12,14},{14,16},{16,... | collective-permute-start | bytes 589832 | tf_op jit(solution)/shard_map/while/body/eval_jaxpr/ppermute | solution.py:14
  921.2 33.9 %collective-permute-start.2 = (bf16[256,384]{0,1:T(8,128)(2,1)S(1)}, bf16[256,384]{0,1:T(8,128)(2,1)}, u32[]{:S(2)}, u32[]{:S(2)}) collective-permute-start(bf16[256,384]{0,1:T(8,128)(2,1)S(1)} %copy.139), channel_id=1, source_target_pairs={{30,0},{0,2},{2,4},{4,6},{6,8},{8,10},{10,12},{12,14},{14,16},{16,... | collective-permute-start | bytes 589832 | tf_op jit(solution)/shard_map/while/body/eval_jaxpr/ppermute | solution.py:14
  922.8 32.2 %collective-permute-start.3 = (bf16[256,384]{0,1:T(8,128)(2,1)}, bf16[256,384]{0,1:T(8,128)(2,1)}, u32[]{:S(2)}, u32[]{:S(2)}) collective-permute-start(bf16[256,384]{0,1:T(8,128)(2,1)} %copy.140), channel_id=1, source_target_pairs={{30,0},{0,2},{2,4},{4,6},{6,8},{8,10},{10,12},{12,14},{14,16},{16,... | collective-permute-start | bytes 589832 | tf_op jit(solution)/shard_map/while/body/eval_jaxpr/ppermute | solution.py:14
  956.0 34.9 %collective-permute-start.2 = (bf16[256,384]{0,1:T(8,128)(2,1)S(1)}, bf16[256,384]{0,1:T(8,128)(2,1)}, u32[]{:S(2)}, u32[]{:S(2)}) collective-permute-start(bf16[256,384]{0,1:T(8,128)(2,1)S(1)} %copy.139), channel_id=1, source_target_pairs={{30,0},{0,2},{2,4},{4,6},{6,8},{8,10},{10,12},{12,14},{14,16},{16,... | collective-permute-start | bytes 589832 | tf_op jit(solution)/shard_map/while/body/eval_jaxpr/ppermute | solution.py:14
  957.7 33.2 %collective-permute-start.3 = (bf16[256,384]{0,1:T(8,128)(2,1)}, bf16[256,384]{0,1:T(8,128)(2,1)}, u32[]{:S(2)}, u32[]{:S(2)}) collective-permute-start(bf16[256,384]{0,1:T(8,128)(2,1)} %copy.140), channel_id=1, source_target_pairs={{30,0},{0,2},{2,4},{4,6},{6,8},{8,10},{10,12},{12,14},{14,16},{16,... | collective-permute-start | bytes 589832 | tf_op jit(solution)/shard_map/while/body/eval_jaxpr/ppermute | solution.py:14
  991.8 34.9 %collective-permute-start.2 = (bf16[256,384]{0,1:T(8,128)(2,1)S(1)}, bf16[256,384]{0,1:T(8,128)(2,1)}, u32[]{:S(2)}, u32[]{:S(2)}) collective-permute-start(bf16[256,384]{0,1:T(8,128)(2,1)S(1)} %copy.139), channel_id=1, source_target_pairs={{30,0},{0,2},{2,4},{4,6},{6,8},{8,10},{10,12},{12,14},{14,16},{16,... | collective-permute-start | bytes 589832 | tf_op jit(solution)/shard_map/while/body/eval_jaxpr/ppermute | solution.py:14
  993.5 33.2 %collective-permute-start.3 = (bf16[256,384]{0,1:T(8,128)(2,1)}, bf16[256,384]{0,1:T(8,128)(2,1)}, u32[]{:S(2)}, u32[]{:S(2)}) collective-permute-start(bf16[256,384]{0,1:T(8,128)(2,1)} %copy.140), channel_id=1, source_target_pairs={{30,0},{0,2},{2,4},{4,6},{6,8},{8,10},{10,12},{12,14},{14,16},{16,... | collective-permute-start | bytes 589832 | tf_op jit(solution)/shard_map/while/body/eval_jaxpr/ppermute | solution.py:14
  1027.6 34.9 %collective-permute-start.2 = (bf16[256,384]{0,1:T(8,128)(2,1)S(1)}, bf16[256,384]{0,1:T(8,128)(2,1)}, u32[]{:S(2)}, u32[]{:S(2)}) collective-permute-start(bf16[256,384]{0,1:T(8,128)(2,1)S(1)} %copy.139), channel_id=1, source_target_pairs={{30,0},{0,2},{2,4},{4,6},{6,8},{8,10},{10,12},{12,14},{14,16},{16,... | collective-permute-start | bytes 589832 | tf_op jit(solution)/shard_map/while/body/eval_jaxpr/ppermute | solution.py:14
  1029.3 33.2 %collective-permute-start.3 = (bf16[256,384]{0,1:T(8,128)(2,1)}, bf16[256,384]{0,1:T(8,128)(2,1)}, u32[]{:S(2)}, u32[]{:S(2)}) collective-permute-start(bf16[256,384]{0,1:T(8,128)(2,1)} %copy.140), channel_id=1, source_target_pairs={{30,0},{0,2},{2,4},{4,6},{6,8},{8,10},{10,12},{12,14},{14,16},{16,... | collective-permute-start | bytes 589832 | tf_op jit(solution)/shard_map/while/body/eval_jaxpr/ppermute | solution.py:14
  1063.5 33.9 %collective-permute-start.2 = (bf16[256,384]{0,1:T(8,128)(2,1)S(1)}, bf16[256,384]{0,1:T(8,128)(2,1)}, u32[]{:S(2)}, u32[]{:S(2)}) collective-permute-start(bf16[256,384]{0,1:T(8,128)(2,1)S(1)} %copy.139), channel_id=1, source_target_pairs={{30,0},{0,2},{2,4},{4,6},{6,8},{8,10},{10,12},{12,14},{14,16},{16,... | collective-permute-start | bytes 589832 | tf_op jit(solution)/shard_map/while/body/eval_jaxpr/ppermute | solution.py:14
  1065.2 32.2 %collective-permute-start.3 = (bf16[256,384]{0,1:T(8,128)(2,1)}, bf16[256,384]{0,1:T(8,128)(2,1)}, u32[]{:S(2)}, u32[]{:S(2)}) collective-permute-start(bf16[256,384]{0,1:T(8,128)(2,1)} %copy.140), channel_id=1, source_target_pairs={{30,0},{0,2},{2,4},{4,6},{6,8},{8,10},{10,12},{12,14},{14,16},{16,... | collective-permute-start | bytes 589832 | tf_op jit(solution)/shard_map/while/body/eval_jaxpr/ppermute | solution.py:14
  1100.8 129.5 %reduce-scatter.28.cloned.1.call-start = ((), (), s32[]{:S(2)}) async-start(), calls=%async_computation.23 | async-start | bytes 2506752 | tf_op jit(solution)/shard_map/reduce_scatter | solution.py:296
  1104.2 191.7 %reduce-scatter.30.cloned.1.call-start = ((), (), s32[]{:S(2)}) async-start(), calls=%async_computation.24 | async-start | bytes 2506752 | tf_op jit(solution)/shard_map/reduce_scatter | solution.py:297
  1107.3 255.0 %reduce-scatter.32.cloned.1.call-start = ((), (), s32[]{:S(2)}) async-start(), calls=%async_computation.25 | async-start | bytes 2506752 | tf_op jit(solution)/shard_map/reduce_scatter | solution.py:298
  1110.7 473.2 %reduce-scatter.34.cloned.1.call-start = ((), (), s32[]{:S(2)}) async-start(), calls=%async_computation.26 | async-start | bytes 23396352 | tf_op jit(solution)/shard_map/reduce_scatter | solution.py:299
  1122.8 683.1 %reduce-scatter.38.cloned.1.call-start = ((), (), s32[]{:S(2)}) async-start(), calls=%async_computation.28 | async-start | bytes 23396352 | tf_op jit(solution)/shard_map/reduce_scatter | solution.py:300
  1133.7 893.9 %reduce-scatter.42.cloned.1.call-start = ((), (), s32[]{:S(2)}) async-start(), calls=%async_computation.30 | async-start | bytes 23396352 | tf_op jit(solution)/shard_map/reduce_scatter | solution.py:301
  1145.7 901.6 %reduce-scatter.54.cloned.1.call-start = ((), (), s32[]{:S(2)}) async-start(), calls=%async_computation.36 | async-start | bytes 12288
  1214.1 840.6 %reduce-scatter.46.cloned.1.call-start = ((), (), s32[]{:S(2)}) async-start(), calls=%async_computation.32 | async-start | bytes 565248
  1216.1 853.7 %reduce-scatter.48.cloned.1.call-start = ((), (), s32[]{:S(2)}) async-start(), calls=%async_computation.33 | async-start | bytes 565248
  1232.3 852.6 %reduce-scatter.50.cloned.1.call-start = ((), (), s32[]{:S(2)}) async-start(), calls=%async_computation.34 | async-start | bytes 565248
  1297.9 802.2 %reduce-scatter.52.cloned.1.call-start = ((), (), s32[]{:S(2)}) async-start(), calls=%async_computation.35 | async-start | bytes 565248
  1364.1 755.0 %reduce-scatter.36.cloned.1.call-start = ((), (), s32[]{:S(2)}) async-start(), calls=%async_computation.27 | async-start | bytes 1032192 | tf_op jit(solution)/shard_map/reduce_scatter | solution.py:325
  1586.2 552.1 %reduce-scatter.40.cloned.1.call-start = ((), (), s32[]{:S(2)}) async-start(), calls=%async_computation.29 | async-start | bytes 1032192 | tf_op jit(solution)/shard_map/reduce_scatter | solution.py:328
  1808.1 348.9 %reduce-scatter.44.cloned.1.call-start = ((), (), s32[]{:S(2)}) async-start(), calls=%async_computation.31 | async-start | bytes 1032192 | tf_op jit(solution)/shard_map/reduce_scatter | solution.py:331
  (301 other events, 1805.3 us)
Sparse Core Ops, SparseCore 0:
  9.6 24.9 all-gather.8
  36.0 22.2 all-gather.10
  59.9 22.2 all-gather.12
  83.5 22.2 all-gather.14
  107.2 130.3 all-gather.16
  239.0 130.2 all-gather.18
  370.8 130.2 all-gather.20
  1101.0 62.9 reduce-scatter.25
  1168.2 62.0 reduce-scatter.27
  1234.0 61.9 reduce-scatter.29
  1300.2 61.9 reduce-scatter.31
  1366.3 217.6 reduce-scatter.33
  1588.1 217.6 reduce-scatter.37
  1809.9 217.6 reduce-scatter.41
  2030.2 8.8 reduce-scatter.53
  2041.7 12.9 reduce-scatter.45
  2056.8 12.9 reduce-scatter.47
  2071.9 12.9 reduce-scatter.49
  2087.1 12.9 reduce-scatter.51
  2102.7 16.3 reduce-scatter.35
  2121.9 16.3 reduce-scatter.39
  2140.6 16.3 reduce-scatter.43
where the time goes:
time: 2180 us; the launch traced here: 2170 us
  waiting for transfers between devices  1010 us (46%)
  local copies, waits for them, and re-layouts  598 us (27%)
  matrix products  210 us (10%)
  other arithmetic  181 us (8%)
  blocking collectives  77.2 us (4%)
  starting transfers between devices  70.9 us (3%)
    while x578, local copies, waits for them, and re-layouts  255 us
    reduce_scatter x1, waiting for transfers between devices, body(): lax.psum_scatter(gate_grad, 'ctx', scatter_dimension=1, tiled=True)  220 us
    reduce_scatter x1, waiting for transfers between devices, body(): lax.psum_scatter(up_grad, 'ctx', scatter_dimension=1, tiled=True)  220 us
    reduce_scatter x1, waiting for transfers between devices, body(): lax.psum_scatter(down_grad, 'ctx', scatter_dimension=0, tiled=True)  219 us
    reshape x32, local copies, waits for them, and re-layouts, skew_expand(): return tiled.reshape(count, length, 2 * length - 1)[:, :, length - 1:]  154 us
    slice x32, local copies, waits for them, and re-layouts, skew_expand(): tiled = jnp.tile(padded, (1, length))[:, :length * (2 * length - 1)]  75.3 us
    all_gather x1, waiting for transfers between devices, body(): lax.all_gather(down_weight, 'wsh', axis=0, tiled=True)  71 us
    ppermute x94, starting transfers between devices, shifted(): return lax.ppermute(block, axis, route)  70 us
  transfers between devices with their start and end apart: 116, of which 16 were waited for; matrix products, arithmetic and copies ran while one was open for 43% of the time, Pallas kernels for 0%

commit v1 on v0

--- a/solution.py
+++ b/solution.py
@@ -1,6 +1,10 @@
+import functools
+
 import jax
 import jax.numpy as jnp
 from jax import lax
+from jax.experimental import pallas as pl
+from jax.experimental.pallas import tpu as pltpu
 from jax.sharding import PartitionSpec as P
 
 EPSILON = 1e-06
@@ -351,6 +355,753 @@
     )
 
 
+BLOCK = 256
+PAIR = 128
+SPAN_ROW = 1024
+CONTRACT_LAST = (((1,), (1,)), ((), ()))
+AXES = ("ctx", "wsh")
+
+
+def head_lanes(rows, second):
+    lane = lax.broadcasted_iota(jnp.int32, (rows, PAIR), 1)
+    return (lane >= PAIR // 2) if second else (lane < PAIR // 2)
+
+
+def pair_select(first, second, rows):
+    return jnp.where(head_lanes(rows, False), first, second)
+
+
+def only_head(block, second):
+    return jnp.where(head_lanes(block.shape[0], second), block, jnp.zeros_like(block))
+
+
+def query_aux(rows):
+    lane = lax.broadcasted_iota(jnp.int32, (rows, PAIR), 1)
+    return jnp.where(lane == 0, 1.0, 0.0).astype(jnp.bfloat16)
+
+
+def key_aux(start, rows, length):
+    lane = lax.broadcasted_iota(jnp.int32, (rows, PAIR), 1)
+    row = lax.broadcasted_iota(jnp.int32, (rows, PAIR), 0)
+    dead = jnp.logical_and(lane == 0, start + row >= length)
+    return jnp.where(dead, MASKED, 0.0).astype(jnp.bfloat16)
+
+
+def contract_last(left, right):
+    return lax.dot_general(left, right, CONTRACT_LAST, preferred_element_type=jnp.float32)
+
+
+def tile_of(key_block, query_block):
+    return jnp.clip(key_block - query_block, -2, 2) + 2
+
+
+def tiles_kernel(row_ref, tile_ref, turned_ref):
+    row = row_ref[0]
+    wide = pltpu.roll(
+        jnp.broadcast_to(row, (BLOCK, SPAN_ROW)), SPAN_ROW - 255, 1, stride=1, stride_axis=0
+    )
+    first = jnp.broadcast_to(row[:, 0:1], (BLOCK, BLOCK))
+    last = jnp.broadcast_to(row[:, SPAN_ROW - 1 : SPAN_ROW], (BLOCK, BLOCK))
+    tiles = [first, wide[:, 0:256], wide[:, 256:512], wide[:, 512:768], last]
+    for spot, tile in enumerate(tiles):
+        tile_ref[0, spot] = tile.astype(jnp.bfloat16)
+        turned_ref[0, spot] = jnp.transpose(tile).astype(jnp.bfloat16)
+
+
+def bias_tiles(offset_rows):
+    heads = offset_rows.shape[0]
+    shape = jax.ShapeDtypeStruct((heads, 5, BLOCK, BLOCK), jnp.bfloat16)
+    spec = pl.BlockSpec((1, 5, BLOCK, BLOCK), lambda h: (h, 0, 0, 0))
+    return pl.pallas_call(
+        tiles_kernel,
+        grid=(heads,),
+        out_shape=(shape, shape),
+        in_specs=[pl.BlockSpec((1, 1, SPAN_ROW), lambda h: (h, 0, 0))],
+        out_specs=(spec, spec),
+        name="bias_tiles",
+    )(offset_rows[:, None, :])
+
+
+def forward_kernel(count, first, last, info_ref, *refs):
+    refs = list(refs)
+    query_ref = refs.pop(0)
+    key_refs, refs = refs[:count], refs[count:]
+    value_refs, refs = refs[:count], refs[count:]
+    tile_ref = refs.pop(0)
+    query_block, length = info_ref[0], info_ref[1]
+    query = query_ref[...]
+    aux = query_aux(BLOCK)
+    if first:
+        old_max = jnp.full((BLOCK, PAIR), MASKED, jnp.float32)
+        total = None
+    else:
+        max_ref, total_ref = refs.pop(0), refs.pop(0)
+        old_max, total = max_ref[...], total_ref[...]
+    keys = []
+    for spot in range(count):
+        start = info_ref[2 + spot] * BLOCK
+        keys.append(
+            jnp.concatenate([key_refs[spot][...], key_aux(start, BLOCK, length)], axis=1)
+        )
+    tops, weights = [], []
+    for head in range(2):
+        left = jnp.concatenate([only_head(query, head == 1), aux], axis=1)
+        scores = []
+        for spot in range(count):
+            tile = tile_ref[head, tile_of(info_ref[2 + spot], query_block)]
+            scores.append(contract_last(left, keys[spot]) + tile.astype(jnp.float32))
+        top = functools.reduce(jnp.maximum, scores)
+        lane = head * (PAIR // 2)
+        top = jnp.maximum(old_max[:, lane : lane + 1], jnp.max(top, axis=1, keepdims=True))
+        tops.append(top)
+        weights.append([jnp.exp(score - top).astype(jnp.bfloat16) for score in scores])
+    new_max = pair_select(tops[0], tops[1], BLOCK)
+    ones = jnp.ones((BLOCK, PAIR), jnp.bfloat16)
+    update = None
+    for spot in range(count):
+        value = value_refs[spot][...]
+        right = jnp.concatenate(
+            [
+                jnp.concatenate([only_head(value, False), only_head(ones, False)], axis=1),
+                jnp.concatenate([only_head(value, True), only_head(ones, True)], axis=1),
+            ],
+            axis=0,
+        )
+        left = jnp.concatenate([weights[0][spot], weights[1][spot]], axis=1)
+        part = jnp.dot(left, right, preferred_element_type=jnp.float32)
+        update = part if update is None else update + part
+    if not first:
+        factor = jnp.exp(old_max - new_max)
+        update = update + total * jnp.concatenate([factor, factor], axis=1)
+    if last:
+        out_ref, low_ref, log_ref = refs
+        out = update[:, :PAIR] / update[:, PAIR:]
+        out_ref[...] = out
+        low_ref[...] = out.astype(jnp.bfloat16)
+        log_ref[...] = new_max + jnp.log(update[:, PAIR:])
+    else:
+        max_out, total_out = refs
+        max_out[...] = new_max
+        total_out[...] = update
+
+
+def forward_call(info, query, keys, values, tiles, state, last):
+    count = len(keys)
+    inner = query.shape[1]
+    pairs = inner // PAIR
+    first = state is None
+    block = pl.BlockSpec((BLOCK, PAIR), lambda p, s: (0, p))
+    double = pl.BlockSpec((BLOCK, 2 * PAIR), lambda p, s: (0, p))
+    tile_spec = pl.BlockSpec((2, 5, BLOCK, BLOCK), lambda p, s: (p, 0, 0, 0))
+    in_specs = [block] * (1 + 2 * count) + [tile_spec]
+    operands = [info, query, *keys, *values, tiles]
+    aliases = {}
+    if not first:
+        in_specs += [block, double]
+        operands += list(state)
+    f32 = functools.partial(jax.ShapeDtypeStruct, dtype=jnp.float32)
+    if last:
+        out_shape = (
+            f32((BLOCK, inner)),
+            jax.ShapeDtypeStruct((BLOCK, inner), jnp.bfloat16),
+            f32((BLOCK, inner)),
+        )
+        out_specs = (block, block, block)
+    else:
+        out_shape = (f32((BLOCK, inner)), f32((BLOCK, 2 * inner)))
+        out_specs = (block, double)
+    return pl.pallas_call(
+        functools.partial(forward_kernel, count, first, last),
+        grid_spec=pltpu.PrefetchScalarGridSpec(
+            num_scalar_prefetch=1, grid=(pairs,), in_specs=in_specs, out_specs=out_specs
+        ),
+        out_shape=out_shape,
+        input_output_aliases=aliases,
+        cost_estimate=pl.CostEstimate(
+            flops=2 * pairs * count * 6 * BLOCK * BLOCK * BLOCK,
+            bytes_accessed=pairs * (count * 2 + 10) * BLOCK * PAIR * 2,
+            transcendentals=pairs * count * 2 * BLOCK * BLOCK,
+        ),
+        name="attention_forward",
+    )(*operands)
+
+
+def query_kernel(blocks, info_ref, query_ref, grad_ref, out_ref, log_ref, key_ref, value_ref, tile_ref, part_ref, diag_ref, sums_ref):
+    query_block, length = info_ref[0], info_ref[1]
+    query, grad = query_ref[...], grad_ref[...]
+    aux = query_aux(BLOCK)
+    product = grad.astype(jnp.float32) * out_ref[...]
+    logs = log_ref[...]
+    sums_ref[...] = jnp.zeros_like(sums_ref)
+    lefts, grads, deltas, shifts = [], [], [], []
+    for head in range(2):
+        lefts.append(jnp.concatenate([only_head(query, head == 1), aux], axis=1))
+        grads.append(only_head(grad, head == 1))
+        deltas.append(jnp.sum(only_head(product, head == 1), axis=1, keepdims=True))
+        lane = head * (PAIR // 2)
+        shifts.append(logs[:, lane : lane + 1])
+    part_ref[...] = jnp.zeros_like(part_ref)
+
+    def one(spot, carry):
+        key_block = info_ref[2 + spot]
+        rows = pl.ds(pl.multiple_of(spot * BLOCK, BLOCK), BLOCK)
+        key, value = key_ref[rows, :], value_ref[rows, :]
+        wide = jnp.concatenate([key, key_aux(key_block * BLOCK, BLOCK, length)], axis=1)
+        tile = tile_of(key_block, query_block)
+        pieces = []
+        for head in range(2):
+            scores = contract_last(lefts[head], wide) + tile_ref[head, tile].astype(jnp.float32)
+            probs = jnp.exp(scores - shifts[head])
+            slope = contract_last(grads[head], value)
+            score_grad = probs * (slope - deltas[head])
+            sums_ref[head, tile] += score_grad
+            pieces.append(score_grad.astype(jnp.bfloat16))
+        right = jnp.concatenate([only_head(key, False), only_head(key, True)], axis=0)
+        part_ref[...] += jnp.dot(
+            jnp.concatenate(pieces, axis=1), right, preferred_element_type=jnp.float32
+        )
+        return carry
+
+    lax.fori_loop(0, blocks, one, 0)
+    rows = []
+    lane = lax.broadcasted_iota(jnp.int32, (1, SPAN_ROW), 1)
+    flip = (
+        lax.broadcasted_iota(jnp.int32, (BLOCK, BLOCK), 0)
+        + lax.broadcasted_iota(jnp.int32, (BLOCK, BLOCK), 1)
+        == BLOCK - 1
+    ).astype(jnp.float32)
+    for head in range(2):
+        near = jnp.concatenate(
+            [sums_ref[head, 1], sums_ref[head, 2], sums_ref[head, 3], jnp.zeros((BLOCK, BLOCK), jnp.float32)],
+            axis=1,
+        )
+        flipped = jnp.dot(flip, near, precision=HIGH, preferred_element_type=jnp.float32)
+        turned = pltpu.roll(flipped, 0, 1, stride=1, stride_axis=0)
+        line = jnp.sum(turned, axis=0, keepdims=True)
+        before = jnp.sum(jnp.sum(sums_ref[head, 0], axis=0, keepdims=True), axis=1, keepdims=True)
+        after = jnp.sum(jnp.sum(sums_ref[head, 4], axis=0, keepdims=True), axis=1, keepdims=True)
+        line = line + jnp.where(lane == 0, before, 0.0) + jnp.where(lane == SPAN_ROW - 2, after, 0.0)
+        rows.append(line)
+    diag_ref[0] = jnp.concatenate(rows + [jnp.zeros((6, SPAN_ROW), jnp.float32)], axis=0)
+
+
+def query_call(info, query, grad, out, logs, keys, values, tiles):
+    inner = query.shape[1]
+    pairs = inner // PAIR
+    blocks = keys.shape[0] // BLOCK
+    block = pl.BlockSpec((BLOCK, PAIR), lambda p, s: (0, p))
+    tall = pl.BlockSpec((blocks * BLOCK, PAIR), lambda p, s: (0, p))
+    tile_spec = pl.BlockSpec((2, 5, BLOCK, BLOCK), lambda p, s: (p, 0, 0, 0))
+    return pl.pallas_call(
+        functools.partial(query_kernel, blocks),
+        grid_spec=pltpu.PrefetchScalarGridSpec(
+            num_scalar_prefetch=1,
+            grid=(pairs,),
+            in_specs=[block, block, block, block, tall, tall, tile_spec],
+            out_specs=(block, pl.BlockSpec((1, 8, SPAN_ROW), lambda p, s: (p, 0, 0))),
+            scratch_shapes=[pltpu.VMEM((2, 5, BLOCK, BLOCK), jnp.float32)],
+        ),
+        out_shape=(
+            jax.ShapeDtypeStruct((BLOCK, inner), jnp.float32),
+            jax.ShapeDtypeStruct((pairs, 8, SPAN_ROW), jnp.float32),
+        ),
+        cost_estimate=pl.CostEstimate(
+            flops=2 * pairs * blocks * 6 * BLOCK * BLOCK * BLOCK,
+            bytes_accessed=pairs * blocks * 2 * BLOCK * PAIR * 2,
+            transcendentals=pairs * blocks * 2 * BLOCK * BLOCK,
+        ),
+        name="attention_query_grad",
+    )(info, query, grad, out, logs, keys, values, tiles)
+
+
+def key_kernel(count, first, last, info_ref, *refs):
+    refs = list(refs)
+    key_ref, value_ref = refs.pop(0), refs.pop(0)
+    query_refs, refs = refs[:count], refs[count:]
+    grad_refs, refs = refs[:count], refs[count:]
+    log_refs, refs = refs[:count], refs[count:]
+    delta_refs, refs = refs[:count], refs[count:]
+    tile_ref = refs.pop(0)
+    if not first:
+        key_in, value_in = refs.pop(0), refs.pop(0)
+    key_out, value_out = refs
+    pair = pl.program_id(0)
+    key_block, length = info_ref[0], info_ref[1]
+    key, value = key_ref[...], value_ref[...]
+    wide = jnp.concatenate([key, key_aux(key_block * BLOCK, BLOCK, length)], axis=1)
+    aux = query_aux(BLOCK)
+    key_sum = value_sum = None
+    for spot in range(count):
+        query_block = info_ref[2 + spot]
+        query, grad = query_refs[spot][...], grad_refs[spot][...]
+        tile = tile_of(key_block, query_block)
+        probs_low, slopes_low, queries, grads = [], [], [], []
+        for head in range(2):
+            row = pl.ds(2 * pair + head, 1)
+            my_query, my_grad = only_head(query, head == 1), only_head(grad, head == 1)
+            scores = contract_last(wide, jnp.concatenate([my_query, aux], axis=1))
+            scores = scores + tile_ref[head, tile].astype(jnp.float32)
+            probs = jnp.exp(scores - log_refs[spot][row, :])
+            slope = contract_last(value, my_grad) - delta_refs[spot][row, :]
+            probs_low.append(probs.astype(jnp.bfloat16))
+            slopes_low.append((probs * slope).astype(jnp.bfloat16))
+            queries.append(my_query)
+            grads.append(my_grad)
+        part_value = jnp.dot(
+            jnp.concatenate(probs_low, axis=1), jnp.concatenate(grads, axis=0), preferred_element_type=jnp.float32
+        )
+        part_key = jnp.dot(
+            jnp.concatenate(slopes_low, axis=1), jnp.concatenate(queries, axis=0), preferred_element_type=jnp.float32
+        )
+        key_sum = part_key if key_sum is None else key_sum + part_key
+        value_sum = part_value if value_sum is None else value_sum + part_value
+    if not first:
+        key_sum, value_sum = key_sum + key_in[...], value_sum + value_in[...]
+    key_out[...] = key_sum.astype(key_out.dtype)
+    value_out[...] = value_sum.astype(value_out.dtype)
+
+
+def key_call(info, key, value, queries, grads, logs, deltas, turned, state, last):
+    count = len(queries)
+    inner = key.shape[1]
+    pairs = inner // PAIR
+    first = state is None
+    block = pl.BlockSpec((BLOCK, PAIR), lambda p, s: (0, p))
+    rows = pl.BlockSpec((8, BLOCK), lambda p, s: (0, 0))
+    tile_spec = pl.BlockSpec((2, 5, BLOCK, BLOCK), lambda p, s: (p, 0, 0, 0))
+    in_specs = [block] * (2 + 2 * count) + [rows] * (2 * count) + [tile_spec]
+    operands = [info, key, value, *queries, *grads, *logs, *deltas, turned]
+    if not first:
+        in_specs += [block, block]
+        operands += list(state)
+    kind = jnp.bfloat16 if last else jnp.float32
+    shape = jax.ShapeDtypeStruct((BLOCK, inner), kind)
+    return pl.pallas_call(
+        functools.partial(key_kernel, count, first, last),
+        grid_spec=pltpu.PrefetchScalarGridSpec(
+            num_scalar_prefetch=1, grid=(pairs,), in_specs=in_specs, out_specs=(block, block)
+        ),
+        out_shape=(shape, shape),
+        cost_estimate=pl.CostEstimate(
+            flops=2 * pairs * count * 8 * BLOCK * BLOCK * BLOCK,
+            bytes_accessed=pairs * (count * 2 + 10) * BLOCK * PAIR * 2,
+            transcendentals=pairs * count * 2 * BLOCK * BLOCK,
+        ),
+        name="attention_key_grad",
+    )(*operands)
+
+
+def grouped_body(
+    tokens,
+    lengths,
+    buckets,
+    attention_gain,
+    query_weight,
+    key_weight,
+    value_weight,
+    output_weight,
+    bias_table,
+    feed_gain,
+    gate_weight,
+    up_weight,
+    down_weight,
+    cotangent,
+):
+    bf16, f32 = jnp.bfloat16, jnp.float32
+    places = lax.axis_size("ctx")
+    chips = places // 2
+    rows_of_chips = chips // 2
+    here = lax.axis_index("ctx")
+    side = lax.axis_index("wsh")
+    core = here % 2
+    chip = here // 2
+    lane_y = chip % 2
+    lane_z = chip // 2
+    length = tokens.shape[1]
+    width = tokens.shape[2]
+    half = width // 2
+    heads = bias_table.shape[1]
+    inner = query_weight.shape[1]
+
+    def spread(block, route):
+        return lax.ppermute(block, AXES, route)
+
+    def route_of(move):
+        pairs = []
+        for c in range(places):
+            for w in range(2):
+                target = move(c // 4, (c // 2) % 2, c % 2, w)
+                if target is not None:
+                    z, y, k, x = target
+                    pairs.append((c * 2 + w, (((z * 2 + y) * 2) + k) * 2 + x))
+        return pairs
+
+    route_core = route_of(lambda z, y, k, x: (z, y, 1 - k, x))
+    route_x = route_of(lambda z, y, k, x: (z, y, k, 1 - x))
+    route_y = route_of(lambda z, y, k, x: (z, 1 - y, k, x))
+    route_far = route_of(lambda z, y, k, x: (z ^ 2, y, k, x))
+    route_near = route_of(lambda z, y, k, x: (z ^ 1, y, k, x))
+    order = [(i, 0) for i in range(rows_of_chips)] + [
+        (rows_of_chips - 1 - i, 1) for i in range(rows_of_chips)
+    ]
+    place = {spot: i for i, spot in enumerate(order)}
+
+    def ring(distance):
+        return route_of(
+            lambda z, y, k, x: (*order[(place[(z, y)] + distance) % chips], k, x)
+        )
+
+    route_up, route_down = ring(1), ring(-1)
+    my_place = jnp.where(lane_y == 0, lane_z, 2 * rows_of_chips - 1 - lane_z)
+
+    def chip_at(spot):
+        spot = spot % chips
+        return jnp.where(
+            spot < rows_of_chips, 2 * spot, 2 * (2 * rows_of_chips - 1 - spot) + 1
+        )
+
+    def swap_core(block):
+        return spread(block, route_core)
+
+    def swap_x(block):
+        return spread(block, route_x)
+
+    def all_sum(block):
+        for route in (route_core, route_x, route_y, route_far, route_near):
+            block = block + spread(block, route)
+        return block
+
+    def both_sides(mine, other, axis):
+        return jnp.where(
+            side == 0,
+            jnp.concatenate([mine, other], axis=axis),
+            jnp.concatenate([other, mine], axis=axis),
+        )
+
+    def fetch_rows(weight):
+        count = weight.shape[0] // 2
+        part = swap_x(lax.dynamic_slice_in_dim(weight, core * count, count, 0))
+        return part, swap_core(part)
+
+    def join_rows(weight, part, traded):
+        other = jnp.where(
+            core == 0,
+            jnp.concatenate([part, traded], axis=0),
+            jnp.concatenate([traded, part], axis=0),
+        )
+        return both_sides(weight, other, 0)
+
+    gain_other = swap_x(attention_gain)
+    projections = jnp.concatenate([key_weight, value_weight, query_weight], axis=1)
+    part, traded = fetch_rows(projections)
+    table_other = swap_x(bias_table)
+    feed_other = swap_x(feed_gain)
+    live_count = jnp.minimum(lengths[0, 0], places * length)
+    count_other = swap_x(live_count.astype(f32).reshape(1, 1))[0, 0].astype(jnp.int32)
+    mine = tokens[0]
+    cot = cotangent[0]
+    gain_one = both_sides(attention_gain, gain_other, 0).astype(f32)
+    gain_two = both_sides(feed_gain, feed_other, 0).astype(f32)
+    table = both_sides(bias_table, table_other, 0)
+
+    positions = here * length + jnp.arange(length, dtype=jnp.int32)
+    pair_positions = (here ^ 1) * length + jnp.arange(length, dtype=jnp.int32)
+    live_own = (positions < live_count).astype(f32)[:, None]
+    live_group = jnp.concatenate(
+        [
+            live_own,
+            (pair_positions < live_count).astype(f32)[:, None],
+            (positions < count_other).astype(f32)[:, None],
+            (pair_positions < count_other).astype(f32)[:, None],
+        ],
+        axis=0,
+    )
+
+    inputs = mine.astype(f32)
+    scale_one = row_scale(inputs)
+    first = (inputs * scale_one * gain_one).astype(bf16)
+    weight_all = join_rows(projections, part, traded)
+    projected = jnp.dot(first, weight_all, preferred_element_type=f32).astype(bf16)
+    keys, values, query = (projected[:, :inner], projected[:, inner : 2 * inner], projected[:, 2 * inner :])
+
+    bucket_count = table.shape[0]
+    reach = (buckets.shape[0] + 1) // 2
+    offsets = jnp.clip(jnp.arange(SPAN_ROW, dtype=jnp.int32) - 511, 1 - reach, reach - 1) + (reach - 1)
+    spots = jnp.arange(buckets.shape[0], dtype=jnp.int32)
+    chosen = jnp.sum(jnp.where(offsets[:, None] == spots[None, :], buckets[None, :], 0), axis=1)
+    onehot = (chosen[:, None] == jnp.arange(bucket_count, dtype=jnp.int32)[None, :]).astype(f32)
+    offset_rows = lax.dot_general(
+        table.astype(f32), onehot, (((0,), (1,)), ((), ())), precision=HIGH, preferred_element_type=f32
+    )
+    tiles, turned = bias_tiles(offset_rows)
+
+    def group_rows(block):
+        other = swap_x(block)
+        return jnp.concatenate([block, swap_core(block), other, swap_core(other)], axis=0)
+
+    def ring_gather(own_parts, use):
+        pieces = [[part, swap_core(part)] for part in own_parts]
+        use(0, pieces, [chip * 2 + core, chip * 2 + 1 - core])
+        ups = downs = list(own_parts)
+        middle = chips // 2
+        for step in range(1, middle + 1):
+            if step < middle:
+                ups = [spread(part, route_up) for part in ups]
+                downs = [spread(part, route_down) for part in downs]
+                pieces = [
+                    [u, swap_core(u), d, swap_core(d)] for u, d in zip(ups, downs)
+                ]
+                a, b = chip_at(my_place + chips - step), chip_at(my_place + step)
+                use(step, pieces, [a * 2 + core, a * 2 + 1 - core, b * 2 + core, b * 2 + 1 - core])
+            else:
+                lasts = [
+                    spread(part_u, route_up) if spot % 2 == 0 else spread(part_d, route_down)
+                    for spot, (part_u, part_d) in enumerate(zip(ups, downs))
+                ]
+                pieces = [[part, swap_core(part)] for part in lasts]
+                a = chip_at(my_place + step)
+                use(step, pieces, [a * 2 + core, a * 2 + 1 - core])
+
+    middle = chips // 2
+    store = {"state": None, "keys": [], "values": [], "blocks": []}
+
+    def forward_use(step, pieces, blocks):
+        key_blocks, value_blocks = pieces
+        info = jnp.stack([here, live_count, *blocks]).astype(jnp.int32)
+        store["state"] = forward_call(
+            info, query, key_blocks, value_blocks, tiles, store["state"], step == middle
+        )
+        store["keys"] += key_blocks
+        store["values"] += value_blocks
+        store["blocks"] += blocks
+
+    ring_gather([keys, values], forward_use)
+    attention, attention_low, logs = store["state"]
+    keys_all = jnp.concatenate(store["keys"], axis=0)
+    values_all = jnp.concatenate(store["values"], axis=0)
+    info_all = jnp.stack([here, live_count, *store["blocks"]]).astype(jnp.int32)
+
+    out_part, out_traded = fetch_columns(output_weight, core, swap_x, swap_core)
+    output_full = both_sides(
+        output_weight,
+        jnp.where(
+            core == 0,
+            jnp.concatenate([out_part, out_traded], axis=0),
+            jnp.concatenate([out_traded, out_part], axis=0),
+        ),
+        1,
+    )
+    tokens_group = group_rows(mine)
+    cot_group = group_rows(cot)
+
+    hidden_units = gate_weight.shape[1] // 2
+    gate_mine = lax.dynamic_slice_in_dim(gate_weight, core * hidden_units, hidden_units, 1)
+    up_mine = lax.dynamic_slice_in_dim(up_weight, core * hidden_units, hidden_units, 1)
+    down_mine = lax.dynamic_slice_in_dim(down_weight, core * hidden_units, hidden_units, 0)
+    outer_low = (cot_group.astype(f32) * live_group).astype(bf16)
+    mixed = group_rows(attention_low)
+    branch = jnp.dot(mixed, output_full, preferred_element_type=f32)
+    middle_rows = tokens_group.astype(f32) + live_group * branch
+    scale_two = row_scale(middle_rows)
+    unit = middle_rows * scale_two
+    second = (unit * gain_two).astype(bf16)
+    gate = jnp.dot(second, gate_mine, preferred_element_type=f32)
+    up = jnp.dot(second, up_mine, preferred_element_type=f32)
+
+    def gated(gate_in, up_in):
+        return jax.nn.gelu(gate_in, approximate=True) * up_in
+
+    hidden_value, gate_pull = jax.vjp(gated, gate, up)
+    hidden = hidden_value.astype(bf16)
+    hidden_grad = jnp.einsum("td,fd->tf", outer_low, down_mine, preferred_element_type=f32)
+    gate_back, up_back = gate_pull(hidden_grad)
+    gate_low = gate_back.astype(bf16)
+    up_low = up_back.astype(bf16)
+    second_grad = jnp.einsum("tf,df->td", gate_low, gate_mine, preferred_element_type=f32) + jnp.einsum(
+        "tf,df->td", up_low, up_mine, preferred_element_type=f32
+    )
+    feed_gain_part = jnp.sum(second_grad * unit, axis=0)
+    scaled = second_grad * gain_two
+    middle_part = scale_two * (scaled - unit * jnp.mean(scaled * unit, axis=-1, keepdims=True))
+    middle_part_low = (live_group * middle_part).astype(bf16)
+    grad_part = jnp.einsum("td,id->ti", middle_part_low, output_full, preferred_element_type=f32)
+
+    def group_sum(block):
+        grid = block.reshape(4, length, block.shape[-1])
+        sent = swap_core(jnp.stack([grid[1], grid[3]]).astype(bf16)).astype(f32)
+        kept, passed = grid[0] + sent[0], grid[2] + sent[1]
+        return kept + swap_x(passed.astype(bf16)).astype(f32)
+
+    outer_own = outer_low[:length].astype(f32)
+    grad_own = jnp.einsum("td,id->ti", outer_low[:length], output_full, preferred_element_type=f32)
+    attention_grad = (group_sum(grad_part) + grad_own).astype(bf16)
+
+    lane_head = jnp.arange(inner, dtype=jnp.int32) // (inner // heads)
+    head_rows = (jnp.arange(8, dtype=jnp.int32)[:, None] == lane_head[None, :]).astype(f32)
+    head_first = head_rows * (jnp.arange(inner, dtype=jnp.int32) % (inner // heads) == 0).astype(f32)[None, :]
+    delta_rows = lax.dot_general(
+        head_rows, attention_grad.astype(f32) * attention, CONTRACT_LAST, precision=HIGH, preferred_element_type=f32
+    )
+    log_rows = lax.dot_general(
+        head_first, logs, CONTRACT_LAST, precision=HIGH, preferred_element_type=f32
+    )
+    back = {"state": None}
+
+    def backward_use(step, pieces, blocks):
+        query_blocks, grad_blocks, log_blocks, delta_blocks = pieces
+        info = jnp.stack([here, live_count, *blocks]).astype(jnp.int32)
+        back["state"] = key_call(
+            info, keys, values, query_blocks, grad_blocks, log_blocks, delta_blocks, turned, back["state"], step == middle
+        )
+
+    query_sum, diagonals = query_call(
+        info_all, query, attention_grad, attention, logs, keys_all, values_all, tiles
+    )
+    ring_gather([query, attention_grad, log_rows, delta_rows], backward_use)
+    keys_low, values_low = back["state"]
+    query_low = query_sum.astype(bf16)
+
+    feed = group_sum(jnp.dot(hidden, down_mine, preferred_element_type=f32))
+    result = (middle_rows[:length] + live_own * feed).astype(bf16)
+    middle_grad = outer_own + group_sum(middle_part)
+    branch_low = (live_own * middle_grad).astype(bf16)
+
+    good = (lane_z // 2) == side
+    z_low = lane_z % 2
+    route_one = route_of(
+        lambda z, y, k, x: {(3, 0): (2, y, k, x), (0, 1): (1, y, k, x)}.get((z, x))
+    )
+    route_two = route_of(
+        lambda z, y, k, x: {(2, 0): (1, y, k, x), (1, 1): (2, y, k, x)}.get((z, x))
+    )
+    route_three = route_of(
+        lambda z, y, k, x: (z ^ 1, y, k, x) if z // 2 == x and z % 2 != k else None
+    )
+    route_four = route_of(
+        lambda z, y, k, x: (z, y, 1 - k, x) if z // 2 == x and z % 2 == k else None
+    )
+    route_five = route_of(lambda z, y, k, x: (z, y, k, 1 - x) if z // 2 == x else None)
+
+    def add_low(left, right):
+        return (left.astype(f32) + right.astype(f32)).astype(bf16)
+
+    def halves(block, bit):
+        size = block.shape[0] // 2
+        kept = lax.dynamic_slice_in_dim(block, bit * size, size, 0)
+        sent = lax.dynamic_slice_in_dim(block, (1 - bit) * size, size, 0)
+        return kept, sent
+
+    def reduce_rows(block):
+        kept, sent = halves(block, lane_y)
+        total = add_low(kept, spread(sent, route_y))
+        total = add_low(total, spread(total, route_one))
+        total = add_low(total, spread(total, route_two))
+        total = add_low(total, spread(total, route_three))
+        kept, sent = halves(total, core)
+        quarter = jnp.where(z_low == core, kept, spread(sent, route_four))
+        kept, sent = halves(quarter, side)
+        return jnp.where(good, kept, spread(sent, route_five)).astype(f32)
+
+    down_full = jnp.einsum("tf,td->fd", hidden, outer_low, preferred_element_type=f32).astype(bf16)
+    gate_full = jnp.einsum("tf,td->fd", gate_low, second, preferred_element_type=f32).astype(bf16)
+    up_full = jnp.einsum("tf,td->fd", up_low, second, preferred_element_type=f32).astype(bf16)
+    down_out = reduce_rows(down_full)
+    gate_out = jnp.transpose(reduce_rows(gate_full))
+    up_out = jnp.transpose(reduce_rows(up_full))
+
+    columns = inner // places
+    target = jnp.arange(inner // 2, dtype=jnp.int32)
+    group_index, inside = target // columns, target % columns
+    y_bit = group_index // rows_of_chips
+    z_index = group_index % rows_of_chips
+
+    def picker(which):
+        source = (((z_index * 2 + y_bit) * 2) + which) * columns + inside
+        return (jnp.arange(inner, dtype=jnp.int32)[:, None] == source[None, :]).astype(bf16)
+
+    pick_kept, pick_sent = picker(core), picker(1 - core)
+
+    def pick(block, chooser):
+        return jnp.dot(block, chooser, preferred_element_type=f32).astype(bf16)
+
+    def lanes_of(block):
+        low_half, high_half = block[:, :half], block[:, half:]
+        return (
+            jnp.where(side == 0, low_half, high_half),
+            jnp.where(side == 0, high_half, low_half),
+        )
+
+    def outer_product(left, right):
+        return jnp.einsum("ti,td->id", left, right, preferred_element_type=f32)
+
+    def reduce_projection(rows, others):
+        kept_x, sent_x, kept_y, sent_y = [], [], [], []
+        for block, (lane_kept, lane_sent) in zip(rows, others):
+            mine_rows, other_rows = pick(block, pick_kept), pick(block, pick_sent)
+            kept_x.append(outer_product(mine_rows, lane_kept))
+            kept_y.append(outer_product(mine_rows, lane_sent))
+            sent_x.append(outer_product(other_rows, lane_kept).astype(bf16))
+            sent_y.append(outer_product(other_rows, lane_sent).astype(bf16))
+        got_x = swap_core(jnp.stack(sent_x)).astype(f32)
+        got_y = swap_core(jnp.stack(sent_y)).astype(f32)
+        passed = (jnp.stack(kept_y) + got_y).astype(bf16)
+        total = (jnp.stack(kept_x) + got_x + swap_x(passed).astype(f32)).astype(bf16)
+        for bit, route in ((lane_y, route_y), (lane_z // 2, route_far), (lane_z % 2, route_near)):
+            size = total.shape[1] // 2
+            kept = lax.dynamic_slice_in_dim(total, bit * size, size, 1)
+            sent = lax.dynamic_slice_in_dim(total, (1 - bit) * size, size, 1)
+            total = add_low(kept, spread(sent, route))
+        return total.astype(f32)
+
+    output_out = reduce_projection([attention_low], [lanes_of(branch_low)])[0]
+    first_lanes = lanes_of(first)
+    projection_out = reduce_projection([query_low, keys_low, values_low], [first_lanes] * 3)
+    projection_out = jnp.transpose(projection_out, (0, 2, 1))
+
+    joined = jnp.concatenate([keys_low, values_low, query_low], axis=1)
+    first_grad = jnp.einsum("ti,di->td", joined, weight_all, preferred_element_type=f32)
+    unit_one = inputs * scale_one
+    gain_one_part = jnp.sum(first_grad * unit_one, axis=0)
+    scaled_one = first_grad * gain_one
+    input_gradient = (
+        middle_grad
+        + scale_one * (scaled_one - unit_one * jnp.mean(scaled_one * unit_one, axis=-1, keepdims=True))
+    ).astype(bf16)
+
+    lines = diagonals[:, :2].reshape(heads, SPAN_ROW)
+    table_part = lax.dot_general(
+        onehot, lines, (((0,), (1,)), ((), ())), precision=HIGH, preferred_element_type=f32
+    )
+    table_sum = all_sum(table_part)
+    feed_gain_sum = all_sum(feed_gain_part)
+    gain_one_sum = all_sum(gain_one_part)
+
+    def my_half(block):
+        size = block.shape[0] // 2
+        return lax.dynamic_slice_in_dim(block, side * size, size, 0)
+
+    return (
+        result[None],
+        input_gradient[None],
+        my_half(gain_one_sum),
+        projection_out[0],
+        projection_out[1],
+        projection_out[2],
+        output_out,
+        my_half(table_sum),
+        my_half(feed_gain_sum),
+        gate_out,
+        up_out,
+        down_out,
+    )
+
+
+def fetch_columns(weight, core, swap_x, swap_core):
+    count = weight.shape[0] // 2
+    part = swap_x(lax.dynamic_slice_in_dim(weight, core * count, count, 0))
+    return part, swap_core(part)
+
+
 def solution(mesh):
     placed = (
         P("wsh", "ctx", None),
@@ -368,8 +1119,9 @@
         P("wsh", None),
         P("wsh", "ctx", None),
     )
+    step = grouped_body if mesh.shape["ctx"] == 16 else body
     return jax.shard_map(
-        body,
+        step,
         mesh=mesh,
         in_specs=placed,
         out_specs=(

time: 2180 us -> 752 us (0.34)
  waiting for transfers between devices: 1010 us -> 305 us
  local copies, waits for them, and re-layouts: 598 us -> 45.5 us
  matrix products: 210 us -> 77.9 us
  other arithmetic: 181 us -> 49.3 us
  Pallas kernels: 0 us -> 110 us
  blocking collectives: 77.2 us -> 0 us
  starting transfers between devices: 70.9 us -> 147 us
    reduce_scatter x10 -> x0, waiting for transfers between devices: 852 us -> none  [the longest x1 220 us: body(): lax.psum_scatter(gate_grad, 'ctx', scatter_dimension=1, tiled=True)]
    ppermute x94 -> x158, waiting for transfers between devices: 0.25 us -> 305 us  [spread(): return lax.ppermute(block, AXES, route)]
    while x578 -> x0, local copies, waits for them, and re-layouts: 255 us -> none
    reshape x49 -> x1, local copies, waits for them, and re-layouts: 204 us -> 0.02 us  [grouped_body(): lines = diagonals[:, :2].reshape(heads, SPAN_ROW)]
    dot_general x181 -> x42, matrix products: 210 us -> 77.9 us  [the longest x1 9.37 us: grouped_body(): jnp.einsum('td,fd->tf', outer_low, down_mine, preferred_element_type=f32)]
    pallas_call x0 -> x12, Pallas kernels: none -> 110 us  [the longest x5 36.6 us: forward_call(): pl.pallas_call(functools.partial(forward_kernel, count, first, last), gri...]
    all_gather x7 -> x0, waiting for transfers between devices: 103 us -> none  [the longest x1 71 us: body(): lax.all_gather(down_weight, 'wsh', axis=0, tiled=True)]
    slice x48 -> x4, local copies, waits for them, and re-layouts: 102 us -> 1.14 us  [the longest x1 0.9 us: grouped_body(): lines = diagonals[:, :2].reshape(heads, SPAN_ROW)]
  transfers between devices with their start and end apart: 116 -> 158, of which waited for: 16 -> 44; matrix products, arithmetic and copies ran while one was open for 43% -> 22% of each run, Pallas kernels for 0% -> 15%
where the time goes in v1:
time: 752 us; the launch traced here: 740 us
  waiting for transfers between devices  305 us (41%)
  starting transfers between devices  147 us (20%)
  Pallas kernels  110 us (15%)
  matrix products  77.9 us (10%)
  other arithmetic  49.3 us (7%)
  local copies, waits for them, and re-layouts  45.5 us (6%)
    ppermute x158, waiting for transfers between devices, spread(): return lax.ppermute(block, AXES, route)  305 us
    ppermute x158, starting transfers between devices, spread(): return lax.ppermute(block, AXES, route)  147 us
    pallas_call x5, Pallas kernels, forward_call(): pl.pallas_call(functools.partial(forward_kernel, count, first, last), gri...  36.6 us
    pallas_call x5, Pallas kernels, key_call(): pl.pallas_call(functools.partial(key_kernel, count, first, last), grid_sp...  35.2 us
    pallas_call x1, Pallas kernels, query_call(): pl.pallas_call(functools.partial(query_kernel, blocks), grid_spec=pltpu.P...  33.3 us
    unnamed x281, local copies, waits for them, and re-layouts  30 us
  transfers between devices with their start and end apart: 158, of which 44 were waited for; matrix products, arithmetic and copies ran while one was open for 22% of the time, Pallas kernels for 15%

profile of v1, /device:TPU:0, one launch (start us, length us, event | category | flops | bytes accessed | tf_op | source)
XLA Modules:
  0.0 740.0 jit_solution(17715513582611508138)
XLA Ops:
  5.3 2.9 collective-permute-start.5
  12.3 22.5 %collective-permute-start.3 = (f32[1,1]{1,0:T(1,128)}, f32[1,1]{1,0:T(1,128)}, u32[]{:S(2)}, u32[]{:S(2)}) collective-permute-start(f32[1,1]{1,0:T(1,128)} %bitcast.2), channel_id=1, source_target_pairs={{0,1},{1,0},{2,3},{3,2},{4,5},{5,4},{6,7},{7,6},{8,9},{9,8},{10,11... | collective-permute-start | bytes 20 | tf_op jit(solution)/shard_map/ppermute | solution.py:727
  43.3 5.2 bias_tiles.1
  49.1 10.3 %collective-permute-done.43 = bf16[736]{0:T(1024)(128)(2,1)S(1)} collective-permute-done((bf16[736]{0:T(1024)(128)(2,1)S(1)}, bf16[736]{0:T(1024)(128)(2,1)S(1)}, u32[]{:S(2)}, u32[]{:S(2)}) %collective-permute-start.43) | collective-permute-done | bytes 1504 | tf_op jit(solution)/shard_map/ppermute | solution.py:727
  62.4 2.4 maximum_select_fusion.5
  65.0 8.5 %collective-permute-done.47 = bf16[256,1472]{0,1:T(8,128)(2,1)S(1)} collective-permute-done((bf16[256,1472]{0,1:T(8,128)(2,1)}, bf16[256,1472]{0,1:T(8,128)(2,1)S(1)}, u32[]{:S(2)}, u32[]{:S(2)}) %collective-permute-start.47) | collective-permute-done | bytes 753696 | tf_op jit(solution)/shard_map/ppermute | solution.py:727
  79.7 3.0 multiply_convert_fusion.1
  88.2 6.2 attention_forward.5
  98.7 3.2 collective-permute-done.19.refs_3_
  106.0 3.7 collective-permute-done.24.refs_5_
  115.2 7.9 %attention_forward.6 = (f32[256,384]{1,0:T(8,128)}, f32[256,768]{1,0:T(8,128)}) custom-call(s32[6]{0:T(128)} %stack.220.info_ref, bf16[256,384]{1,0:T(8,128)(2,1)} %get-tuple-element.133.refs_0_.refs_2_.query_ref, bf16[256,384]{1,0:T(8,128)(2,1)} %copy-done.39, bf16[256,384]{1,0:T(8,128)(2,1)} %copy-done.50, bf16[256,384]{1,0:T(8,128)(2,1)} %copy-done.43, ...), custom_call_target="tpu_custom_call" | custom-call | flops 2415919104 | bytes 3538944 | tf_op jit(solution)/shard_map/attention_forward/pallas_call | solution.py:513
  128.4 4.5 collective-permute-done.25.refs_5_
  137.4 7.9 %attention_forward.7 = (f32[256,384]{1,0:T(8,128)}, f32[256,768]{1,0:T(8,128)}) custom-call(s32[6]{0:T(128)} %stack.215.info_ref, bf16[256,384]{1,0:T(8,128)(2,1)} %get-tuple-element.133.refs_0_.refs_2_.query_ref, bf16[256,384]{1,0:T(8,128)(2,1)} %copy-done.37, bf16[256,384]{1,0:T(8,128)(2,1)} %copy-done.49, bf16[256,384]{1,0:T(8,128)(2,1)} %copy-done.34, ...), custom_call_target="tpu_custom_call" | custom-call | flops 2415919104 | bytes 3538944 | tf_op jit(solution)/shard_map/attention_forward/pallas_call | solution.py:513
  151.7 2.9 collective-permute-done.15.refs_3_
  159.7 7.9 %attention_forward.8 = (f32[256,384]{1,0:T(8,128)}, f32[256,768]{1,0:T(8,128)}) custom-call(s32[6]{0:T(128)} %stack.210.info_ref, bf16[256,384]{1,0:T(8,128)(2,1)} %get-tuple-element.133.refs_0_.refs_2_.query_ref, bf16[256,384]{1,0:T(8,128)(2,1)} %copy-done.38, bf16[256,384]{1,0:T(8,128)(2,1)} %copy-done.48, bf16[256,384]{1,0:T(8,128)(2,1)} %copy-done.40, ...), custom_call_target="tpu_custom_call" | custom-call | flops 2415919104 | bytes 3538944 | tf_op jit(solution)/shard_map/attention_forward/pallas_call | solution.py:513
  168.4 6.8 attention_forward.9
  187.5 4.4 multiply_reduce_fusion.2
  192.5 3.5 fusion.14
  196.6 5.4 fusion.18
  202.0 9.4 %multiply_convert_fusion.3 = (bf16[1024,896]{1,0:T(8,128)(2,1)S(1)}, bf16[1024,896]{1,0:T(8,128)(2,1)S(1)}, bf16[1024,896]{1,0:T(8,128)(2,1)}) fusion(f32[1024,896]{1,0:T(8,128)} %fusion.18, f32[1024,896]{1,0:T(8,128)S(1)} %fusion.14, bf16[1024,1472]{0,1:T(8,128)(2,1)S(1)} %copy-done.7, bf16[1792,1472]{0,1:T(8,128)(2,1)} %param.26, s32[]{:T(128)S(6)} %select_n.402), kind=kOutput, calls=%fused_computation.18 | convolution fusion | flops 2724986880 | bytes 18497540 | tf_op jit(solution)/shard_map/td,fd->tf/dot_general | solution.py:916
  211.4 4.7 convolution_convert_fusion.2
  216.1 5.2 fusion.16
  221.3 4.5 convolution_convert_fusion
  225.8 5.7 fusion.149
  231.5 4.5 convolution_convert_fusion.1
  235.9 5.9 multiply_reduce_fusion
  252.8 3.9 collective-permute-done.57
  258.1 33.3 %attention_query_grad.1 = (f32[256,384]{1,0:T(8,128)}, f32[3,8,1024]{2,1,0:T(8,128)}) custom-call(s32[18]{0:T(128)} %stack.227.info_ref, bf16[256,384]{1,0:T(8,128)(2,1)} %get-tuple-element.133.refs_0_.refs_2_.query_ref, bf16[256,384]{1,0:T(8,128)(2,1)} %fusion.74.refs_4_.grad_ref, f32[256,384]{1,0:T(8,128)} %get-tuple-element.48.out_ref, ...), custom_call_target="tpu_custom_call" | custom-call | flops 9663676416 | bytes 6291456 | tf_op jit(solution)/shard_map/attention_query_grad/pallas_call | solution.py:595
  302.0 3.0 collective-permute-done.53.refs_2_
  331.1 25.6 %collective-permute-done.68.refs_16_ = f32[8,256]{1,0:T(8,128)S(1)} collective-permute-done((f32[8,256]{1,0:T(8,128)S(1)}, f32[8,256]{1,0:T(8,128)S(1)}, u32[]{:S(2)}, u32[]{:S(2)}) %collective-permute-start.68) | collective-permute-done | bytes 8224 | tf_op jit(solution)/shard_map/ppermute | solution.py:727
  356.7 3.0 collective-permute-start.69
  371.7 6.1 attention_key_grad.5
  378.0 26.2 %collective-permute-done.79.refs_6_ = bf16[256,384]{1,0:T(8,128)(2,1)} collective-permute-done((bf16[256,384]{1,0:T(8,128)(2,1)}, bf16[256,384]{1,0:T(8,128)(2,1)}, u32[]{:S(2)}, u32[]{:S(2)}) %collective-permute-start.79) | collective-permute-done | bytes 196640 | tf_op jit(solution)/shard_map/ppermute | solution.py:727
  404.7 7.7 %attention_key_grad.6 = (f32[256,384]{1,0:T(8,128)}, f32[256,384]{1,0:T(8,128)}) custom-call(s32[6]{0:T(128)} %stack.220.info_ref, bf16[256,384]{1,0:T(8,128)(2,1)} %copy-done.19, bf16[256,384]{1,0:T(8,128)(2,1)} %copy-done.18, bf16[256,384]{1,0:T(8,128)(2,1)} %collective-permute-done.51.refs_2_, bf16[256,384]{1,0:T(8,128)(2,1)} %copy-done.70, ...), custom_call_target="tpu_custom_call" | custom-call | flops 3221225472 | bytes 3538944 | tf_op jit(solution)/shard_map/attention_key_grad/pallas_call | solution.py:679
  415.5 7.6 %attention_key_grad.7 = (f32[256,384]{1,0:T(8,128)}, f32[256,384]{1,0:T(8,128)}) custom-call(s32[6]{0:T(128)} %stack.215.info_ref, bf16[256,384]{1,0:T(8,128)(2,1)} %copy-done.19, bf16[256,384]{1,0:T(8,128)(2,1)} %copy-done.18, bf16[256,384]{1,0:T(8,128)(2,1)} %collective-permute-done.52.refs_2_, bf16[256,384]{1,0:T(8,128)(2,1)} %copy-done.68, ...), custom_call_target="tpu_custom_call" | custom-call | flops 3221225472 | bytes 3538944 | tf_op jit(solution)/shard_map/attention_key_grad/pallas_call | solution.py:679
  423.0 21.9 %collective-permute-done.90.refs_14_ = f32[8,256]{1,0:T(8,128)S(1)} collective-permute-done((f32[8,256]{1,0:T(8,128)S(1)}, f32[8,256]{1,0:T(8,128)S(1)}, u32[]{:S(2)}, u32[]{:S(2)}) %collective-permute-start.90) | collective-permute-done | bytes 8224 | tf_op jit(solution)/shard_map/ppermute | solution.py:727
  445.5 3.2 add_convert_fusion.3
  451.2 2.8 add_convert_fusion.7
  454.0 2.3 collective-permute-done.80.refs_6_
  461.3 7.6 %attention_key_grad.8 = (f32[256,384]{1,0:T(8,128)}, f32[256,384]{1,0:T(8,128)}) custom-call(s32[6]{0:T(128)} %stack.210.info_ref, bf16[256,384]{1,0:T(8,128)(2,1)} %copy-done.19, bf16[256,384]{1,0:T(8,128)(2,1)} %copy-done.18, bf16[256,384]{1,0:T(8,128)(2,1)} %copy-done.64, bf16[256,384]{1,0:T(8,128)(2,1)} %copy-done.66, bf16[256,384]{1,0:T(8,128)(2,1)} %copy-done.65, ...), custom_call_target="tpu_custom_call" | custom-call | flops 3221225472 | bytes 3538944 | tf_op jit(solution)/shard_map/attention_key_grad/pallas_call | solution.py:679
  472.0 3.5 fusion.36
  481.0 2.5 fusion.41
  485.4 3.4 collective-permute-start.45
  489.6 6.3 attention_key_grad.9
  497.1 4.9 fusion.33
  507.8 15.1 %collective-permute-done.114 = f32[1472]{0:T(1024)S(1)} collective-permute-done((f32[1472]{0:T(1024)S(1)}, f32[1472]{0:T(1024)S(1)}, u32[]{:S(2)}, u32[]{:S(2)}) %collective-permute-start.114) | collective-permute-done | bytes 5920 | tf_op jit(solution)/shard_map/ppermute | solution.py:727
  524.3 2.2 collective-permute-done.115
  526.7 4.4 collective-permute-done.116
  531.1 9.3 %collective-permute-start.117 = (f32[1472]{0:T(1024)S(1)}, f32[1472]{0:T(1024)S(1)}, u32[]{:S(2)}, u32[]{:S(2)}) collective-permute-start(f32[1472]{0:T(1024)S(1)} %add.658), channel_id=1, source_target_pairs={{0,8},{1,9},{2,10},{3,11},{4,12},{5,13},{6,14},{7,15},{8,0},{9,1},... | collective-permute-start | bytes 17672 | tf_op jit(solution)/shard_map/ppermute | solution.py:727
  543.6 4.6 multiply_convert_fusion.6
  552.2 2.1 add_convert_fusion.2
  555.2 5.7 collective-permute-done.126
  563.0 2.1 add_convert_fusion.6
  567.9 5.4 collective-permute-start.128
  573.4 5.6 collective-permute-done.120
  581.5 50.8 %collective-permute-done.128 = bf16[1,48,736]{2,1,0:T(8,128)(2,1)S(1)} collective-permute-done((bf16[1,48,736]{2,1,0:T(8,128)(2,1)S(1)}, bf16[1,48,736]{2,1,0:T(8,128)(2,1)S(1)}, u32[]{:S(2)}, u32[]{:S(2)}) %collective-permute-start.128) | collective-permute-done | bytes 70688 | tf_op jit(solution)/shard_map/ppermute | solution.py:727
  632.7 3.7 collective-permute-done.129
  637.0 29.4 %collective-permute-done.122 = bf16[3,48,736]{2,1,0:T(8,128)(2,1)S(1)} collective-permute-done((bf16[3,48,736]{2,1,0:T(8,128)(2,1)S(1)}, bf16[3,48,736]{2,1,0:T(8,128)(2,1)S(1)}, u32[]{:S(2)}, u32[]{:S(2)}) %collective-permute-start.122) | collective-permute-done | bytes 212000 | tf_op jit(solution)/shard_map/ppermute | solution.py:727
  672.4 14.7 %collective-permute-done.155 = bf16[448,1472]{1,0:T(8,128)(2,1)S(1)} collective-permute-done((bf16[448,1472]{1,0:T(8,128)(2,1)S(1)}, bf16[448,1472]{1,0:T(8,128)(2,1)S(1)}, u32[]{:S(2)}, u32[]{:S(2)}) %collective-permute-start.155) | collective-permute-done | bytes 1318944 | tf_op jit(solution)/shard_map/ppermute | solution.py:727
  688.8 13.0 %collective-permute-done.149 = bf16[448,1472]{1,0:T(8,128)(2,1)S(1)} collective-permute-done((bf16[448,1472]{1,0:T(8,128)(2,1)S(1)}, bf16[448,1472]{1,0:T(8,128)(2,1)S(1)}, u32[]{:S(2)}, u32[]{:S(2)}) %collective-permute-start.149) | collective-permute-done | bytes 1318944 | tf_op jit(solution)/shard_map/ppermute | solution.py:727
  703.6 13.0 %collective-permute-done.143 = bf16[448,1472]{1,0:T(8,128)(2,1)S(1)} collective-permute-done((bf16[448,1472]{1,0:T(8,128)(2,1)S(1)}, bf16[448,1472]{1,0:T(8,128)(2,1)S(1)}, u32[]{:S(2)}, u32[]{:S(2)}) %collective-permute-start.143) | collective-permute-done | bytes 1318944 | tf_op jit(solution)/shard_map/ppermute | solution.py:727
  723.0 5.4 collective-permute-done.157
  729.3 5.9 collective-permute-done.151
  736.1 2.7 collective-permute-done.145
  (702 shorter events, 207.2 us)
Async XLA Ops:
  5.3 43.5 %collective-permute-start.5 = (bf16[368,1152]{1,0:T(8,128)(2,1)}, bf16[368,1152]{1,0:T(8,128)(2,1)}, u32[]{:S(2)}, u32[]{:S(2)}) collective-permute-start(bf16[368,1152]{1,0:T(8,128)(2,1)} %constant_dynamic-slice_fusion.17), channel_id=1, source_target_pairs={{0,1},{1,0},{2,3},{3,2},{4,5},{5,4},{6,7},{7,6},{8,9},{9,8},{10,11... | collective-permute-start | bytes 2543624 | tf_op jit(solution)/shard_map/ppermute | solution.py:727
  8.2 40.2 %collective-permute-start.4 = (bf16[736]{0:T(1024)(128)(2,1)S(1)}, bf16[736]{0:T(1024)(128)(2,1)S(1)}, u32[]{:S(2)}, u32[]{:S(2)}) collective-permute-start(bf16[736]{0:T(1024)(128)(2,1)S(1)} %copy-done.61), channel_id=1, source_target_pairs={{0,1},{1,0},{2,3},{3,2},{4,5},{5,4},{6,7},{7,6},{8,9},{9,8},{10,11... | collective-permute-start | bytes 4424 | tf_op jit(solution)/shard_map/ppermute | solution.py:727
  8.3 32.2 %collective-permute-start.17 = (bf16[16,6]{0,1:T(8,128)(2,1)S(1)}, bf16[16,6]{0,1:T(8,128)(2,1)S(1)}, u32[]{:S(2)}, u32[]{:S(2)}) collective-permute-start(bf16[16,6]{0,1:T(8,128)(2,1)S(1)} %copy-done.110), channel_id=1, source_target_pairs={{0,1},{1,0},{2,3},{3,2},{4,5},{5,4},{6,7},{7,6},{8,9},{9,8},{10,11... | collective-permute-start | bytes 584 | tf_op jit(solution)/shard_map/ppermute | solution.py:727
  11.5 47.9 %collective-permute-start.41 = (bf16[192,736]{0,1:T(8,128)(2,1)S(1)}, bf16[192,736]{0,1:T(8,128)(2,1)}, u32[]{:S(2)}, u32[]{:S(2)}) collective-permute-start(bf16[192,736]{0,1:T(8,128)(2,1)S(1)} %constant_dynamic-slice_fusion.16), channel_id=1, source_target_pairs={{0,1},{1,0},{2,3},{3,2},{4,5},{5,4},{6,7},{7,6},{8,9},{9,8},{10,11... | collective-permute-start | bytes 847880 | tf_op jit(solution)/shard_map/ppermute | solution.py:727
  12.3 27.3 %collective-permute-start.3 = (f32[1,1]{1,0:T(1,128)}, f32[1,1]{1,0:T(1,128)}, u32[]{:S(2)}, u32[]{:S(2)}) collective-permute-start(f32[1,1]{1,0:T(1,128)} %bitcast.2), channel_id=1, source_target_pairs={{0,1},{1,0},{2,3},{3,2},{4,5},{5,4},{6,7},{7,6},{8,9},{9,8},{10,11... | collective-permute-start | bytes 20 | tf_op jit(solution)/shard_map/ppermute | solution.py:727
  39.6 25.3 %collective-permute-start.1 = (bf16[256,1472]{0,1:T(8,128)(2,1)S(1)}, bf16[256,1472]{0,1:T(8,128)(2,1)}, u32[]{:S(2)}, u32[]{:S(2)}) collective-permute-start(bf16[256,1472]{0,1:T(8,128)(2,1)S(1)} %bitcast.207), channel_id=1, source_target_pairs={{0,1},{1,0},{2,3},{3,2},{4,5},{5,4},{6,7},{7,6},{8,9},{9,8},{10,11... | collective-permute-start | bytes 2261000 | tf_op jit(solution)/shard_map/ppermute | solution.py:727
  40.5 18.9 %collective-permute-start.43 = (bf16[736]{0:T(1024)(128)(2,1)S(1)}, bf16[736]{0:T(1024)(128)(2,1)S(1)}, u32[]{:S(2)}, u32[]{:S(2)}) collective-permute-start(bf16[736]{0:T(1024)(128)(2,1)S(1)} %copy-done.62), channel_id=1, source_target_pairs={{0,1},{1,0},{2,3},{3,2},{4,5},{5,4},{6,7},{7,6},{8,9},{9,8},{10,11... | collective-permute-start | bytes 4424 | tf_op jit(solution)/shard_map/ppermute | solution.py:727
  48.5 25.0 %collective-permute-start.47 = (bf16[256,1472]{0,1:T(8,128)(2,1)}, bf16[256,1472]{0,1:T(8,128)(2,1)S(1)}, u32[]{:S(2)}, u32[]{:S(2)}) collective-permute-start(bf16[256,1472]{0,1:T(8,128)(2,1)} %bitcast.28), channel_id=1, source_target_pairs={{0,1},{1,0},{2,3},{3,2},{4,5},{5,4},{6,7},{7,6},{8,9},{9,8},{10,11... | collective-permute-start | bytes 2261000 | tf_op jit(solution)/shard_map/ppermute | solution.py:727
  48.8 24.6 %collective-permute-start.6 = (bf16[368,1152]{1,0:T(8,128)(2,1)}, bf16[368,1152]{1,0:T(8,128)(2,1)S(1)}, u32[]{:S(2)}, u32[]{:S(2)}) collective-permute-start(bf16[368,1152]{1,0:T(8,128)(2,1)} %collective-permute-done.5), channel_id=1, source_target_pairs={{0,2},{1,3},{2,0},{3,1},{4,6},{5,7},{6,4},{7,5},{8,10},{9,11},{10,... | collective-permute-start | bytes 2543624 | tf_op jit(solution)/shard_map/ppermute | solution.py:727
  59.4 123.0 %collective-permute-start = (bf16[256,1472]{0,1:T(8,128)(2,1)S(1)}, bf16[256,1472]{0,1:T(8,128)(2,1)}, u32[]{:S(2)}, u32[]{:S(2)}) collective-permute-start(bf16[256,1472]{0,1:T(8,128)(2,1)S(1)} %bitcast.208), channel_id=1, source_target_pairs={{0,2},{1,3},{2,0},{3,1},{4,6},{5,7},{6,4},{7,5},{8,10},{9,11},{10,... | collective-permute-start | bytes 2261000 | tf_op jit(solution)/shard_map/ppermute | solution.py:727
  62.1 16.0 %collective-permute-start.46 = (bf16[256,1472]{0,1:T(8,128)(2,1)}, bf16[256,1472]{0,1:T(8,128)(2,1)S(1)}, u32[]{:S(2)}, u32[]{:S(2)}) collective-permute-start(bf16[256,1472]{0,1:T(8,128)(2,1)} %bitcast.28), channel_id=1, source_target_pairs={{0,2},{1,3},{2,0},{3,1},{4,6},{5,7},{6,4},{7,5},{8,10},{9,11},{10,... | collective-permute-start | bytes 2261000 | tf_op jit(solution)/shard_map/ppermute | solution.py:727
  64.8 119.9 %collective-permute-start.2 = (bf16[256,1472]{0,1:T(8,128)(2,1)}, bf16[256,1472]{0,1:T(8,128)(2,1)}, u32[]{:S(2)}, u32[]{:S(2)}) collective-permute-start(bf16[256,1472]{0,1:T(8,128)(2,1)} %collective-permute-done.1), channel_id=1, source_target_pairs={{0,2},{1,3},{2,0},{3,1},{4,6},{5,7},{6,4},{7,5},{8,10},{9,11},{10,... | collective-permute-start | bytes 2261000 | tf_op jit(solution)/shard_map/ppermute | solution.py:727
  82.6 11.7 %collective-permute-start.7 = (bf16[256,384]{1,0:T(8,128)(2,1)S(1)}, bf16[256,384]{1,0:T(8,128)(2,1)S(1)}, u32[]{:S(2)}, u32[]{:S(2)}) collective-permute-start(bf16[256,384]{1,0:T(8,128)(2,1)S(1)} %get-tuple-element.132.refs_1_.refs_0_), channel_id=1, source_target_pairs={{0,8},{1,9},{2,10},{3,11},{4,0},{5,1},{6,2},{7,3},{8,16},{9,17},{1... | collective-permute-start | bytes 589832 | tf_op jit(solution)/shard_map/ppermute | solution.py:727
  85.0 11.8 %collective-permute-start.12 = (bf16[256,384]{1,0:T(8,128)(2,1)S(1)}, bf16[256,384]{1,0:T(8,128)(2,1)S(1)}, u32[]{:S(2)}, u32[]{:S(2)}) collective-permute-start(bf16[256,384]{1,0:T(8,128)(2,1)S(1)} %get-tuple-element.131.refs_3_.refs_1_), channel_id=1, source_target_pairs={{0,4},{1,5},{2,6},{3,7},{4,12},{5,13},{6,14},{7,15},{8,0},{9,1},{1... | collective-permute-start | bytes 589832 | tf_op jit(solution)/shard_map/ppermute | solution.py:727
  109.7 15.4 %collective-permute-start.20 = (bf16[256,384]{1,0:T(8,128)(2,1)S(1)}, bf16[256,384]{1,0:T(8,128)(2,1)S(1)}, u32[]{:S(2)}, u32[]{:S(2)}) collective-permute-start(bf16[256,384]{1,0:T(8,128)(2,1)S(1)} %collective-permute-done.19.refs_3_), channel_id=1, source_target_pairs={{0,4},{1,5},{2,6},{3,7},{4,12},{5,13},{6,14},{7,15},{8,0},{9,1},{1... | collective-permute-start | bytes 589832 | tf_op jit(solution)/shard_map/ppermute | solution.py:727
  112.0 11.0 %collective-permute-start.13 = (bf16[256,384]{1,0:T(8,128)(2,1)S(1)}, bf16[256,384]{1,0:T(8,128)(2,1)S(1)}, u32[]{:S(2)}, u32[]{:S(2)}) collective-permute-start(bf16[256,384]{1,0:T(8,128)(2,1)S(1)} %collective-permute-done.12.refs_7_), channel_id=1, source_target_pairs={{0,4},{1,5},{2,6},{3,7},{4,12},{5,13},{6,14},{7,15},{8,0},{9,1},{1... | collective-permute-start | bytes 589832 | tf_op jit(solution)/shard_map/ppermute | solution.py:727
  132.9 14.4 %collective-permute-start.21 = (bf16[256,384]{1,0:T(8,128)(2,1)S(1)}, bf16[256,384]{1,0:T(8,128)(2,1)S(1)}, u32[]{:S(2)}, u32[]{:S(2)}) collective-permute-start(bf16[256,384]{1,0:T(8,128)(2,1)S(1)} %collective-permute-done.20.refs_3_), channel_id=1, source_target_pairs={{0,4},{1,5},{2,6},{3,7},{4,12},{5,13},{6,14},{7,15},{8,0},{9,1},{1... | collective-permute-start | bytes 589832 | tf_op jit(solution)/shard_map/ppermute | solution.py:727
  154.6 30.5 %collective-permute-start.51 = (bf16[256,384]{1,0:T(8,128)(2,1)}, bf16[256,384]{1,0:T(8,128)(2,1)}, u32[]{:S(2)}, u32[]{:S(2)}) collective-permute-start(bf16[256,384]{1,0:T(8,128)(2,1)} %get-tuple-element.133.refs_0_.refs_2_.query_ref), channel_id=1, source_target_pairs={{0,8},{1,9},{2,10},{3,11},{4,0},{5,1},{6,2},{7,3},{8,16},{9,17},{1... | collective-permute-start | bytes 589832 | tf_op jit(solution)/shard_map/ppermute | solution.py:727
  167.6 19.2 %collective-permute-start.74 = (bf16[256,384]{1,0:T(8,128)(2,1)}, bf16[256,384]{1,0:T(8,128)(2,1)}, u32[]{:S(2)}, u32[]{:S(2)}) collective-permute-start(bf16[256,384]{1,0:T(8,128)(2,1)} %get-tuple-element.133.refs_0_.refs_2_.query_ref), channel_id=1, source_target_pairs={{0,4},{1,5},{2,6},{3,7},{4,12},{5,13},{6,14},{7,15},{8,0},{9,1},{1... | collective-permute-start | bytes 589832 | tf_op jit(solution)/shard_map/ppermute | solution.py:727
  184.8 111.8 %collective-permute-start.109 = (bf16[256,384]{1,0:T(8,128)(2,1)}, bf16[256,384]{1,0:T(8,128)(2,1)}, u32[]{:S(2)}, u32[]{:S(2)}) collective-permute-start(bf16[256,384]{1,0:T(8,128)(2,1)} %get-tuple-element.133.refs_0_.refs_2_.query_ref), channel_id=1, source_target_pairs={{0,2},{1,3},{2,0},{3,1},{4,6},{5,7},{6,4},{7,5},{8,10},{9,11},{10,... | collective-permute-start | bytes 589832 | tf_op jit(solution)/shard_map/ppermute | solution.py:727
  185.0 111.6 %collective-permute-start.52 = (bf16[256,384]{1,0:T(8,128)(2,1)}, bf16[256,384]{1,0:T(8,128)(2,1)}, u32[]{:S(2)}, u32[]{:S(2)}) collective-permute-start(bf16[256,384]{1,0:T(8,128)(2,1)} %collective-permute-done.51.refs_2_), channel_id=1, source_target_pairs={{0,8},{1,9},{2,10},{3,11},{4,0},{5,1},{6,2},{7,3},{8,16},{9,17},{1... | collective-permute-start | bytes 589832 | tf_op jit(solution)/shard_map/ppermute | solution.py:727
  186.9 110.3 %collective-permute-start.75 = (bf16[256,384]{1,0:T(8,128)(2,1)}, bf16[256,384]{1,0:T(8,128)(2,1)}, u32[]{:S(2)}, u32[]{:S(2)}) collective-permute-start(bf16[256,384]{1,0:T(8,128)(2,1)} %collective-permute-done.74.refs_4_), channel_id=1, source_target_pairs={{0,4},{1,5},{2,6},{3,7},{4,12},{5,13},{6,14},{7,15},{8,0},{9,1},{1... | collective-permute-start | bytes 589832 | tf_op jit(solution)/shard_map/ppermute | solution.py:727
  251.8 42.3 %collective-permute-start.137 = (f32[1472]{0:T(1024)S(1)}, f32[1472]{0:T(1024)S(1)}, u32[]{:S(2)}, u32[]{:S(2)}) collective-permute-start(f32[1472]{0:T(1024)S(1)} %add.696), channel_id=1, source_target_pairs={{0,4},{1,5},{2,6},{3,7},{4,0},{5,1},{6,2},{7,3},{8,12},{9,13},{10,... | collective-permute-start | bytes 17672 | tf_op jit(solution)/shard_map/ppermute | solution.py:727
  301.9 11.2 %collective-permute-start.94 = (bf16[256,384]{1,0:T(8,128)(2,1)}, bf16[256,384]{1,0:T(8,128)(2,1)S(1)}, u32[]{:S(2)}, u32[]{:S(2)}) collective-permute-start(bf16[256,384]{1,0:T(8,128)(2,1)} %collective-permute-done.75.refs_4_), channel_id=1, source_target_pairs={{0,2},{1,3},{2,0},{3,1},{4,6},{5,7},{6,4},{7,5},{8,10},{9,11},{10,... | collective-permute-start | bytes 589832 | tf_op jit(solution)/shard_map/ppermute | solution.py:727
  325.9 119.5 %collective-permute-start.152 = (bf16[448,1472]{1,0:T(8,128)(2,1)S(1)}, bf16[448,1472]{1,0:T(8,128)(2,1)}, u32[]{:S(2)}, u32[]{:S(2)}) collective-permute-start(bf16[448,1472]{1,0:T(8,128)(2,1)S(1)} %constant_dynamic-slice_fusion.2), channel_id=1, source_target_pairs={{0,4},{1,5},{2,6},{3,7},{4,0},{5,1},{6,2},{7,3},{8,12},{9,13},{10,... | collective-permute-start | bytes 3956744 | tf_op jit(solution)/shard_map/ppermute | solution.py:727
  326.9 29.8 %collective-permute-start.112 = (f32[8,256]{1,0:T(8,128)S(1)}, f32[8,256]{1,0:T(8,128)S(1)}, u32[]{:S(2)}, u32[]{:S(2)}) collective-permute-start(f32[8,256]{1,0:T(8,128)S(1)} %fusion.89.refs_8_), channel_id=1, source_target_pairs={{0,2},{1,3},{2,0},{3,1},{4,6},{5,7},{6,4},{7,5},{8,10},{9,11},{10,... | collective-permute-start | bytes 24584 | tf_op jit(solution)/shard_map/ppermute | solution.py:727
  326.9 32.8 %collective-permute-start.88 = (f32[8,256]{1,0:T(8,128)S(1)}, f32[8,256]{1,0:T(8,128)S(1)}, u32[]{:S(2)}, u32[]{:S(2)}) collective-permute-start(f32[8,256]{1,0:T(8,128)S(1)} %fusion.89.refs_8_), channel_id=1, source_target_pairs={{0,8},{1,9},{2,10},{3,11},{4,0},{5,1},{6,2},{7,3},{8,16},{9,17},{1... | collective-permute-start | bytes 24584 | tf_op jit(solution)/shard_map/ppermute | solution.py:727
  328.1 28.6 %collective-permute-start.68 = (f32[8,256]{1,0:T(8,128)S(1)}, f32[8,256]{1,0:T(8,128)S(1)}, u32[]{:S(2)}, u32[]{:S(2)}) collective-permute-start(f32[8,256]{1,0:T(8,128)S(1)} %fusion.89.refs_8_), channel_id=1, source_target_pairs={{0,4},{1,5},{2,6},{3,7},{4,12},{5,13},{6,14},{7,15},{8,0},{9,1},{1... | collective-permute-start | bytes 24584 | tf_op jit(solution)/shard_map/ppermute | solution.py:727
  329.0 34.4 %collective-permute-start.78 = (bf16[256,384]{1,0:T(8,128)(2,1)S(1)}, bf16[256,384]{1,0:T(8,128)(2,1)}, u32[]{:S(2)}, u32[]{:S(2)}) collective-permute-start(bf16[256,384]{1,0:T(8,128)(2,1)S(1)} %copy-done.58), channel_id=1, source_target_pairs={{0,8},{1,9},{2,10},{3,11},{4,0},{5,1},{6,2},{7,3},{8,16},{9,17},{1... | collective-permute-start | bytes 589832 | tf_op jit(solution)/shard_map/ppermute | solution.py:727
  367.4 81.8 %collective-permute-start.146 = (bf16[448,1472]{1,0:T(8,128)(2,1)}, bf16[448,1472]{1,0:T(8,128)(2,1)}, u32[]{:S(2)}, u32[]{:S(2)}) collective-permute-start(bf16[448,1472]{1,0:T(8,128)(2,1)} %constant_dynamic-slice_fusion.5), channel_id=1, source_target_pairs={{0,4},{1,5},{2,6},{3,7},{4,0},{5,1},{6,2},{7,3},{8,12},{9,13},{10,... | collective-permute-start | bytes 3956744 | tf_op jit(solution)/shard_map/ppermute | solution.py:727
  368.9 35.4 %collective-permute-start.79 = (bf16[256,384]{1,0:T(8,128)(2,1)}, bf16[256,384]{1,0:T(8,128)(2,1)}, u32[]{:S(2)}, u32[]{:S(2)}) collective-permute-start(bf16[256,384]{1,0:T(8,128)(2,1)} %collective-permute-done.78.refs_6_), channel_id=1, source_target_pairs={{0,8},{1,9},{2,10},{3,11},{4,0},{5,1},{6,2},{7,3},{8,16},{9,17},{1... | collective-permute-start | bytes 589832 | tf_op jit(solution)/shard_map/ppermute | solution.py:727
  369.0 35.2 %collective-permute-start.59 = (bf16[256,384]{1,0:T(8,128)(2,1)}, bf16[256,384]{1,0:T(8,128)(2,1)}, u32[]{:S(2)}, u32[]{:S(2)}) collective-permute-start(bf16[256,384]{1,0:T(8,128)(2,1)} %collective-permute-done.58.refs_8_), channel_id=1, source_target_pairs={{0,4},{1,5},{2,6},{3,7},{4,12},{5,13},{6,14},{7,15},{8,0},{9,1},{1... | collective-permute-start | bytes 589832 | tf_op jit(solution)/shard_map/ppermute | solution.py:727
  377.8 34.6 %collective-permute-start.99 = (f32[8,256]{1,0:T(8,128)}, f32[8,256]{1,0:T(8,128)S(1)}, u32[]{:S(2)}, u32[]{:S(2)}) collective-permute-start(f32[8,256]{1,0:T(8,128)} %copy-done.96), channel_id=1, source_target_pairs={{0,2},{1,3},{2,0},{3,1},{4,6},{5,7},{6,4},{7,5},{8,10},{9,11},{10,... | collective-permute-start | bytes 24584 | tf_op jit(solution)/shard_map/ppermute | solution.py:727
  412.4 45.3 %collective-permute-start.140 = (bf16[448,1472]{1,0:T(8,128)(2,1)}, bf16[448,1472]{1,0:T(8,128)(2,1)}, u32[]{:S(2)}, u32[]{:S(2)}) collective-permute-start(bf16[448,1472]{1,0:T(8,128)(2,1)} %constant_dynamic-slice_fusion.8), channel_id=1, source_target_pairs={{0,4},{1,5},{2,6},{3,7},{4,0},{5,1},{6,2},{7,3},{8,12},{9,13},{10,... | collective-permute-start | bytes 3956744 | tf_op jit(solution)/shard_map/ppermute | solution.py:727
  413.4 31.5 %collective-permute-start.90 = (f32[8,256]{1,0:T(8,128)S(1)}, f32[8,256]{1,0:T(8,128)S(1)}, u32[]{:S(2)}, u32[]{:S(2)}) collective-permute-start(f32[8,256]{1,0:T(8,128)S(1)} %copy-done.97), channel_id=1, source_target_pairs={{0,8},{1,9},{2,10},{3,11},{4,0},{5,1},{6,2},{7,3},{8,16},{9,17},{1... | collective-permute-start | bytes 24584 | tf_op jit(solution)/shard_map/ppermute | solution.py:727
  413.5 31.4 %collective-permute-start.70 = (f32[8,256]{1,0:T(8,128)S(1)}, f32[8,256]{1,0:T(8,128)S(1)}, u32[]{:S(2)}, u32[]{:S(2)}) collective-permute-start(f32[8,256]{1,0:T(8,128)S(1)} %copy-done.93), channel_id=1, source_target_pairs={{0,4},{1,5},{2,6},{3,7},{4,12},{5,13},{6,14},{7,15},{8,0},{9,1},{1... | collective-permute-start | bytes 24584 | tf_op jit(solution)/shard_map/ppermute | solution.py:727
  444.9 24.0 %collective-permute-start.49 = (bf16[2,256,1472]{1,2,0:T(8,128)(2,1)}, bf16[2,256,1472]{1,2,0:T(8,128)(2,1)}, u32[]{:S(2)}, u32[]{:S(2)}) collective-permute-start(bf16[2,256,1472]{1,2,0:T(8,128)(2,1)} %pad_maximum_fusion.1), channel_id=1, source_target_pairs={{0,2},{1,3},{2,0},{3,1},{4,6},{5,7},{6,4},{7,5},{8,10},{9,11},{10,... | collective-permute-start | bytes 4521992 | tf_op jit(solution)/shard_map/ppermute | solution.py:727
  448.7 29.1 %collective-permute-start.44 = (bf16[2,256,1472]{1,2,0:T(8,128)(2,1)}, bf16[2,256,1472]{1,2,0:T(8,128)(2,1)}, u32[]{:S(2)}, u32[]{:S(2)}) collective-permute-start(bf16[2,256,1472]{1,2,0:T(8,128)(2,1)} %pad_maximum_fusion), channel_id=1, source_target_pairs={{0,2},{1,3},{2,0},{3,1},{4,6},{5,7},{6,4},{7,5},{8,10},{9,11},{10,... | collective-permute-start | bytes 4521992 | tf_op jit(solution)/shard_map/ppermute | solution.py:727
  460.0 23.5 %collective-permute-start.55 = (bf16[256,384]{1,0:T(8,128)(2,1)}, bf16[256,384]{1,0:T(8,128)(2,1)}, u32[]{:S(2)}, u32[]{:S(2)}) collective-permute-start(bf16[256,384]{1,0:T(8,128)(2,1)} %collective-permute-done.54.refs_2_), channel_id=1, source_target_pairs={{0,2},{1,3},{2,0},{3,1},{4,6},{5,7},{6,4},{7,5},{8,10},{9,11},{10,... | collective-permute-start | bytes 589832 | tf_op jit(solution)/shard_map/ppermute | solution.py:727
  460.1 25.3 %collective-permute-start.67 = (f32[8,256]{1,0:T(8,128)S(1)}, f32[8,256]{1,0:T(8,128)S(1)}, u32[]{:S(2)}, u32[]{:S(2)}) collective-permute-start(f32[8,256]{1,0:T(8,128)S(1)} %collective-permute-done.66.refs_6_), channel_id=1, source_target_pairs={{0,2},{1,3},{2,0},{3,1},{4,6},{5,7},{6,4},{7,5},{8,10},{9,11},{10,... | collective-permute-start | bytes 24584 | tf_op jit(solution)/shard_map/ppermute | solution.py:727
  460.7 28.2 %collective-permute-start.72 = (f32[8,256]{1,0:T(8,128)S(1)}, f32[8,256]{1,0:T(8,128)S(1)}, u32[]{:S(2)}, u32[]{:S(2)}) collective-permute-start(f32[8,256]{1,0:T(8,128)S(1)} %collective-permute-done.71.refs_8_), channel_id=1, source_target_pairs={{0,2},{1,3},{2,0},{3,1},{4,6},{5,7},{6,4},{7,5},{8,10},{9,11},{10,... | collective-permute-start | bytes 24584 | tf_op jit(solution)/shard_map/ppermute | solution.py:727
  476.1 74.8 %collective-permute-start.153 = (bf16[448,1472]{1,0:T(8,128)(2,1)}, bf16[448,1472]{1,0:T(8,128)(2,1)}, u32[]{:S(2)}, u32[]{:S(2)}) collective-permute-start(bf16[448,1472]{1,0:T(8,128)(2,1)} %add_convert_fusion.3), channel_id=1, source_target_pairs={{1,9},{3,11},{5,13},{7,15},{24,16},{26,18},{28,20},{30,22}} | collective-permute-start | bytes 3956744 | tf_op jit(solution)/shard_map/ppermute | solution.py:727
  477.8 11.1 %collective-permute-start.62 = (bf16[256,384]{1,0:T(8,128)(2,1)S(1)}, bf16[256,384]{1,0:T(8,128)(2,1)S(1)}, u32[]{:S(2)}, u32[]{:S(2)}) collective-permute-start(bf16[256,384]{1,0:T(8,128)(2,1)S(1)} %collective-permute-done.61.refs_4_), channel_id=1, source_target_pairs={{0,2},{1,3},{2,0},{3,1},{4,6},{5,7},{6,4},{7,5},{8,10},{9,11},{10,... | collective-permute-start | bytes 589832 | tf_op jit(solution)/shard_map/ppermute | solution.py:727
  483.5 78.4 %collective-permute-start.147 = (bf16[448,1472]{1,0:T(8,128)(2,1)}, bf16[448,1472]{1,0:T(8,128)(2,1)}, u32[]{:S(2)}, u32[]{:S(2)}) collective-permute-start(bf16[448,1472]{1,0:T(8,128)(2,1)} %add_convert_fusion.7), channel_id=1, source_target_pairs={{1,9},{3,11},{5,13},{7,15},{24,16},{26,18},{28,20},{30,22}} | collective-permute-start | bytes 3956744 | tf_op jit(solution)/shard_map/ppermute | solution.py:727
  485.4 58.1 %collective-permute-start.45 = (bf16[256,1472]{0,1:T(8,128)(2,1)}, bf16[256,1472]{0,1:T(8,128)(2,1)}, u32[]{:S(2)}, u32[]{:S(2)}) collective-permute-start(bf16[256,1472]{0,1:T(8,128)(2,1)} %fusion.41), channel_id=1, source_target_pairs={{0,1},{1,0},{2,3},{3,2},{4,5},{5,4},{6,7},{7,6},{8,9},{9,8},{10,11... | collective-permute-start | bytes 2261000 | tf_op jit(solution)/shard_map/ppermute | solution.py:727
  488.9 54.7 %collective-permute-start.50 = (bf16[256,1472]{0,1:T(8,128)(2,1)}, bf16[256,1472]{0,1:T(8,128)(2,1)}, u32[]{:S(2)}, u32[]{:S(2)}) collective-permute-start(bf16[256,1472]{0,1:T(8,128)(2,1)} %fusion.36), channel_id=1, source_target_pairs={{0,1},{1,0},{2,3},{3,2},{4,5},{5,4},{6,7},{7,6},{8,9},{9,8},{10,11... | collective-permute-start | bytes 2261000 | tf_op jit(solution)/shard_map/ppermute | solution.py:727
  505.6 17.3 %collective-permute-start.114 = (f32[1472]{0:T(1024)S(1)}, f32[1472]{0:T(1024)S(1)}, u32[]{:S(2)}, u32[]{:S(2)}) collective-permute-start(f32[1472]{0:T(1024)S(1)} %add.655), channel_id=1, source_target_pairs={{0,1},{1,0},{2,3},{3,2},{4,5},{5,4},{6,7},{7,6},{8,9},{9,8},{10,11... | collective-permute-start | bytes 17672 | tf_op jit(solution)/shard_map/ppermute | solution.py:727
  531.1 11.0 %collective-permute-start.117 = (f32[1472]{0:T(1024)S(1)}, f32[1472]{0:T(1024)S(1)}, u32[]{:S(2)}, u32[]{:S(2)}) collective-permute-start(f32[1472]{0:T(1024)S(1)} %add.658), channel_id=1, source_target_pairs={{0,8},{1,9},{2,10},{3,11},{4,12},{5,13},{6,14},{7,15},{8,0},{9,1},... | collective-permute-start | bytes 17672 | tf_op jit(solution)/shard_map/ppermute | solution.py:727
  542.1 38.4 %collective-permute-start.141 = (bf16[448,1472]{1,0:T(8,128)(2,1)S(1)}, bf16[448,1472]{1,0:T(8,128)(2,1)S(1)}, u32[]{:S(2)}, u32[]{:S(2)}) collective-permute-start(bf16[448,1472]{1,0:T(8,128)(2,1)S(1)} %add_convert_fusion.11), channel_id=1, source_target_pairs={{1,9},{3,11},{5,13},{7,15},{24,16},{26,18},{28,20},{30,22}} | collective-permute-start | bytes 3956744 | tf_op jit(solution)/shard_map/ppermute | solution.py:727
  549.3 18.6 %collective-permute-start.118 = (bf16[3,192,736]{2,1,0:T(8,128)(2,1)S(1)}, bf16[3,192,736]{2,1,0:T(8,128)(2,1)S(1)}, u32[]{:S(2)}, u32[]{:S(2)}) collective-permute-start(bf16[3,192,736]{2,1,0:T(8,128)(2,1)S(1)} %pad_maximum_fusion.2), channel_id=1, source_target_pairs={{0,2},{1,3},{2,0},{3,1},{4,6},{5,7},{6,4},{7,5},{8,10},{9,11},{10,... | collective-permute-start | bytes 2543624 | tf_op jit(solution)/shard_map/ppermute | solution.py:727
  554.3 24.7 %collective-permute-start.120 = (bf16[3,192,736]{2,1,0:T(8,128)(2,1)S(1)}, bf16[3,192,736]{2,1,0:T(8,128)(2,1)S(1)}, u32[]{:S(2)}, u32[]{:S(2)}) collective-permute-start(bf16[3,192,736]{2,1,0:T(8,128)(2,1)S(1)} %fusion.26), channel_id=1, source_target_pairs={{0,1},{1,0},{2,3},{3,2},{4,5},{5,4},{6,7},{7,6},{8,9},{9,8},{10,11... | collective-permute-start | bytes 2543624 | tf_op jit(solution)/shard_map/ppermute | solution.py:727
  560.8 105.7 %collective-permute-start.154 = (bf16[448,1472]{1,0:T(8,128)(2,1)S(1)}, bf16[448,1472]{1,0:T(8,128)(2,1)S(1)}, u32[]{:S(2)}, u32[]{:S(2)}) collective-permute-start(bf16[448,1472]{1,0:T(8,128)(2,1)S(1)} %add_convert_fusion.2), channel_id=1, source_target_pairs={{9,17},{11,19},{13,21},{15,23},{16,8},{18,10},{20,12},{22,14}} | collective-permute-start | bytes 3956744 | tf_op jit(solution)/shard_map/ppermute | solution.py:727
  567.1 101.1 %collective-permute-start.148 = (bf16[448,1472]{1,0:T(8,128)(2,1)S(1)}, bf16[448,1472]{1,0:T(8,128)(2,1)S(1)}, u32[]{:S(2)}, u32[]{:S(2)}) collective-permute-start(bf16[448,1472]{1,0:T(8,128)(2,1)S(1)} %add_convert_fusion.6), channel_id=1, source_target_pairs={{9,17},{11,19},{13,21},{15,23},{16,8},{18,10},{20,12},{22,14}} | collective-permute-start | bytes 3956744 | tf_op jit(solution)/shard_map/ppermute | solution.py:727
  567.9 64.4 %collective-permute-start.128 = (bf16[1,48,736]{2,1,0:T(8,128)(2,1)S(1)}, bf16[1,48,736]{2,1,0:T(8,128)(2,1)S(1)}, u32[]{:S(2)}, u32[]{:S(2)}) collective-permute-start(bf16[1,48,736]{2,1,0:T(8,128)(2,1)S(1)} %constant_dynamic-slice_fusion.11), channel_id=1, source_target_pairs={{0,16},{1,17},{2,18},{3,19},{4,20},{5,21},{6,22},{7,23},{8,24},{9,... | collective-permute-start | bytes 211976 | tf_op jit(solution)/shard_map/ppermute | solution.py:727
  579.4 53.0 %collective-permute-start.121 = (bf16[3,96,736]{2,1,0:T(8,128)(2,1)S(1)}, bf16[3,96,736]{2,1,0:T(8,128)(2,1)S(1)}, u32[]{:S(2)}, u32[]{:S(2)}) collective-permute-start(bf16[3,96,736]{2,1,0:T(8,128)(2,1)S(1)} %constant_dynamic-slice_fusion.15), channel_id=1, source_target_pairs={{0,4},{1,5},{2,6},{3,7},{4,0},{5,1},{6,2},{7,3},{8,12},{9,13},{10,... | collective-permute-start | bytes 1271816 | tf_op jit(solution)/shard_map/ppermute | solution.py:727
  580.8 89.3 %collective-permute-start.142 = (bf16[448,1472]{1,0:T(8,128)(2,1)S(1)}, bf16[448,1472]{1,0:T(8,128)(2,1)S(1)}, u32[]{:S(2)}, u32[]{:S(2)}) collective-permute-start(bf16[448,1472]{1,0:T(8,128)(2,1)S(1)} %add_convert_fusion.10), channel_id=1, source_target_pairs={{9,17},{11,19},{13,21},{15,23},{16,8},{18,10},{20,12},{22,14}} | collective-permute-start | bytes 3956744 | tf_op jit(solution)/shard_map/ppermute | solution.py:727
  632.6 33.8 %collective-permute-start.122 = (bf16[3,48,736]{2,1,0:T(8,128)(2,1)S(1)}, bf16[3,48,736]{2,1,0:T(8,128)(2,1)S(1)}, u32[]{:S(2)}, u32[]{:S(2)}) collective-permute-start(bf16[3,48,736]{2,1,0:T(8,128)(2,1)S(1)} %constant_dynamic-slice_fusion.14), channel_id=1, source_target_pairs={{0,16},{1,17},{2,18},{3,19},{4,20},{5,21},{6,22},{7,23},{8,24},{9,... | collective-permute-start | bytes 635912 | tf_op jit(solution)/shard_map/ppermute | solution.py:727
  666.9 20.2 %collective-permute-start.155 = (bf16[448,1472]{1,0:T(8,128)(2,1)S(1)}, bf16[448,1472]{1,0:T(8,128)(2,1)S(1)}, u32[]{:S(2)}, u32[]{:S(2)}) collective-permute-start(bf16[448,1472]{1,0:T(8,128)(2,1)S(1)} %add_convert_fusion.1), channel_id=1, source_target_pairs={{2,10},{6,14},{8,0},{12,4},{19,27},{23,31},{25,17},{29,21}} | collective-permute-start | bytes 3956744 | tf_op jit(solution)/shard_map/ppermute | solution.py:727
  668.5 33.3 %collective-permute-start.149 = (bf16[448,1472]{1,0:T(8,128)(2,1)S(1)}, bf16[448,1472]{1,0:T(8,128)(2,1)S(1)}, u32[]{:S(2)}, u32[]{:S(2)}) collective-permute-start(bf16[448,1472]{1,0:T(8,128)(2,1)S(1)} %add_convert_fusion.5), channel_id=1, source_target_pairs={{2,10},{6,14},{8,0},{12,4},{19,27},{23,31},{25,17},{29,21}} | collective-permute-start | bytes 3956744 | tf_op jit(solution)/shard_map/ppermute | solution.py:727
  670.4 46.2 %collective-permute-start.143 = (bf16[448,1472]{1,0:T(8,128)(2,1)S(1)}, bf16[448,1472]{1,0:T(8,128)(2,1)S(1)}, u32[]{:S(2)}, u32[]{:S(2)}) collective-permute-start(bf16[448,1472]{1,0:T(8,128)(2,1)S(1)} %add_convert_fusion.9), channel_id=1, source_target_pairs={{2,10},{6,14},{8,0},{12,4},{19,27},{23,31},{25,17},{29,21}} | collective-permute-start | bytes 3956744 | tf_op jit(solution)/shard_map/ppermute | solution.py:727
  687.5 30.8 %collective-permute-start.156 = (bf16[224,1472]{1,0:T(8,128)(2,1)S(1)}, bf16[224,1472]{1,0:T(8,128)(2,1)S(1)}, u32[]{:S(2)}, u32[]{:S(2)}) collective-permute-start(bf16[224,1472]{1,0:T(8,128)(2,1)S(1)} %constant_dynamic-slice_fusion.1), channel_id=1, source_target_pairs={{0,2},{4,6},{10,8},{14,12},{17,19},{21,23},{27,25},{31,29}} | collective-permute-start | bytes 1978376 | tf_op jit(solution)/shard_map/ppermute | solution.py:727
  702.2 17.6 %collective-permute-start.150 = (bf16[224,1472]{1,0:T(8,128)(2,1)S(1)}, bf16[224,1472]{1,0:T(8,128)(2,1)S(1)}, u32[]{:S(2)}, u32[]{:S(2)}) collective-permute-start(bf16[224,1472]{1,0:T(8,128)(2,1)S(1)} %constant_dynamic-slice_fusion.4), channel_id=1, source_target_pairs={{0,2},{4,6},{10,8},{14,12},{17,19},{21,23},{27,25},{31,29}} | collective-permute-start | bytes 1978376 | tf_op jit(solution)/shard_map/ppermute | solution.py:727
  720.1 15.1 %collective-permute-start.151 = (bf16[112,1472]{1,0:T(8,128)(2,1)S(1)}, bf16[112,1472]{1,0:T(8,128)(2,1)S(1)}, u32[]{:S(2)}, u32[]{:S(2)}) collective-permute-start(bf16[112,1472]{1,0:T(8,128)(2,1)S(1)} %constant_dynamic-slice_fusion.3), channel_id=1, source_target_pairs={{0,1},{2,3},{4,5},{6,7},{8,9},{10,11},{12,13},{14,15},{17,16},{19,... | collective-permute-start | bytes 989192 | tf_op jit(solution)/shard_map/ppermute | solution.py:727
  721.7 17.2 %collective-permute-start.145 = (bf16[112,1472]{1,0:T(8,128)(2,1)S(1)}, bf16[112,1472]{1,0:T(8,128)(2,1)S(1)}, u32[]{:S(2)}, u32[]{:S(2)}) collective-permute-start(bf16[112,1472]{1,0:T(8,128)(2,1)S(1)} %constant_dynamic-slice_fusion.6), channel_id=1, source_target_pairs={{0,1},{2,3},{4,5},{6,7},{8,9},{10,11},{12,13},{14,15},{17,16},{19,... | collective-permute-start | bytes 989192 | tf_op jit(solution)/shard_map/ppermute | solution.py:727
  (219 other events, 3054.0 us)

commit v2 on v0

--- a/solution.py
+++ b/solution.py
@@ -1,6 +1,10 @@
+import functools
+
 import jax
 import jax.numpy as jnp
 from jax import lax
+from jax.experimental import pallas as pl
+from jax.experimental.pallas import tpu as pltpu
 from jax.sharding import PartitionSpec as P
 
 EPSILON = 1e-06
@@ -351,6 +355,925 @@
     )
 
 
+BLOCK = 256
+PAIR = 128
+SPAN_ROW = 1024
+CONTRACT_LAST = (((1,), (1,)), ((), ()))
+AXES = ("ctx", "wsh")
+LEFT_LANE, RIGHT_LANE, DEAD_LANE = 125, 126, 127
+NEAR, BEFORE, AFTER = 0, 1, 2
+
+
+def lanes(rows=BLOCK):
+    return lax.broadcasted_iota(jnp.int32, (rows, PAIR), 1)
+
+
+def only_head(block, second):
+    lane = lanes(block.shape[0])
+    keep = lane >= PAIR // 2 if second else lane < PAIR // 2
+    return jnp.where(keep, block, jnp.zeros_like(block))
+
+
+def pair_select(first, second):
+    return jnp.where(lanes(first.shape[0]) < PAIR // 2, first, second)
+
+
+def contract_last(left, right):
+    return lax.dot_general(left, right, CONTRACT_LAST, preferred_element_type=jnp.float32)
+
+
+def stack_heads(block):
+    return jnp.concatenate([only_head(block, False), only_head(block, True)], axis=0)
+
+
+def dead_rows(start, limit):
+    row = lax.broadcasted_iota(jnp.int32, (BLOCK, PAIR), 0)
+    return start + row >= limit
+
+
+def other_aux(start, limit, kind):
+    lane = lanes()
+    value = jnp.where(jnp.logical_and(lane < 48, lane % 8 < 6), 1.0, 0.0)
+    value = jnp.where(jnp.logical_and(lane == LEFT_LANE, kind == BEFORE), 1.0, value)
+    value = jnp.where(jnp.logical_and(lane == RIGHT_LANE, kind == AFTER), 1.0, value)
+    value = jnp.where(jnp.logical_and(lane == DEAD_LANE, dead_rows(start, limit)), MASKED, value)
+    return value.astype(jnp.bfloat16)
+
+
+def own_lanes(far_ref, head, heads):
+    lane = lanes()
+    value = jnp.where(lane == DEAD_LANE, 1.0, 0.0)
+    value = jnp.where(lane == LEFT_LANE, far_ref[head], value)
+    return jnp.where(lane == RIGHT_LANE, far_ref[heads + head], value)
+
+
+def parts_of(value):
+    first = value.astype(jnp.bfloat16).astype(jnp.float32)
+    second = (value - first).astype(jnp.bfloat16).astype(jnp.float32)
+    return first, second, value - first - second
+
+
+def place_parts(base, value, lane_start):
+    lane = lanes()
+    for spot, part in enumerate(parts_of(value)):
+        base = jnp.where(lane == lane_start + spot, part, base)
+    return base
+
+
+def kind_of(block, own):
+    return jnp.where(block < own, BEFORE, AFTER)
+
+
+def tiles_kernel(row_ref, tile_ref, turned_ref):
+    row = row_ref[0]
+    wide = pltpu.roll(
+        jnp.broadcast_to(row, (BLOCK, SPAN_ROW)), SPAN_ROW - 255, 1, stride=1, stride_axis=0
+    )
+    for spot in range(3):
+        tile = wide[:, spot * BLOCK : (spot + 1) * BLOCK]
+        tile_ref[0, spot] = tile.astype(jnp.bfloat16)
+        turned_ref[0, spot] = jnp.transpose(tile).astype(jnp.bfloat16)
+
+
+def bias_tiles(offset_rows):
+    heads = offset_rows.shape[0]
+    shape = jax.ShapeDtypeStruct((heads, 3, BLOCK, BLOCK), jnp.bfloat16)
+    spec = pl.BlockSpec((1, 3, BLOCK, BLOCK), lambda h: (h, 0, 0, 0))
+    return pl.pallas_call(
+        tiles_kernel,
+        grid=(heads,),
+        out_shape=(shape, shape),
+        in_specs=[pl.BlockSpec((1, 1, SPAN_ROW), lambda h: (h, 0, 0))],
+        out_specs=(spec, spec),
+        name="bias_tiles",
+    )(offset_rows[:, None, :])
+
+
+def view_spec(row, lane_block):
+    return pl.BlockSpec((BLOCK, PAIR), lambda p, i, f: (row, lane_block(p)))
+
+
+def tile_spec():
+    return pl.BlockSpec((2, 3, BLOCK, BLOCK), lambda p, i, f: (p, 0, 0, 0))
+
+
+def run_pairs(kernel, info, far, operands, in_specs, out_shape, out_specs, work, name):
+    pairs = 3
+    return pl.pallas_call(
+        kernel,
+        grid_spec=pltpu.PrefetchScalarGridSpec(
+            num_scalar_prefetch=2, grid=(pairs,), in_specs=in_specs, out_specs=out_specs
+        ),
+        out_shape=out_shape,
+        cost_estimate=pl.CostEstimate(
+            flops=2 * pairs * work * BLOCK * BLOCK * BLOCK,
+            bytes_accessed=pairs * work * BLOCK * PAIR * 2,
+            transcendentals=pairs * work * BLOCK * BLOCK,
+        ),
+        name=name,
+    )(info, far, *operands)
+
+
+def forward_kernel(count, near, first, last, heads, info_ref, far_ref, *refs):
+    refs = list(refs)
+    query_ref = refs.pop(0)
+    key_refs, refs = refs[:count], refs[count:]
+    value_refs, refs = refs[:count], refs[count:]
+    tile_ref = refs.pop(0) if near else None
+    pair = pl.program_id(0)
+    own = info_ref[0]
+    query = query_ref[...]
+    if first:
+        old_max = jnp.full((BLOCK, PAIR), MASKED, jnp.float32)
+        total = None
+    else:
+        max_ref, total_ref = refs.pop(0), refs.pop(0)
+        old_max, total = max_ref[...], total_ref[...]
+    keys = []
+    for spot in range(count):
+        block, limit = info_ref[1 + 2 * spot], info_ref[2 + 2 * spot]
+        kind = NEAR if near else kind_of(block, own)
+        keys.append(
+            jnp.concatenate([key_refs[spot][...], other_aux(block * BLOCK, limit, kind)], axis=1)
+        )
+    tops, weights = [], []
+    for head in range(2):
+        aux = own_lanes(far_ref, 2 * pair + head, heads).astype(jnp.bfloat16)
+        left = jnp.concatenate([only_head(query, head == 1), aux], axis=1)
+        scores = []
+        for spot in range(count):
+            score = contract_last(left, keys[spot])
+            if near:
+                place = jnp.clip(info_ref[1 + 2 * spot] - own, -1, 1) + 1
+                score = score + tile_ref[head, place].astype(jnp.float32)
+            scores.append(score)
+        top = functools.reduce(jnp.maximum, scores)
+        lane = head * (PAIR // 2)
+        top = jnp.maximum(old_max[:, lane : lane + 1], jnp.max(top, axis=1, keepdims=True))
+        tops.append(top)
+        weights.append([jnp.exp(score - top).astype(jnp.bfloat16) for score in scores])
+    new_max = pair_select(tops[0], tops[1])
+    ones = stack_heads(jnp.ones((BLOCK, PAIR), jnp.bfloat16))
+    update = None
+    for spot in range(count):
+        right = jnp.concatenate([stack_heads(value_refs[spot][...]), ones], axis=1)
+        left = jnp.concatenate([weights[0][spot], weights[1][spot]], axis=1)
+        part = jnp.dot(left, right, preferred_element_type=jnp.float32)
+        update = part if update is None else update + part
+    if not first:
+        factor = jnp.exp(old_max - new_max)
+        update = update + total * jnp.concatenate([factor, factor], axis=1)
+    if last:
+        out_ref, low_ref, aux_ref = refs
+        out = update[:, :PAIR] / update[:, PAIR:]
+        out_ref[...] = out
+        low_ref[...] = out.astype(jnp.bfloat16)
+        log = -(new_max + jnp.log(update[:, PAIR:]))
+        base = jnp.where(lanes() >= LEFT_LANE, 1.0, 0.0)
+        base = jnp.where(pair == 0, base, aux_ref[...])
+        for head in range(2):
+            lane = head * (PAIR // 2)
+            base = place_parts(base, log[:, lane : lane + 1], 8 * (2 * pair + head) + 3)
+        aux_ref[...] = base
+    else:
+        max_out, total_out = refs
+        max_out[...] = new_max
+        total_out[...] = update
+
+
+def forward_call(info, far, query, blocks, tiles, state, last):
+    count, near, first = len(blocks), tiles is not None, state is None
+    inner = query.shape[1]
+    pairs = inner // PAIR
+    in_specs = [view_spec(0, lambda p: p)]
+    in_specs += [view_spec(row, lambda p: p) for _, row in blocks]
+    in_specs += [view_spec(row, lambda p: p + pairs) for _, row in blocks]
+    operands = [query] + [array for array, _ in blocks] * 2
+    if near:
+        in_specs.append(tile_spec())
+        operands.append(tiles)
+    block = view_spec(0, lambda p: p)
+    double = pl.BlockSpec((BLOCK, 2 * PAIR), lambda p, i, f: (0, p))
+    if not first:
+        in_specs += [block, double]
+        operands += list(state)
+    f32 = functools.partial(jax.ShapeDtypeStruct, dtype=jnp.float32)
+    if last:
+        out_shape = (
+            f32((BLOCK, inner)),
+            jax.ShapeDtypeStruct((BLOCK, inner), jnp.bfloat16),
+            f32((BLOCK, PAIR)),
+        )
+        out_specs = (block, block, view_spec(0, lambda p: 0))
+    else:
+        out_shape = (f32((BLOCK, inner)), f32((BLOCK, 2 * inner)))
+        out_specs = (block, double)
+    kernel = functools.partial(forward_kernel, count, near, first, last, 2 * pairs)
+    return run_pairs(
+        kernel, info, far, operands, in_specs, out_shape, out_specs, 6 * count, "attention_forward"
+    )
+
+
+def head_aux(aux, head, start):
+    lane = lanes()
+    keep = jnp.logical_and(lane // 8 == head, jnp.logical_and(lane % 8 >= start, lane % 8 < start + 3))
+    return jnp.where(jnp.logical_and(keep, lane < 48), aux, 0.0)
+
+
+def query_kernel(count, near, first, last, heads, info_ref, far_ref, *refs):
+    refs = list(refs)
+    query_ref, grad_ref, aux_ref = refs.pop(0), refs.pop(0), refs.pop(0)
+    key_refs, refs = refs[:count], refs[count:]
+    value_refs, refs = refs[:count], refs[count:]
+    tile_ref = refs.pop(0) if near else None
+    pair = pl.program_id(0)
+    own = info_ref[0]
+    query, grad = query_ref[...], grad_ref[...]
+    aux = aux_ref[...].astype(jnp.float32)
+    total = None if first else refs.pop(0)[...]
+    lefts, grads = [], []
+    for head in range(2):
+        which = 2 * pair + head
+        mine = own_lanes(far_ref, which, heads) + head_aux(aux, which, 3)
+        lefts.append(jnp.concatenate([only_head(query, head == 1), mine.astype(jnp.bfloat16)], axis=1))
+        delta = head_aux(aux, which, 0).astype(jnp.bfloat16)
+        grads.append(jnp.concatenate([only_head(grad, head == 1), delta], axis=1))
+    if near:
+        diag_ref = refs.pop()
+        strips = [[jnp.zeros((BLOCK, BLOCK), jnp.float32)] * 3 for _ in range(2)]
+    lane = lanes()
+    for spot in range(count):
+        block, limit = info_ref[1 + 2 * spot], info_ref[2 + 2 * spot]
+        kind = NEAR if near else kind_of(block, own)
+        key, value = key_refs[spot][...], value_refs[spot][...]
+        side = other_aux(block * BLOCK, limit, kind)
+        wide_key = jnp.concatenate([key, side], axis=1)
+        wide_value = jnp.concatenate([value, jnp.where(lane < 48, side, jnp.zeros_like(side))], axis=1)
+        place = jnp.clip(block - own, -1, 1) + 1
+        pieces, counts = [], []
+        for head in range(2):
+            scores = contract_last(lefts[head], wide_key)
+            if near:
+                scores = scores + tile_ref[head, place].astype(jnp.float32)
+            score_grad = jnp.exp(scores) * contract_last(grads[head], wide_value)
+            if near:
+                strips[head] = [
+                    strip + jnp.where(place == spot_of, score_grad, 0.0)
+                    for spot_of, strip in enumerate(strips[head])
+                ]
+            pieces.append(score_grad.astype(jnp.bfloat16))
+            counts.append(jnp.where(lane == 4 * head + kind, 1.0, 0.0).astype(jnp.bfloat16))
+        right = jnp.concatenate([stack_heads(key), jnp.concatenate(counts, axis=0)], axis=1)
+        part = jnp.dot(jnp.concatenate(pieces, axis=1), right, preferred_element_type=jnp.float32)
+        total = part if total is None else total + part
+    if near:
+        rows = []
+        flip = (
+            lax.broadcasted_iota(jnp.int32, (BLOCK, BLOCK), 0)
+            + lax.broadcasted_iota(jnp.int32, (BLOCK, BLOCK), 1)
+            == BLOCK - 1
+        ).astype(jnp.float32)
+        for head in range(2):
+            wide = jnp.concatenate(strips[head] + [jnp.zeros((BLOCK, BLOCK), jnp.float32)], axis=1)
+            flipped = jnp.dot(flip, wide, precision=HIGH, preferred_element_type=jnp.float32)
+            turned = pltpu.roll(flipped, 0, 1, stride=1, stride_axis=0)
+            rows.append(jnp.sum(turned, axis=0, keepdims=True))
+        diag_ref[0] = jnp.concatenate(rows + [jnp.zeros((6, SPAN_ROW), jnp.float32)], axis=0)
+    if last:
+        low_ref, sum_ref = refs
+        low_ref[...] = total[:, :PAIR].astype(jnp.bfloat16)
+        sum_ref[0] = jnp.broadcast_to(jnp.sum(total[:, PAIR:], axis=0, keepdims=True), (8, PAIR))
+    else:
+        (total_ref,) = refs
+        total_ref[...] = total
+
+
+def query_call(info, far, query, grads, blocks, tiles, state, last):
+    count, near, first = len(blocks), tiles is not None, state is None
+    inner = query.shape[1]
+    pairs = inner // PAIR
+    own = view_spec(0, lambda p: p)
+    in_specs = [own, own, view_spec(0, lambda p: pairs)]
+    in_specs += [view_spec(row, lambda p: p) for _, row in blocks]
+    in_specs += [view_spec(row, lambda p: p + pairs) for _, row in blocks]
+    operands = [query, grads, grads] + [array for array, _ in blocks] * 2
+    if near:
+        in_specs.append(tile_spec())
+        operands.append(tiles)
+    double = pl.BlockSpec((BLOCK, 2 * PAIR), lambda p, i, f: (0, p))
+    if not first:
+        in_specs.append(double)
+        operands.append(state)
+    f32 = functools.partial(jax.ShapeDtypeStruct, dtype=jnp.float32)
+    if last:
+        out_shape = [jax.ShapeDtypeStruct((BLOCK, inner), jnp.bfloat16), f32((pairs, 8, PAIR))]
+        out_specs = [own, pl.BlockSpec((1, 8, PAIR), lambda p, i, f: (p, 0, 0))]
+    else:
+        out_shape, out_specs = [f32((BLOCK, 2 * inner))], [double]
+    if near:
+        out_shape.append(f32((pairs, 8, SPAN_ROW)))
+        out_specs.append(pl.BlockSpec((1, 8, SPAN_ROW), lambda p, i, f: (p, 0, 0)))
+    kernel = functools.partial(query_kernel, count, near, first, last, 2 * pairs)
+    return run_pairs(
+        kernel, info, far, operands, in_specs, out_shape, out_specs, 8 * count, "attention_query_grad"
+    )
+
+
+def key_kernel(count, near, first, last, heads, info_ref, far_ref, *refs):
+    refs = list(refs)
+    key_ref, value_ref = refs.pop(0), refs.pop(0)
+    query_refs, refs = refs[:count], refs[count:]
+    grad_refs, refs = refs[:count], refs[count:]
+    aux_refs, refs = refs[:count], refs[count:]
+    tile_ref = refs.pop(0) if near else None
+    pair = pl.program_id(0)
+    own = info_ref[0]
+    key, value = key_ref[...], value_ref[...]
+    key_sum = value_sum = None
+    if not first:
+        key_sum, value_sum = refs.pop(0)[...], refs.pop(0)[...]
+    key_out, value_out = refs
+    lane = lanes()
+    keys = [only_head(key, False), only_head(key, True)]
+    values = []
+    for head in range(2):
+        pick = jnp.logical_and(lane // 8 == 2 * pair + head, lane % 8 < 3)
+        values.append(
+            jnp.concatenate([only_head(value, head == 1), jnp.where(pick, 1.0, 0.0).astype(jnp.bfloat16)], axis=1)
+        )
+    for spot in range(count):
+        block, limit = info_ref[1 + 2 * spot], info_ref[2 + 2 * spot]
+        kind = NEAR if near else kind_of(own, block)
+        query, grad, aux = query_refs[spot][...], grad_refs[spot][...], aux_refs[spot][...]
+        wide_query = jnp.concatenate([query, aux], axis=1)
+        wide_grad = jnp.concatenate([grad, aux], axis=1)
+        place = jnp.clip(own - block, -1, 1) + 1
+        dead = jnp.logical_and(lane == DEAD_LANE, dead_rows(own * BLOCK, limit))
+        probs_low, slopes_low = [], []
+        for head in range(2):
+            which = 2 * pair + head
+            pick = jnp.logical_and(lane // 8 == which, jnp.logical_and(lane % 8 >= 3, lane % 8 < 6))
+            side = jnp.where(pick, 1.0, 0.0)
+            if not near:
+                constant = jnp.where(kind == BEFORE, far_ref[which], far_ref[heads + which])
+                side = jnp.where(lane == RIGHT_LANE, constant, side)
+            side = jnp.where(dead, MASKED, side).astype(jnp.bfloat16)
+            scores = contract_last(jnp.concatenate([keys[head], side], axis=1), wide_query)
+            if near:
+                scores = scores + tile_ref[head, place].astype(jnp.float32)
+            probs = jnp.exp(scores)
+            slopes = probs * contract_last(values[head], wide_grad)
+            probs_low.append(probs.astype(jnp.bfloat16))
+            slopes_low.append(slopes.astype(jnp.bfloat16))
+        part_value = jnp.dot(
+            jnp.concatenate(probs_low, axis=1), stack_heads(grad), preferred_element_type=jnp.float32
+        )
+        part_key = jnp.dot(
+            jnp.concatenate(slopes_low, axis=1), stack_heads(query), preferred_element_type=jnp.float32
+        )
+        key_sum = part_key if key_sum is None else key_sum + part_key
+        value_sum = part_value if value_sum is None else value_sum + part_value
+    key_out[...] = key_sum.astype(key_out.dtype)
+    value_out[...] = value_sum.astype(value_out.dtype)
+
+
+def key_call(info, far, joined, queries, grads, turned, state, last):
+    count, near, first = len(queries), turned is not None, state is None
+    inner = joined.shape[1] // 2
+    pairs = inner // PAIR
+    own = view_spec(0, lambda p: p)
+    in_specs = [own, view_spec(0, lambda p: p + pairs)]
+    in_specs += [view_spec(row, lambda p: p) for _, row in queries]
+    in_specs += [view_spec(row, lambda p: p) for _, row in grads]
+    in_specs += [view_spec(row, lambda p: pairs) for _, row in grads]
+    arrays = [array for array, _ in grads]
+    operands = [joined, joined] + [array for array, _ in queries] + arrays + arrays
+    if near:
+        in_specs.append(tile_spec())
+        operands.append(turned)
+    if not first:
+        in_specs += [own, own]
+        operands += list(state)
+    shape = jax.ShapeDtypeStruct((BLOCK, inner), jnp.bfloat16 if last else jnp.float32)
+    kernel = functools.partial(key_kernel, count, near, first, last, 2 * pairs)
+    return run_pairs(
+        kernel, info, far, operands, in_specs, (shape, shape), (own, own), 10 * count, "attention_key_grad"
+    )
+
+
+def grads_kernel(first_ref, second_ref, third_ref, out_ref, aux_ref, grad_ref):
+    total = first_ref[...] + second_ref[...].astype(jnp.float32) + third_ref[...]
+    low = total.astype(jnp.bfloat16)
+    inner = low.shape[1]
+    grad_ref[:, :inner] = low
+    product = low.astype(jnp.float32) * out_ref[...]
+    base = aux_ref[...]
+    for pair in range(inner // PAIR):
+        piece = product[:, pair * PAIR : (pair + 1) * PAIR]
+        for head in range(2):
+            delta = -jnp.sum(only_head(piece, head == 1), axis=1, keepdims=True)
+            base = place_parts(base, delta, 8 * (2 * pair + head))
+    grad_ref[:, inner:] = base.astype(jnp.bfloat16)
+
+
+def finish_grads(first, second, third, out, aux):
+    return pl.pallas_call(
+        grads_kernel,
+        out_shape=jax.ShapeDtypeStruct((BLOCK, out.shape[1] + PAIR), jnp.bfloat16),
+        name="attention_out_grad",
+    )(first, second, third, out, aux)
+
+
+def grouped_body(
+    tokens,
+    lengths,
+    buckets,
+    attention_gain,
+    query_weight,
+    key_weight,
+    value_weight,
+    output_weight,
+    bias_table,
+    feed_gain,
+    gate_weight,
+    up_weight,
+    down_weight,
+    cotangent,
+):
+    bf16, f32 = jnp.bfloat16, jnp.float32
+    places = lax.axis_size("ctx")
+    chips = places // 2
+    rows_of_chips = chips // 2
+    here = lax.axis_index("ctx")
+    side = lax.axis_index("wsh")
+    core = here % 2
+    chip = here // 2
+    lane_y = chip % 2
+    lane_z = chip // 2
+    length = tokens.shape[1]
+    half = tokens.shape[2] // 2
+    heads = bias_table.shape[1]
+    inner = query_weight.shape[1]
+    nowhere = -(1 << 20)
+
+    def spread(block, route):
+        return lax.ppermute(block, AXES, route)
+
+    def route_of(move):
+        pairs = []
+        for c in range(places):
+            for w in range(2):
+                target = move(c // 4, (c // 2) % 2, c % 2, w)
+                if target is not None:
+                    z, y, k, x = target
+                    pairs.append((c * 2 + w, (((z * 2 + y) * 2) + k) * 2 + x))
+        return pairs
+
+    route_core = route_of(lambda z, y, k, x: (z, y, 1 - k, x))
+    route_x = route_of(lambda z, y, k, x: (z, y, k, 1 - x))
+    route_y = route_of(lambda z, y, k, x: (z, 1 - y, k, x))
+    route_far = route_of(lambda z, y, k, x: (z ^ 2, y, k, x))
+    route_near = route_of(lambda z, y, k, x: (z ^ 1, y, k, x))
+    order = [(i, 0) for i in range(rows_of_chips)] + [
+        (rows_of_chips - 1 - i, 1) for i in range(rows_of_chips)
+    ]
+    place = {spot: i for i, spot in enumerate(order)}
+    route_ring = route_of(
+        lambda z, y, k, x: (*order[(place[(z, y)] + 1 - 2 * k) % chips], k, x)
+    )
+    route_next = [
+        ((c * 2 + w), (c + (1 if c % 2 else -1)) * 2 + w)
+        for c in range(places)
+        for w in range(2)
+        if 0 <= c + (1 if c % 2 else -1) < places
+    ]
+    my_place = jnp.where(lane_y == 0, lane_z, 2 * rows_of_chips - 1 - lane_z)
+    toward = jnp.where(core == 0, -1, 1)
+    next_block = here - 1 + 2 * core
+    has_next = jnp.logical_and(next_block >= 0, next_block < places)
+
+    def chip_at(spot):
+        spot = (spot + 2 * chips) % chips
+        return jnp.where(
+            spot < rows_of_chips, 2 * spot, 2 * (2 * rows_of_chips - 1 - spot) + 1
+        )
+
+    def swap_core(block):
+        return spread(block, route_core)
+
+    def swap_x(block):
+        return spread(block, route_x)
+
+    def both_sides(mine, other, axis):
+        return jnp.where(
+            side == 0,
+            jnp.concatenate([mine, other], axis=axis),
+            jnp.concatenate([other, mine], axis=axis),
+        )
+
+    def after(block, *others):
+        return lax.optimization_barrier((block, *others))[0]
+
+    live_count = jnp.minimum(lengths[0, 0], places * length)
+    small = jnp.concatenate(
+        [
+            attention_gain,
+            feed_gain,
+            bias_table.reshape(-1),
+            jnp.stack([live_count // 128, live_count % 128]).astype(bf16),
+        ]
+    )
+    size_small = small.shape[0]
+    small = jnp.pad(small, (0, -size_small % 2048)).reshape(-1, 128)
+    small_other = swap_x(small).reshape(-1)
+    gain_other = small_other[:half]
+    feed_other = small_other[half : 2 * half]
+    table_other = small_other[2 * half : size_small - 2].reshape(bias_table.shape)
+    counts = small_other[size_small - 2 : size_small].astype(f32).astype(jnp.int32)
+    count_other = counts[0] * 128 + counts[1]
+    quarter = half // 2
+
+    def my_rows(block, which, count):
+        return lax.dynamic_slice_in_dim(block, which * count, count, 0)
+
+    projections = [key_weight, value_weight, query_weight]
+    sent_rows = jnp.concatenate([my_rows(w, core, quarter) for w in projections], axis=1)
+    part = swap_x(sent_rows)
+    traded = swap_core(part)
+    other_rows = jnp.where(
+        core == 0,
+        jnp.concatenate([part, traded], axis=0),
+        jnp.concatenate([traded, part], axis=0),
+    )
+    weight_all = both_sides(jnp.concatenate(projections, axis=1), other_rows, 0)
+    gain_one = both_sides(attention_gain, gain_other, 0).astype(f32)
+    gain_two = both_sides(feed_gain, feed_other, 0).astype(f32)
+    table = both_sides(bias_table, table_other, 0)
+
+    mine = tokens[0]
+    cot = cotangent[0]
+    out_rows = inner // 2
+    out_part = swap_x(after(my_rows(output_weight, core, out_rows), part))
+    out_traded = swap_core(out_part)
+    output_full = both_sides(
+        output_weight,
+        jnp.where(
+            core == 0,
+            jnp.concatenate([out_part, out_traded], axis=0),
+            jnp.concatenate([out_traded, out_part], axis=0),
+        ),
+        1,
+    )
+    rows_own = jnp.concatenate([mine, cot], axis=0)
+    rows_side = swap_x(after(rows_own, part))
+    rows_core = swap_core(jnp.concatenate([rows_own, rows_side], axis=0))
+
+    def group_of(which):
+        at = which * length
+        return jnp.concatenate(
+            [
+                rows_own[at : at + length],
+                rows_core[at : at + length],
+                rows_side[at : at + length],
+                rows_core[2 * length + at : 3 * length + at],
+            ],
+            axis=0,
+        )
+
+    positions = here * length + jnp.arange(length, dtype=jnp.int32)
+    pair_positions = (here ^ 1) * length + jnp.arange(length, dtype=jnp.int32)
+    live_group = jnp.concatenate(
+        [
+            (positions < live_count).astype(f32)[:, None],
+            (pair_positions < live_count).astype(f32)[:, None],
+            (positions < count_other).astype(f32)[:, None],
+            (pair_positions < count_other).astype(f32)[:, None],
+        ],
+        axis=0,
+    )
+    live_own = live_group[:length]
+
+    inputs = mine.astype(f32)
+    scale_one = row_scale(inputs)
+    first = (inputs * scale_one * gain_one).astype(bf16)
+    projected = jnp.dot(first, weight_all, preferred_element_type=f32).astype(bf16)
+    joined, query = projected[:, : 2 * inner], projected[:, 2 * inner :]
+
+    bucket_count = table.shape[0]
+    reach = (buckets.shape[0] + 1) // 2
+    offsets = jnp.clip(jnp.arange(SPAN_ROW, dtype=jnp.int32) - 511, 1 - reach, reach - 1) + (reach - 1)
+    spots = jnp.arange(buckets.shape[0], dtype=jnp.int32)
+    chosen = jnp.sum(jnp.where(offsets[:, None] == spots[None, :], buckets[None, :], 0), axis=1)
+    onehot = (chosen[:, None] == jnp.arange(bucket_count, dtype=jnp.int32)[None, :]).astype(f32)
+    offset_rows = lax.dot_general(
+        table.astype(f32), onehot, (((0,), (1,)), ((), ())), precision=HIGH, preferred_element_type=f32
+    )
+    tiles, turned = bias_tiles(offset_rows)
+    far = jnp.concatenate([offset_rows[:, 0], offset_rows[:, SPAN_ROW - 2]])
+
+    middle = chips // 2
+
+    def start_ring(block):
+        return jnp.concatenate([block, swap_core(block)], axis=0)
+
+    def next_chunk(chunk, step):
+        if step == middle:
+            return spread(chunk[:length], route_ring)
+        return spread(chunk, route_ring)
+
+    def views(chunk):
+        return [(chunk, row) for row in range(chunk.shape[0] // length)]
+
+    def blocks_at(step):
+        ahead = chip_at(my_place + toward * step)
+        if step == middle:
+            return [ahead * 2 + core, ahead * 2 + 1 - core]
+        behind = chip_at(my_place - toward * step)
+        return [ahead * 2 + core, ahead * 2 + 1 - core, behind * 2 + 1 - core, behind * 2 + core]
+
+    def info_of(blocks, near):
+        entries = [here]
+        for block in blocks:
+            limit = live_count
+            if near:
+                limit = jnp.where(jnp.logical_or(block != next_block, has_next), limit, nowhere)
+            else:
+                limit = jnp.where(block == next_block, nowhere, limit)
+            entries += [block, limit]
+        return jnp.stack(entries).astype(jnp.int32)
+
+    near_info = info_of([here, here ^ 1, next_block], True)
+    far_info = [info_of(blocks_at(step), False) for step in range(1, middle + 1)]
+
+    chunk = start_ring(joined)
+    next_joined = spread(joined, route_next)
+    near_views = views(chunk) + [(next_joined, 0)]
+    received = next_chunk(chunk, 1)
+    state = forward_call(near_info, far, query, near_views, tiles, None, False)
+    query_first = query_chunk = start_ring(query)
+    query_next = spread(query, route_next)
+    far_views, query_views = [], []
+    for step in range(1, middle + 1):
+        partner = swap_core(received)
+        now = views(received) + views(partner)
+        far_views.append(now)
+        query_received = next_chunk(query_chunk, step)
+        query_partner = swap_core(query_received)
+        query_views.append(views(query_received) + views(query_partner))
+        query_chunk = query_received
+        if step < middle:
+            received = next_chunk(received, step + 1)
+        state = forward_call(far_info[step - 1], far, query, now, None, state, step == middle)
+    attention, attention_low, aux = state
+
+    hidden_units = gate_weight.shape[1] // 2
+    gate_mine = lax.dynamic_slice_in_dim(gate_weight, core * hidden_units, hidden_units, 1)
+    up_mine = lax.dynamic_slice_in_dim(up_weight, core * hidden_units, hidden_units, 1)
+    down_mine = lax.dynamic_slice_in_dim(down_weight, core * hidden_units, hidden_units, 0)
+    outer_low = (group_of(1).astype(f32) * live_group).astype(bf16)
+    mixed_side = swap_x(attention_low)
+    mixed_core = swap_core(jnp.concatenate([attention_low, mixed_side], axis=0))
+    mixed = jnp.concatenate(
+        [attention_low, mixed_core[:length], mixed_side, mixed_core[length:]], axis=0
+    )
+    branch = jnp.dot(mixed, output_full, preferred_element_type=f32)
+    middle_rows = group_of(0).astype(f32) + live_group * branch
+    scale_two = row_scale(middle_rows)
+    unit = middle_rows * scale_two
+    second = (unit * gain_two).astype(bf16)
+    gate = jnp.dot(second, gate_mine, preferred_element_type=f32)
+    up = jnp.dot(second, up_mine, preferred_element_type=f32)
+
+    def gated(gate_in, up_in):
+        return jax.nn.gelu(gate_in, approximate=True) * up_in
+
+    def add_low(left, right):
+        return (left.astype(f32) + right.astype(f32)).astype(bf16)
+
+    def halves(block, bit):
+        size = block.shape[0] // 2
+        return (my_rows(block, bit, size), my_rows(block, 1 - bit, size))
+
+    outer_chips = [0, rows_of_chips - 1]
+    route_inward = route_of(
+        lambda z, y, k, x: ((1 if z == 0 else 2), y, k, x) if z in outer_chips else None
+    )
+    route_across = route_of(lambda z, y, k, x: (3 - z, y, k, x) if z in (1, 2) else None)
+    route_third = route_of(lambda z, y, k, x: (z ^ 1, y, k, x) if z % 2 != k else None)
+    route_fourth = route_of(lambda z, y, k, x: (z, y, 1 - k, x) if z % 2 == k else None)
+    z_low = lane_z % 2
+    upper = lane_z // 2
+
+    def reduce_y(block):
+        kept, sent = halves(block, lane_y)
+        return add_low(kept, spread(sent, route_y))
+
+    def reduce_x(block):
+        grid = block.reshape(2, 2, block.shape[0] // 4, block.shape[1])
+        kept = lax.dynamic_index_in_dim(grid, side, 1, keepdims=False)
+        sent = lax.dynamic_index_in_dim(grid, 1 - side, 1, keepdims=False)
+        got = swap_x(sent)
+        return jnp.where(side == upper, kept, got), jnp.where(side == upper, got, kept)
+
+    def reduce_z(pair):
+        stays, leaves = pair
+        leaves = add_low(leaves, spread(leaves, route_inward))
+        stays = add_low(stays, spread(leaves, route_across))
+        return add_low(stays, spread(stays, route_third))
+
+    def reduce_last(block):
+        kept = lax.dynamic_index_in_dim(block, core, 0, keepdims=False)
+        sent = lax.dynamic_index_in_dim(block, 1 - core, 0, keepdims=False)
+        return jnp.where(z_low == core, kept, spread(sent, route_fourth)).astype(f32)
+
+    hidden_value, gate_pull = jax.vjp(gated, gate, up)
+    hidden = hidden_value.astype(bf16)
+    down_full = jnp.einsum("tf,td->fd", hidden, outer_low, preferred_element_type=f32).astype(bf16)
+    down_y = reduce_y(down_full)
+    outer_next = after(outer_low, down_full)
+    hidden_grad = jnp.einsum("td,fd->tf", outer_next, down_mine, preferred_element_type=f32)
+    gate_back, up_back = gate_pull(hidden_grad)
+    gate_low = gate_back.astype(bf16)
+    up_low = up_back.astype(bf16)
+    gate_full = jnp.einsum("tf,td->fd", gate_low, second, preferred_element_type=f32).astype(bf16)
+    gate_y = reduce_y(gate_full)
+    up_next = after(up_low, gate_full)
+    second_grad = jnp.einsum("tf,df->td", gate_low, gate_mine, preferred_element_type=f32) + jnp.einsum(
+        "tf,df->td", up_next, up_mine, preferred_element_type=f32
+    )
+    feed_gain_part = jnp.sum(second_grad * unit, axis=0)
+    scaled = second_grad * gain_two
+    middle_part = (
+        live_group * scale_two * (scaled - unit * jnp.mean(scaled * unit, axis=-1, keepdims=True))
+    ).astype(bf16)
+    grad_part = jnp.einsum("td,id->ti", middle_part, output_full, preferred_element_type=f32)
+    outer_own = outer_low[:length]
+    grad_own = jnp.einsum("td,id->ti", outer_own, output_full, preferred_element_type=f32)
+
+    def sum_core(block):
+        grid = block.reshape(4, length, block.shape[-1])
+        sent = swap_core(jnp.stack([grid[1], grid[3]]).astype(bf16)).astype(f32)
+        return grid[0] + sent[0], grid[2] + sent[1]
+
+    grad_kept, grad_passed = sum_core(grad_part)
+    grad_got = swap_x(grad_passed.astype(bf16))
+    grads = finish_grads(grad_kept, grad_got, grad_own, attention, aux)
+
+    grad_chunk = start_ring(grads)
+    grad_next = spread(grads, route_next)
+    received = next_chunk(grad_chunk, 1)
+    query_state, diagonals = query_call(near_info, far, query, grads, near_views, tiles, None, False)
+    grad_views = []
+    for step in range(1, middle + 1):
+        received = after(received, query_state)
+        partner = swap_core(received)
+        grad_views.append(views(received) + views(partner))
+        following = next_chunk(received, step + 1) if step < middle else None
+        outs = query_call(
+            far_info[step - 1], far, query, grads, far_views[step - 1], None, query_state, step == middle
+        )
+        query_state = outs[0]
+        received = following
+    query_low, far_sums = outs
+
+    up_full = jnp.einsum(
+        "tf,td->fd", after(up_low, grads), second, preferred_element_type=f32
+    ).astype(bf16)
+    up_y = reduce_y(after(up_full, grad_views[-1][0][0]))
+    down_x = reduce_x(after(down_y, grads))
+    gate_x = reduce_x(after(gate_y, grads))
+    feed_part = jnp.dot(after(hidden, grads), down_mine, preferred_element_type=f32)
+    both_parts = jnp.concatenate([feed_part.astype(bf16), middle_part], axis=1)
+    both_kept, both_passed = sum_core(both_parts)
+    both_sum = both_kept + swap_x(both_passed.astype(bf16)).astype(f32)
+    width = tokens.shape[2]
+    result = (middle_rows[:length] + live_own * both_sum[:, :width]).astype(bf16)
+    middle_grad = outer_own.astype(f32) + both_sum[:, width:]
+    branch_low = (live_own * middle_grad).astype(bf16)
+
+    key_state = key_call(
+        near_info,
+        far,
+        joined,
+        views(query_first) + [(query_next, 0)],
+        views(grad_chunk) + [(grad_next, 0)],
+        turned,
+        None,
+        False,
+    )
+    for step in range(1, middle + 1):
+        key_state = key_call(
+            far_info[step - 1],
+            far,
+            joined,
+            query_views[step - 1],
+            grad_views[step - 1],
+            None,
+            key_state,
+            step == middle,
+        )
+    keys_low, values_low = key_state
+
+    down_out = reduce_last(reduce_z(after(down_x, grad_views[-1][0][0])))
+    gate_out = jnp.transpose(reduce_last(reduce_z(after(gate_x, grad_views[-1][0][0]))))
+    up_out = jnp.transpose(reduce_last(reduce_z(reduce_x(up_y))))
+
+    columns = inner // places
+    target = jnp.arange(inner // 2, dtype=jnp.int32)
+    group_index, inside = target // columns, target % columns
+    y_bit = group_index // rows_of_chips
+    z_index = group_index % rows_of_chips
+
+    def picker(which):
+        source = (((z_index * 2 + y_bit) * 2) + which) * columns + inside
+        return (jnp.arange(inner, dtype=jnp.int32)[:, None] == source[None, :]).astype(bf16)
+
+    pick_kept, pick_sent = picker(core), picker(1 - core)
+
+    def pick(block, chooser):
+        return jnp.dot(block, chooser, preferred_element_type=f32).astype(bf16)
+
+    def lanes_of(block):
+        low_half, high_half = block[:, :half], block[:, half:]
+        return (
+            jnp.where(side == 0, low_half, high_half),
+            jnp.where(side == 0, high_half, low_half),
+        )
+
+    def outer_product(left, right):
+        return jnp.einsum("ti,td->id", left, right, preferred_element_type=f32)
+
+    first_lanes = lanes_of(first)
+    branch_lanes = lanes_of(branch_low)
+    kept_x, kept_y, sent_x, sent_y = [], [], [], []
+    for block, (lane_kept, lane_sent) in (
+        (query_low, first_lanes),
+        (keys_low, first_lanes),
+        (values_low, first_lanes),
+        (attention_low, branch_lanes),
+    ):
+        mine_rows, other_rows_of = pick(block, pick_kept), pick(block, pick_sent)
+        kept_x.append(outer_product(mine_rows, lane_kept))
+        kept_y.append(outer_product(mine_rows, lane_sent))
+        sent_x.append(outer_product(other_rows_of, lane_kept).astype(bf16))
+        sent_y.append(outer_product(other_rows_of, lane_sent).astype(bf16))
+    got = swap_core(jnp.stack(sent_x + sent_y)).astype(f32)
+    passed = (jnp.stack(kept_y) + got[4:]).astype(bf16)
+    total = (jnp.stack(kept_x) + got[:4] + swap_x(passed).astype(f32)).astype(bf16)
+    for bit, route in ((lane_y, route_y), (upper, route_far), (z_low, route_near)):
+        size = total.shape[1] // 2
+        kept = lax.dynamic_slice_in_dim(total, bit * size, size, 1)
+        sent = lax.dynamic_slice_in_dim(total, (1 - bit) * size, size, 1)
+        total = add_low(kept, spread(sent, route))
+    total = total.astype(f32)
+    projection_out = jnp.transpose(total[:3], (0, 2, 1))
+
+    gradients = jnp.concatenate([keys_low, values_low, query_low], axis=1)
+    first_grad = jnp.einsum("ti,di->td", gradients, weight_all, preferred_element_type=f32)
+    unit_one = inputs * scale_one
+    gain_one_part = jnp.sum(first_grad * unit_one, axis=0)
+    scaled_one = first_grad * gain_one
+    input_gradient = (
+        middle_grad
+        + scale_one * (scaled_one - unit_one * jnp.mean(scaled_one * unit_one, axis=-1, keepdims=True))
+    ).astype(bf16)
+
+    lines = diagonals[:, :2].reshape(heads, SPAN_ROW)
+    outside = far_sums[:, 0].reshape(heads // 2, PAIR)[:, :8].reshape(heads, 4)
+    lines = lines.at[:, 0].add(outside[:, BEFORE]).at[:, SPAN_ROW - 2].add(outside[:, AFTER])
+    table_part = lax.dot_general(
+        onehot, lines, (((0,), (1,)), ((), ())), precision=HIGH, preferred_element_type=f32
+    )
+    flat = jnp.concatenate([gain_one_part, feed_gain_part, table_part.reshape(-1)])
+    used = flat.shape[0]
+    flat = jnp.pad(flat, (0, -used % 1024)).reshape(-1, 128)
+    for route in (route_core, route_x, route_y, route_far, route_near):
+        flat = flat + spread(flat, route)
+    flat = flat.reshape(-1)
+    gain_one_sum = flat[:width]
+    feed_gain_sum = flat[width : 2 * width]
+    table_sum = flat[2 * width : used].reshape(bucket_count, heads)
+
+    def my_half(block):
+        size = block.shape[0] // 2
+        return lax.dynamic_slice_in_dim(block, side * size, size, 0)
+
+    return (
+        result[None],
+        input_gradient[None],
+        my_half(gain_one_sum),
+        projection_out[0],
+        projection_out[1],
+        projection_out[2],
+        total[3],
+        my_half(table_sum),
+        my_half(feed_gain_sum),
+        gate_out,
+        up_out,
+        down_out,
+    )
+
+
 def solution(mesh):
     placed = (
         P("wsh", "ctx", None),
@@ -368,8 +1291,9 @@
         P("wsh", None),
         P("wsh", "ctx", None),
     )
+    step = grouped_body if mesh.shape["ctx"] == 16 else body
     return jax.shard_map(
-        body,
+        step,
         mesh=mesh,
         in_specs=placed,
         out_specs=(

time: 2180 us -> 560 us (0.26)
  waiting for transfers between devices: 1010 us -> 129 us
  local copies, waits for them, and re-layouts: 598 us -> 59.5 us
  other arithmetic: 181 us -> 62.9 us
  Pallas kernels: 0 us -> 112 us
  matrix products: 210 us -> 104 us
  blocking collectives: 77.2 us -> 0 us
    reduce_scatter x10 -> x0, waiting for transfers between devices: 852 us -> none  [the longest x1 220 us: body(): lax.psum_scatter(gate_grad, 'ctx', scatter_dimension=1, tiled=True)]
    while x578 -> x0, local copies, waits for them, and re-layouts: 255 us -> none
    reshape x49 -> x9, local copies, waits for them, and re-layouts: 204 us -> 0.6 us  [the longest x2 0.19 us: grouped_body(): table_other = small_other[2 * half:size_small - 2].reshape(bias_table.shape)]
    ppermute x94 -> x71, waiting for transfers between devices: 0.25 us -> 129 us  [spread(): return lax.ppermute(block, AXES, route)]
    pallas_call x0 -> x17, Pallas kernels: none -> 112 us  [the longest x15 105 us: run_pairs(): pl.pallas_call(kernel, grid_spec=pltpu.PrefetchScalarGridSpec(num_scalar_...]
    dot_general x181 -> x40, matrix products: 210 us -> 104 us  [the longest x1 19.6 us: grouped_body(): jnp.einsum('td,fd->tf', outer_next, down_mine, preferred_element_type=f32)]
    all_gather x7 -> x0, waiting for transfers between devices: 103 us -> none  [the longest x1 71 us: body(): lax.all_gather(down_weight, 'wsh', axis=0, tiled=True)]
    slice x48 -> x17, local copies, waits for them, and re-layouts: 102 us -> 12.7 us  [the longest x3 5.06 us: next_chunk(): return spread(chunk[:length], route_ring)]
  transfers between devices with their start and end apart: 116 -> 71, of which waited for: 16 -> 21; matrix products, arithmetic and copies ran while one was open for 43% -> 39% of each run, Pallas kernels for 0% -> 20%
where the time goes in v2:
time: 560 us; the launch traced here: 551 us
  waiting for transfers between devices  129 us (23%)
  Pallas kernels  112 us (20%)
  matrix products  104 us (19%)
  starting transfers between devices  78.6 us (14%)
  other arithmetic  62.9 us (11%)
  local copies, waits for them, and re-layouts  59.5 us (11%)
    ppermute x71, waiting for transfers between devices, spread(): return lax.ppermute(block, AXES, route)  129 us
    pallas_call x15, Pallas kernels, run_pairs(): pl.pallas_call(kernel, grid_spec=pltpu.PrefetchScalarGridSpec(num_scalar_...  105 us
    ppermute x71, starting transfers between devices, spread(): return lax.ppermute(block, AXES, route)  78.6 us
    dot_general x1, matrix products, grouped_body(): jnp.einsum('td,fd->tf', outer_next, down_mine, preferred_element_type=f32)  19.6 us
    dynamic_slice x8, local copies, waits for them, and re-layouts, my_rows(): return lax.dynamic_slice_in_dim(block, which * count, count, 0)  15.7 us
    dot_general x16, matrix products, outer_product(): return jnp.einsum('ti,td->id', left, right, preferred_element_type=f32)  15.6 us
    convert_element_type x14, other arithmetic, add_low(): return (left.astype(f32) + right.astype(f32)).astype(bf16)  14.1 us
    dot_general x8, matrix products, pick(): return jnp.dot(block, chooser, preferred_element_type=f32).astype(bf16)  11.7 us
  transfers between devices with their start and end apart: 71, of which 21 were waited for; matrix products, arithmetic and copies ran while one was open for 39% of the time, Pallas kernels for 20%

profile of v2, /device:TPU:0, one launch (start us, length us, event | category | flops | bytes accessed | tf_op | source)
XLA Modules:
  0.0 550.6 jit_solution(14529049258646027636)
XLA Ops:
  4.0 2.9 collective-permute-start
  12.3 13.9 %collective-permute-done = bf16[368,1152]{1,0:T(8,128)(2,1)} collective-permute-done((bf16[368,1152]{1,0:T(8,128)(2,1)}, bf16[368,1152]{1,0:T(8,128)(2,1)}, u32[]{:S(2)}, u32[]{:S(2)}) %collective-permute-start) | collective-permute-done | bytes 847904 | tf_op jit(solution)/shard_map/ppermute | solution.py:820
  31.2 3.8 convolution_convert_fusion.4
  53.7 3.5 collective-permute-done.6.refs_1_.refs_2_.refs_5_.refs_6_.refs_3_.refs_4_.refs_7_.refs_8_
  59.1 3.2 collective-permute-done.1
  72.3 6.1 %collective-permute-done.17 = bf16[192,736]{0,1:T(8,128)(2,1)} collective-permute-done((bf16[192,736]{0,1:T(8,128)(2,1)S(1)}, bf16[192,736]{0,1:T(8,128)(2,1)}, u32[]{:S(2)}, u32[]{:S(2)}) %collective-permute-start.17) | collective-permute-done | bytes 282656 | tf_op jit(solution)/shard_map/ppermute | solution.py:820
  80.5 4.5 bias_tiles.1
  85.1 3.9 collective-permute-start.26
  89.6 2.7 maximum_select_fusion.5
  92.8 6.5 %attention_forward.5 = (f32[256,384]{1,0:T(8,128)}, f32[256,768]{1,0:T(8,128)}) custom-call(s32[7]{0:T(128)} %stack.236.info_ref, f32[12]{0:T(128)} %pad_maximum_fusion.11.far_ref, bf16[256,384]{1,0:T(8,128)(2,1)} %slice.290.refs_0_, bf16[512,768]{1,0:T(8,128)(2,1)} %pad_maximum_fusion.6.refs_1_.refs_2_.refs_4_.refs_5_.refs_3_.refs_6_.refs_7_, ...), custom_call_target="tpu_custom_call" | custom-call | flops 1811939328 | bytes 3538944 | tf_op jit(solution)/shard_map/attention_forward/pallas_call | solution.py:462
  107.5 7.5 %attention_forward.6 = (f32[256,384]{1,0:T(8,128)}, f32[256,768]{1,0:T(8,128)}) custom-call(s32[9]{0:T(128)} %stack.230.info_ref, f32[12]{0:T(128)} %pad_maximum_fusion.11.far_ref, bf16[256,384]{1,0:T(8,128)(2,1)} %slice.290.refs_0_, bf16[512,768]{1,0:T(8,128)(2,1)} %collective-permute-done.6.refs_1_.refs_2_.refs_5_.refs_6_.refs_3_.refs_4_.refs_7_.refs_8_, ...), custom_call_target="tpu_custom_call" | custom-call | flops 2415919104 | bytes 4718592 | tf_op jit(solution)/shard_map/attention_forward/pallas_call | solution.py:462
  116.5 7.5 %attention_forward.7 = (f32[256,384]{1,0:T(8,128)}, f32[256,768]{1,0:T(8,128)}) custom-call(s32[9]{0:T(128)} %stack.221.info_ref, f32[12]{0:T(128)} %pad_maximum_fusion.11.far_ref, bf16[256,384]{1,0:T(8,128)(2,1)} %slice.290.refs_0_, bf16[512,768]{1,0:T(8,128)(2,1)} %collective-permute-done.7.refs_1_.refs_2_.refs_5_.refs_6_.refs_3_.refs_4_.refs_7_.refs_8_, ...), custom_call_target="tpu_custom_call" | custom-call | flops 2415919104 | bytes 4718592 | tf_op jit(solution)/shard_map/attention_forward/pallas_call | solution.py:462
  124.0 7.5 %attention_forward.8 = (f32[256,384]{1,0:T(8,128)}, f32[256,768]{1,0:T(8,128)}) custom-call(s32[9]{0:T(128)} %stack.212.info_ref, f32[12]{0:T(128)} %pad_maximum_fusion.11.far_ref, bf16[256,384]{1,0:T(8,128)(2,1)} %slice.290.refs_0_, bf16[512,768]{1,0:T(8,128)(2,1)} %collective-permute-done.8.refs_1_.refs_2_.refs_5_.refs_6_.refs_3_.refs_4_.refs_7_.refs_8_, ...), custom_call_target="tpu_custom_call" | custom-call | flops 2415919104 | bytes 4718592 | tf_op jit(solution)/shard_map/attention_forward/pallas_call | solution.py:462
  132.3 6.2 %attention_forward.9 = (f32[256,384]{1,0:T(8,128)}, bf16[256,384]{1,0:T(8,128)(2,1)}, f32[256,128]{1,0:T(8,128)}) custom-call(s32[5]{0:T(128)} %stack.203.info_ref, f32[12]{0:T(128)} %pad_maximum_fusion.11.far_ref, bf16[256,384]{1,0:T(8,128)(2,1)} %slice.290.refs_0_, bf16[256,768]{1,0:T(8,128)(2,1)} %collective-permute-done.9.refs_1_.refs_3_.refs_5_, ...), custom_call_target="tpu_custom_call" | custom-call | flops 1207959552 | bytes 2359296 | tf_op jit(solution)/shard_map/attention_forward/pallas_call | solution.py:462
  150.6 3.5 fusion.25
  155.7 6.1 %multiply_convert_fusion.4 = (bf16[1024,896]{1,0:T(8,128)(2,1)S(1)}, f32[1024,896]{1,0:T(8,128)}) fusion(f32[1024,896]{1,0:T(8,128)S(1)} %fusion.25, bf16[1024,1472]{0,1:T(8,128)(2,1)S(1)} %multiply_convert_fusion.2, bf16[1472,1792]{1,0:T(8,128)(2,1)S(1)} %bitcast.260, s32[]{:T(128)S(6)} %select_n.448), kind=kOutput, calls=%fused_computation.27 | convolution fusion | flops 2710306816 | bytes 14827524 | tf_op jit(solution)/shard_map/dot_general | solution.py:1045
  161.8 3.5 convolution_convert_fusion.2
  165.3 19.6 %multiply_convert_fusion.3 = (bf16[1024,896]{1,0:T(8,128)(2,1)}, bf16[1024,896]{1,0:T(8,128)(2,1)S(1)}) fusion(f32[1024,896]{1,0:T(8,128)S(1)} %fusion.25, f32[1024,896]{1,0:T(8,128)} %get-tuple-element.217, bf16[1024,1472]{0,1:T(8,128)(2,1)S(1)} %multiply_convert_fusion.1, bf16[1792,1472]{0,1:T(8,128)(2,1)S(1)} %bitcast.270, s32[]{:T(128)S(6)} %select_n.448), kind=kOutput, calls=%fused_computation.26 | convolution fusion | flops 2723151872 | bytes 16662532 | tf_op jit(solution)/shard_map/td,fd->tf/dot_general | solution.py:1094
  186.1 4.6 convolution_convert_fusion.1
  190.7 5.0 fusion.23
  195.7 6.5 %multiply_reduce_fusion = (f32[1472]{0:T(1024)}, f32[1024]{0:T(1024)S(1)}, f32[1024,1472]{0,1:T(8,128)S(1)}) fusion(f32[1024,1472]{0,1:T(8,128)S(1)} %get-tuple-element.215, f32[1024]{0:T(1024)S(1)} %get-tuple-element.209, f32[1472]{0:T(1024)S(1)} %fusion.105, f32[1024,1472]{0,1:T(8,128)S(1)} %fusion.23, bf16[1024,896]{1,0:T(8,128)(2,1)S(1)} %copy-done.27, ...), kind=kOutput, calls=%fused_computation.6 | convolution fusion | flops 2711680512 | bytes 22580740 | tf_op jit(solution)/shard_map/tf,df->td/dot_general | solution.py:1101
  203.9 3.0 fusion.134
  211.2 2.6 copy.73
  222.0 2.6 copy.69
  226.1 2.4 attention_out_grad.1.refs_1_.refs_2_
  229.9 11.4 %attention_query_grad.5 = (f32[256,768]{1,0:T(8,128)}, f32[3,8,1024]{2,1,0:T(8,128)}) custom-call(s32[7]{0:T(128)} %stack.236.info_ref, f32[12]{0:T(128)} %pad_maximum_fusion.11.far_ref, bf16[256,384]{1,0:T(8,128)(2,1)} %slice.290.refs_0_, bf16[256,512]{1,0:T(8,128)(2,1)} %attention_out_grad.1.refs_1_.refs_2_, ...), custom_call_target="tpu_custom_call" | custom-call | flops 2415919104 | bytes 4718592 | tf_op jit(solution)/shard_map/attention_query_grad/pallas_call | solution.py:462
  241.3 6.4 %attention_query_grad.6.refs_11_ = f32[256,768]{1,0:T(8,128)} custom-call(s32[9]{0:T(128)} %stack.230.info_ref, f32[12]{0:T(128)} %pad_maximum_fusion.11.far_ref, bf16[256,384]{1,0:T(8,128)(2,1)} %slice.290.refs_0_, bf16[256,512]{1,0:T(8,128)(2,1)} %attention_out_grad.1.refs_1_.refs_2_, bf16[256,512]{1,0:T(8,128)(2,1)} %attention_out_grad.1.refs_1_.refs_2_, ...), custom_call_target="tpu_custom_call" | custom-call | flops 3221225472 | bytes 6291456 | tf_op jit(solution)/shard_map/attention_query_grad/pallas_call | solution.py:462
  247.8 6.5 %attention_query_grad.7.refs_11_ = f32[256,768]{1,0:T(8,128)} custom-call(s32[9]{0:T(128)} %stack.221.info_ref, f32[12]{0:T(128)} %pad_maximum_fusion.11.far_ref, bf16[256,384]{1,0:T(8,128)(2,1)} %slice.290.refs_0_, bf16[256,512]{1,0:T(8,128)(2,1)} %attention_out_grad.1.refs_1_.refs_2_, bf16[256,512]{1,0:T(8,128)(2,1)} %attention_out_grad.1.refs_1_.refs_2_, ...), custom_call_target="tpu_custom_call" | custom-call | flops 3221225472 | bytes 6291456 | tf_op jit(solution)/shard_map/attention_query_grad/pallas_call | solution.py:462
  254.3 6.4 %attention_query_grad.8.refs_7_ = f32[256,768]{1,0:T(8,128)} custom-call(s32[9]{0:T(128)} %stack.212.info_ref, f32[12]{0:T(128)} %pad_maximum_fusion.11.far_ref, bf16[256,384]{1,0:T(8,128)(2,1)} %slice.290.refs_0_, bf16[256,512]{1,0:T(8,128)(2,1)} %attention_out_grad.1.refs_1_.refs_2_, bf16[256,512]{1,0:T(8,128)(2,1)} %attention_out_grad.1.refs_1_.refs_2_, ...), custom_call_target="tpu_custom_call" | custom-call | flops 3221225472 | bytes 6291456 | tf_op jit(solution)/shard_map/attention_query_grad/pallas_call | solution.py:462
  260.7 5.2 attention_query_grad.9
  269.0 5.6 %convolution_convert_fusion = bf16[1024,1472]{0,1:T(8,128)(2,1)S(1)} fusion(bf16[1024,896]{1,0:T(8,128)(2,1)} %copy-done.67, bf16[1792,1472]{0,1:T(8,128)(2,1)} %param.30, s32[]{:T(128)S(6)} %select_n.448), kind=kOutput, calls=%fused_computation.18 | convolution fusion | flops 2702639104 | bytes 7487492 | tf_op jit(solution)/shard_map/dot_general | solution.py:1145
  274.6 2.4 fusion.43
  281.6 3.9 pad_maximum_fusion.2
  286.6 4.6 convolution_convert_fusion.3
  297.5 4.1 collective-permute-start.30
  301.6 6.5 %attention_key_grad.5 = (f32[256,384]{1,0:T(8,128)}, f32[256,384]{1,0:T(8,128)}) custom-call(s32[7]{0:T(128)} %stack.236.info_ref, f32[12]{0:T(128)} %pad_maximum_fusion.11.far_ref, bf16[256,768]{1,0:T(8,128)(2,1)} %copy-done.30, bf16[256,768]{1,0:T(8,128)(2,1)} %copy-done.30, bf16[512,384]{1,0:T(8,128)(2,1)} %copy-done.43, bf16[512,384]{1,0:T(8,128)(2,1)} %copy-done.43, ...), custom_call_target="tpu_custom_call" | custom-call | flops 3019898880 | bytes 5898240 | tf_op jit(solution)/shard_map/attention_key_grad/pallas_call | solution.py:462
  308.1 2.6 copy.74
  310.7 4.1 add_convert_fusion
  314.7 2.6 copy.75
  320.4 2.6 copy.70
  324.9 4.1 add_convert_fusion.1
  329.0 2.5 copy.71
  336.4 7.0 %attention_key_grad.6 = (f32[256,384]{1,0:T(8,128)}, f32[256,384]{1,0:T(8,128)}) custom-call(s32[9]{0:T(128)} %stack.230.info_ref, f32[12]{0:T(128)} %pad_maximum_fusion.11.far_ref, bf16[256,768]{1,0:T(8,128)(2,1)} %copy-done.30, bf16[256,768]{1,0:T(8,128)(2,1)} %copy-done.30, bf16[512,384]{1,0:T(8,128)(2,1)} %collective-permute-done.24.refs_2_.refs_3_, ...), custom_call_target="tpu_custom_call" | custom-call | flops 4026531840 | bytes 7864320 | tf_op jit(solution)/shard_map/attention_key_grad/pallas_call | solution.py:462
  343.5 2.6 bitcast_select_fusion
  346.5 6.2 %collective-permute-done.54 = bf16[2,112,1472]{2,1,0:T(8,128)(2,1)} collective-permute-done((bf16[2,112,1472]{2,1,0:T(8,128)(2,1)}, bf16[2,112,1472]{2,1,0:T(8,128)(2,1)}, u32[]{:S(2)}, u32[]{:S(2)}) %collective-permute-start.54) | collective-permute-done | bytes 659488 | tf_op jit(solution)/shard_map/ppermute | solution.py:820
  358.0 7.1 %attention_key_grad.7 = (f32[256,384]{1,0:T(8,128)}, f32[256,384]{1,0:T(8,128)}) custom-call(s32[9]{0:T(128)} %stack.221.info_ref, f32[12]{0:T(128)} %pad_maximum_fusion.11.far_ref, bf16[256,768]{1,0:T(8,128)(2,1)} %copy-done.30, bf16[256,768]{1,0:T(8,128)(2,1)} %copy-done.30, bf16[512,384]{1,0:T(8,128)(2,1)} %collective-permute-done.25.refs_2_.refs_3_, ...), custom_call_target="tpu_custom_call" | custom-call | flops 4026531840 | bytes 7864320 | tf_op jit(solution)/shard_map/attention_key_grad/pallas_call | solution.py:462
  365.4 2.5 constant_dynamic-slice_fusion.1
  367.9 4.0 collective-permute-start.67
  372.5 7.3 %attention_key_grad.8 = (f32[256,384]{1,0:T(8,128)}, f32[256,384]{1,0:T(8,128)}) custom-call(s32[9]{0:T(128)} %stack.212.info_ref, f32[12]{0:T(128)} %pad_maximum_fusion.11.far_ref, bf16[256,768]{1,0:T(8,128)(2,1)} %copy-done.30, bf16[256,768]{1,0:T(8,128)(2,1)} %copy-done.30, bf16[512,384]{1,0:T(8,128)(2,1)} %collective-permute-done.26.refs_2_.refs_3_, ...), custom_call_target="tpu_custom_call" | custom-call | flops 4026531840 | bytes 7864320 | tf_op jit(solution)/shard_map/attention_key_grad/pallas_call | solution.py:462
  381.9 5.6 %attention_key_grad.9 = (bf16[256,384]{1,0:T(8,128)(2,1)}, bf16[256,384]{1,0:T(8,128)(2,1)}) custom-call(s32[5]{0:T(128)} %stack.203.info_ref, f32[12]{0:T(128)} %pad_maximum_fusion.11.far_ref, bf16[256,768]{1,0:T(8,128)(2,1)} %copy-done.30, bf16[256,768]{1,0:T(8,128)(2,1)} %copy-done.30, bf16[256,384]{1,0:T(8,128)(2,1)} %collective-permute-done.27.refs_2_, ...), custom_call_target="tpu_custom_call" | custom-call | flops 2013265920 | bytes 3932160 | tf_op jit(solution)/shard_map/attention_key_grad/pallas_call | solution.py:462
  389.4 6.0 %fusion.37 = (f32[1472]{0:T(1024)S(1)}, f32[256]{0:T(256)S(1)}, f32[256,1472]{0,1:T(8,128)}) fusion(f32[256]{0:T(256)S(1)} %copy-done.53, bf16[1,256,1472]{1,2,0:T(8,128)(2,1)} %param.18, f32[1472]{0:T(1024)S(1)} %copy-done.49, bf16[736,1152]{1,0:T(8,128)(2,1)} %copy-done.29, bf16[736,1152]{1,0:T(8,128)(2,1)} %constant_dynamic-update-slice_fusion, ...), kind=kOutput, calls=%fused_computation.75 | convolution fusion | flops 887888192 | bytes 6256129 | tf_op jit(solution)/shard_map/ti,di->td/dot_general | solution.py:1232
  411.5 3.5 collective-permute-done.46
  416.1 2.6 collective-permute-done.47
  423.3 2.4 convert_element_type.389
  433.7 28.6 %collective-permute-done.22 = bf16[256,2944]{0,1:T(8,128)(2,1)S(1)} collective-permute-done((bf16[256,2944]{0,1:T(8,128)(2,1)S(1)}, bf16[256,2944]{0,1:T(8,128)(2,1)S(1)}, u32[]{:S(2)}, u32[]{:S(2)}) %collective-permute-start.22) | collective-permute-done | bytes 1507360 | tf_op jit(solution)/shard_map/ppermute | solution.py:820
  463.0 3.5 multiply_convert_fusion.5
  469.8 5.7 %collective-permute-start.70 = (bf16[112,1472]{1,0:T(8,128)(2,1)S(1)}, bf16[112,1472]{1,0:T(8,128)(2,1)S(1)}, u32[]{:S(2)}, u32[]{:S(2)}) collective-permute-start(bf16[112,1472]{1,0:T(8,128)(2,1)S(1)} %dynamic-slice_bitcast_fusion.3), channel_id=1, source_target_pairs={{0,2},{1,3},{4,6},{5,7},{10,8},{11,9},{14,12},{15,13},{16,18},{17,... | collective-permute-start | bytes 989192 | tf_op jit(solution)/shard_map/ppermute | solution.py:820
  476.9 4.2 collective-permute-done.57
  481.3 4.2 collective-permute-start.58
  488.6 4.2 collective-permute-done.61
  494.8 20.1 %collective-permute-done.49 = bf16[4,192,736]{2,1,0:T(8,128)(2,1)S(1)} collective-permute-done((bf16[4,192,736]{2,1,0:T(8,128)(2,1)S(1)}, bf16[4,192,736]{2,1,0:T(8,128)(2,1)S(1)}, u32[]{:S(2)}, u32[]{:S(2)}) %collective-permute-start.49) | collective-permute-done | bytes 1130528 | tf_op jit(solution)/shard_map/ppermute | solution.py:820
  519.0 10.2 %collective-permute-done.50 = bf16[4,96,736]{2,1,0:T(8,128)(2,1)S(1)} collective-permute-done((bf16[4,96,736]{2,1,0:T(8,128)(2,1)S(1)}, bf16[4,96,736]{2,1,0:T(8,128)(2,1)S(1)}, u32[]{:S(2)}, u32[]{:S(2)}) %collective-permute-start.50) | collective-permute-done | bytes 565280 | tf_op jit(solution)/shard_map/ppermute | solution.py:820
  531.1 12.3 %collective-permute-done.51 = bf16[4,48,736]{2,1,0:T(8,128)(2,1)S(1)} collective-permute-done((bf16[4,48,736]{2,1,0:T(8,128)(2,1)S(1)}, bf16[4,48,736]{2,1,0:T(8,128)(2,1)S(1)}, u32[]{:S(2)}, u32[]{:S(2)}) %collective-permute-start.51) | collective-permute-done | bytes 282656 | tf_op jit(solution)/shard_map/ppermute | solution.py:820
  544.6 4.2 collective-permute-done.52
  (431 shorter events, 171.1 us)
Async XLA Ops:
  4.0 22.2 %collective-permute-start = (bf16[368,1152]{1,0:T(8,128)(2,1)}, bf16[368,1152]{1,0:T(8,128)(2,1)}, u32[]{:S(2)}, u32[]{:S(2)}) collective-permute-start(bf16[368,1152]{1,0:T(8,128)(2,1)} %pad_maximum_fusion.5), channel_id=1, source_target_pairs={{0,1},{1,0},{2,3},{3,2},{4,5},{5,4},{6,7},{7,6},{8,9},{9,8},{10,11... | collective-permute-start | bytes 2543624 | tf_op jit(solution)/shard_map/ppermute | solution.py:820
  8.0 18.2 %collective-permute-start.3 = (bf16[16,128]{1,0:T(8,128)(2,1)S(1)}, bf16[16,128]{1,0:T(8,128)(2,1)S(1)}, u32[]{:S(2)}, u32[]{:S(2)}) collective-permute-start(bf16[16,128]{1,0:T(8,128)(2,1)S(1)} %pad_bitcast_fusion.1), channel_id=1, source_target_pairs={{0,1},{1,0},{2,3},{3,2},{4,5},{5,4},{6,7},{7,6},{8,9},{9,8},{10,11... | collective-permute-start | bytes 12296 | tf_op jit(solution)/shard_map/ppermute | solution.py:820
  26.6 35.7 %collective-permute-start.1 = (bf16[512,1472]{0,1:T(8,128)(2,1)}, bf16[512,1472]{0,1:T(8,128)(2,1)S(1)}, u32[]{:S(2)}, u32[]{:S(2)}) collective-permute-start(bf16[512,1472]{0,1:T(8,128)(2,1)} %pad_maximum_fusion.4), channel_id=1, source_target_pairs={{0,1},{1,0},{2,3},{3,2},{4,5},{5,4},{6,7},{7,6},{8,9},{9,8},{10,11... | collective-permute-start | bytes 4521992 | tf_op jit(solution)/shard_map/ppermute | solution.py:820
  35.9 7.2 %collective-permute-start.5 = (bf16[256,768]{1,0:T(8,128)(2,1)S(1)}, bf16[256,768]{1,0:T(8,128)(2,1)}, u32[]{:S(2)}, u32[]{:S(2)}) collective-permute-start(bf16[256,768]{1,0:T(8,128)(2,1)S(1)} %slice.291.refs_0_.refs_1_), channel_id=1, source_target_pairs={{0,2},{1,3},{2,0},{3,1},{4,6},{5,7},{6,4},{7,5},{8,10},{9,11},{10,... | collective-permute-start | bytes 1179656 | tf_op jit(solution)/shard_map/ppermute | solution.py:820
  45.0 12.3 %collective-permute-start.6 = (bf16[512,768]{1,0:T(8,128)(2,1)}, bf16[512,768]{1,0:T(8,128)(2,1)}, u32[]{:S(2)}, u32[]{:S(2)}) collective-permute-start(bf16[512,768]{1,0:T(8,128)(2,1)} %pad_maximum_fusion.6.refs_1_.refs_2_.refs_4_.refs_5_.refs_3_.refs_6_.refs_7_), channel_id=1, source_target_pairs={{0,8},{1,9},{2,6},{3,7},{4,0},{5,1},{6,14},{7,15},{8,16},{9,17},{1... | collective-permute-start | bytes 2359304 | tf_op jit(solution)/shard_map/ppermute | solution.py:820
  52.1 16.8 %collective-permute-start.24 = (bf16[512,384]{1,0:T(8,128)(2,1)S(1)}, bf16[512,384]{1,0:T(8,128)(2,1)}, u32[]{:S(2)}, u32[]{:S(2)}) collective-permute-start(bf16[512,384]{1,0:T(8,128)(2,1)S(1)} %pad_maximum_fusion.10.refs_2_.refs_3_), channel_id=1, source_target_pairs={{0,8},{1,9},{2,6},{3,7},{4,0},{5,1},{6,14},{7,15},{8,16},{9,17},{1... | collective-permute-start | bytes 1179656 | tf_op jit(solution)/shard_map/ppermute | solution.py:820
  57.3 13.3 %collective-permute-start.7 = (bf16[512,768]{1,0:T(8,128)(2,1)}, bf16[512,768]{1,0:T(8,128)(2,1)}, u32[]{:S(2)}, u32[]{:S(2)}) collective-permute-start(bf16[512,768]{1,0:T(8,128)(2,1)} %collective-permute-done.6.refs_1_.refs_2_.refs_5_.refs_6_.refs_3_.refs_4_.refs_7_.refs_8_), channel_id=1, source_target_pairs={{0,8},{1,9},{2,6},{3,7},{4,0},{5,1},{6,14},{7,15},{8,16},{9,17},{1... | collective-permute-start | bytes 2359304 | tf_op jit(solution)/shard_map/ppermute | solution.py:820
  64.4 79.3 %collective-permute-start.2 = (bf16[1024,1472]{0,1:T(8,128)(2,1)}, bf16[1024,1472]{0,1:T(8,128)(2,1)}, u32[]{:S(2)}, u32[]{:S(2)}) collective-permute-start(bf16[1024,1472]{0,1:T(8,128)(2,1)} %fusion.9), channel_id=1, source_target_pairs={{0,2},{1,3},{2,0},{3,1},{4,6},{5,7},{6,4},{7,5},{8,10},{9,11},{10,... | collective-permute-start | bytes 9043976 | tf_op jit(solution)/shard_map/ppermute | solution.py:820
  67.2 11.3 %collective-permute-start.17 = (bf16[192,736]{0,1:T(8,128)(2,1)S(1)}, bf16[192,736]{0,1:T(8,128)(2,1)}, u32[]{:S(2)}, u32[]{:S(2)}) collective-permute-start(bf16[192,736]{0,1:T(8,128)(2,1)S(1)} %copy-done.44), channel_id=1, source_target_pairs={{0,1},{1,0},{2,3},{3,2},{4,5},{5,4},{6,7},{7,6},{8,9},{9,8},{10,11... | collective-permute-start | bytes 847880 | tf_op jit(solution)/shard_map/ppermute | solution.py:820
  68.9 16.1 %collective-permute-start.25 = (bf16[512,384]{1,0:T(8,128)(2,1)}, bf16[512,384]{1,0:T(8,128)(2,1)}, u32[]{:S(2)}, u32[]{:S(2)}) collective-permute-start(bf16[512,384]{1,0:T(8,128)(2,1)} %collective-permute-done.24.refs_2_.refs_3_), channel_id=1, source_target_pairs={{0,8},{1,9},{2,6},{3,7},{4,0},{5,1},{6,14},{7,15},{8,16},{9,17},{1... | collective-permute-start | bytes 1179656 | tf_op jit(solution)/shard_map/ppermute | solution.py:820
  70.6 28.7 %collective-permute-start.8 = (bf16[512,768]{1,0:T(8,128)(2,1)}, bf16[512,768]{1,0:T(8,128)(2,1)}, u32[]{:S(2)}, u32[]{:S(2)}) collective-permute-start(bf16[512,768]{1,0:T(8,128)(2,1)} %collective-permute-done.7.refs_1_.refs_2_.refs_5_.refs_6_.refs_3_.refs_4_.refs_7_.refs_8_), channel_id=1, source_target_pairs={{0,8},{1,9},{2,6},{3,7},{4,0},{5,1},{6,14},{7,15},{8,16},{9,17},{1... | collective-permute-start | bytes 2359304 | tf_op jit(solution)/shard_map/ppermute | solution.py:820
  78.5 11.1 %collective-permute-start.18 = (bf16[192,736]{0,1:T(8,128)(2,1)}, bf16[192,736]{0,1:T(8,128)(2,1)}, u32[]{:S(2)}, u32[]{:S(2)}) collective-permute-start(bf16[192,736]{0,1:T(8,128)(2,1)} %collective-permute-done.17), channel_id=1, source_target_pairs={{0,2},{1,3},{2,0},{3,1},{4,6},{5,7},{6,4},{7,5},{8,10},{9,11},{10,... | collective-permute-start | bytes 847880 | tf_op jit(solution)/shard_map/ppermute | solution.py:820
  78.5 13.8 %collective-permute-start.14 = (bf16[256,768]{1,0:T(8,128)(2,1)}, bf16[256,768]{1,0:T(8,128)(2,1)}, u32[]{:S(2)}, u32[]{:S(2)}) collective-permute-start(bf16[256,768]{1,0:T(8,128)(2,1)} %copy-done.30), channel_id=1, source_target_pairs={{2,4},{3,5},{4,2},{5,3},{6,8},{7,9},{8,6},{9,7},{10,12},{11,13},{1... | collective-permute-start | bytes 1179656 | tf_op jit(solution)/shard_map/ppermute | solution.py:820
  85.1 17.9 %collective-permute-start.26 = (bf16[512,384]{1,0:T(8,128)(2,1)}, bf16[512,384]{1,0:T(8,128)(2,1)}, u32[]{:S(2)}, u32[]{:S(2)}) collective-permute-start(bf16[512,384]{1,0:T(8,128)(2,1)} %collective-permute-done.25.refs_2_.refs_3_), channel_id=1, source_target_pairs={{0,8},{1,9},{2,6},{3,7},{4,0},{5,1},{6,14},{7,15},{8,16},{9,17},{1... | collective-permute-start | bytes 1179656 | tf_op jit(solution)/shard_map/ppermute | solution.py:820
  89.6 16.4 %collective-permute-start.13 = (bf16[512,768]{1,0:T(8,128)(2,1)}, bf16[512,768]{1,0:T(8,128)(2,1)}, u32[]{:S(2)}, u32[]{:S(2)}) collective-permute-start(bf16[512,768]{1,0:T(8,128)(2,1)} %collective-permute-done.6.refs_1_.refs_2_.refs_5_.refs_6_.refs_3_.refs_4_.refs_7_.refs_8_), channel_id=1, source_target_pairs={{0,2},{1,3},{2,0},{3,1},{4,6},{5,7},{6,4},{7,5},{8,10},{9,11},{10,... | collective-permute-start | bytes 2359304 | tf_op jit(solution)/shard_map/ppermute | solution.py:820
  92.3 24.2 %collective-permute-start.12 = (bf16[512,768]{1,0:T(8,128)(2,1)}, bf16[512,768]{1,0:T(8,128)(2,1)}, u32[]{:S(2)}, u32[]{:S(2)}) collective-permute-start(bf16[512,768]{1,0:T(8,128)(2,1)} %collective-permute-done.7.refs_1_.refs_2_.refs_5_.refs_6_.refs_3_.refs_4_.refs_7_.refs_8_), channel_id=1, source_target_pairs={{0,2},{1,3},{2,0},{3,1},{4,6},{5,7},{6,4},{7,5},{8,10},{9,11},{10,... | collective-permute-start | bytes 2359304 | tf_op jit(solution)/shard_map/ppermute | solution.py:820
  101.0 14.0 %collective-permute-start.9 = (bf16[256,768]{1,0:T(8,128)(2,1)}, bf16[256,768]{1,0:T(8,128)(2,1)}, u32[]{:S(2)}, u32[]{:S(2)}) collective-permute-start(bf16[256,768]{1,0:T(8,128)(2,1)} %slice.292), channel_id=1, source_target_pairs={{0,8},{1,9},{2,6},{3,7},{4,0},{5,1},{6,14},{7,15},{8,16},{9,17},{1... | collective-permute-start | bytes 1179656 | tf_op jit(solution)/shard_map/ppermute | solution.py:820
  102.9 21.1 %collective-permute-start.11 = (bf16[512,768]{1,0:T(8,128)(2,1)}, bf16[512,768]{1,0:T(8,128)(2,1)}, u32[]{:S(2)}, u32[]{:S(2)}) collective-permute-start(bf16[512,768]{1,0:T(8,128)(2,1)} %collective-permute-done.8.refs_1_.refs_2_.refs_5_.refs_6_.refs_3_.refs_4_.refs_7_.refs_8_), channel_id=1, source_target_pairs={{0,2},{1,3},{2,0},{3,1},{4,6},{5,7},{6,4},{7,5},{8,10},{9,11},{10,... | collective-permute-start | bytes 2359304 | tf_op jit(solution)/shard_map/ppermute | solution.py:820
  106.0 191.5 %collective-permute-start.41 = (bf16[256,384]{1,0:T(8,128)(2,1)}, bf16[256,384]{1,0:T(8,128)(2,1)}, u32[]{:S(2)}, u32[]{:S(2)}) collective-permute-start(bf16[256,384]{1,0:T(8,128)(2,1)} %slice.290.refs_0_), channel_id=1, source_target_pairs={{2,4},{3,5},{4,2},{5,3},{6,8},{7,9},{8,6},{9,7},{10,12},{11,13},{1... | collective-permute-start | bytes 589832 | tf_op jit(solution)/shard_map/ppermute | solution.py:820
  115.0 16.5 %collective-permute-start.10 = (bf16[256,768]{1,0:T(8,128)(2,1)}, bf16[256,768]{1,0:T(8,128)(2,1)S(1)}, u32[]{:S(2)}, u32[]{:S(2)}) collective-permute-start(bf16[256,768]{1,0:T(8,128)(2,1)} %collective-permute-done.9.refs_1_.refs_3_.refs_5_), channel_id=1, source_target_pairs={{0,2},{1,3},{2,0},{3,1},{4,6},{5,7},{6,4},{7,5},{8,10},{9,11},{10,... | collective-permute-start | bytes 1179656 | tf_op jit(solution)/shard_map/ppermute | solution.py:820
  138.5 7.4 %collective-permute-start.15 = (bf16[256,384]{1,0:T(8,128)(2,1)}, bf16[256,384]{1,0:T(8,128)(2,1)S(1)}, u32[]{:S(2)}, u32[]{:S(2)}) collective-permute-start(bf16[256,384]{1,0:T(8,128)(2,1)} %get-tuple-element.90), channel_id=1, source_target_pairs={{0,1},{1,0},{2,3},{3,2},{4,5},{5,4},{6,7},{7,6},{8,9},{9,8},{10,11... | collective-permute-start | bytes 589832 | tf_op jit(solution)/shard_map/ppermute | solution.py:820
  207.7 8.2 %collective-permute-start.19 = (bf16[2,256,384]{2,1,0:T(8,128)(2,1)}, bf16[2,256,384]{2,1,0:T(8,128)(2,1)}, u32[]{:S(2)}, u32[]{:S(2)}) collective-permute-start(bf16[2,256,384]{2,1,0:T(8,128)(2,1)} %pad_maximum_fusion.9), channel_id=1, source_target_pairs={{0,2},{1,3},{2,0},{3,1},{4,6},{5,7},{6,4},{7,5},{8,10},{9,11},{10,... | collective-permute-start | bytes 1179656 | tf_op jit(solution)/shard_map/ppermute | solution.py:820
  213.8 94.3 %collective-permute-start.65 = (bf16[448,1472]{1,0:T(8,128)(2,1)}, bf16[448,1472]{1,0:T(8,128)(2,1)}, u32[]{:S(2)}, u32[]{:S(2)}) collective-permute-start(bf16[448,1472]{1,0:T(8,128)(2,1)} %copy.73), channel_id=1, source_target_pairs={{0,4},{1,5},{2,6},{3,7},{4,0},{5,1},{6,2},{7,3},{8,12},{9,13},{10,... | collective-permute-start | bytes 3956744 | tf_op jit(solution)/shard_map/ppermute | solution.py:820
  219.0 7.1 %collective-permute-start.20 = (bf16[256,384]{1,0:T(8,128)(2,1)}, bf16[256,384]{1,0:T(8,128)(2,1)}, u32[]{:S(2)}, u32[]{:S(2)}) collective-permute-start(bf16[256,384]{1,0:T(8,128)(2,1)} %get-tuple-element.189), channel_id=1, source_target_pairs={{0,1},{1,0},{2,3},{3,2},{4,5},{5,4},{6,7},{7,6},{8,9},{9,8},{10,11... | collective-permute-start | bytes 589832 | tf_op jit(solution)/shard_map/ppermute | solution.py:820
  224.6 95.8 %collective-permute-start.53 = (bf16[448,1472]{1,0:T(8,128)(2,1)}, bf16[448,1472]{1,0:T(8,128)(2,1)}, u32[]{:S(2)}, u32[]{:S(2)}) collective-permute-start(bf16[448,1472]{1,0:T(8,128)(2,1)} %copy.69), channel_id=1, source_target_pairs={{0,4},{1,5},{2,6},{3,7},{4,0},{5,1},{6,2},{7,3},{8,12},{9,13},{10,... | collective-permute-start | bytes 3956744 | tf_op jit(solution)/shard_map/ppermute | solution.py:820
  228.5 65.9 %collective-permute-start.29 = (bf16[256,512]{1,0:T(8,128)(2,1)}, bf16[256,512]{1,0:T(8,128)(2,1)}, u32[]{:S(2)}, u32[]{:S(2)}) collective-permute-start(bf16[256,512]{1,0:T(8,128)(2,1)} %attention_out_grad.1.refs_1_.refs_2_), channel_id=1, source_target_pairs={{0,2},{1,3},{2,0},{3,1},{4,6},{5,7},{6,4},{7,5},{8,10},{9,11},{10,... | collective-permute-start | bytes 786440 | tf_op jit(solution)/shard_map/ppermute | solution.py:820
  228.5 69.0 %collective-permute-start.42 = (bf16[256,512]{1,0:T(8,128)(2,1)}, bf16[256,512]{1,0:T(8,128)(2,1)}, u32[]{:S(2)}, u32[]{:S(2)}) collective-permute-start(bf16[256,512]{1,0:T(8,128)(2,1)} %attention_out_grad.1.refs_1_.refs_2_), channel_id=1, source_target_pairs={{2,4},{3,5},{4,2},{5,3},{6,8},{7,9},{8,6},{9,7},{10,12},{11,13},{1... | collective-permute-start | bytes 786440 | tf_op jit(solution)/shard_map/ppermute | solution.py:820
  294.4 40.2 %collective-permute-start.39 = (bf16[512,384]{1,0:T(8,128)(2,1)}, bf16[512,384]{1,0:T(8,128)(2,1)}, u32[]{:S(2)}, u32[]{:S(2)}) collective-permute-start(bf16[512,384]{1,0:T(8,128)(2,1)} %collective-permute-done.24.refs_2_.refs_3_), channel_id=1, source_target_pairs={{0,2},{1,3},{2,0},{3,1},{4,6},{5,7},{6,4},{7,5},{8,10},{9,11},{10,... | collective-permute-start | bytes 1179656 | tf_op jit(solution)/shard_map/ppermute | solution.py:820
  297.5 59.6 %collective-permute-start.37 = (bf16[512,384]{1,0:T(8,128)(2,1)}, bf16[512,384]{1,0:T(8,128)(2,1)}, u32[]{:S(2)}, u32[]{:S(2)}) collective-permute-start(bf16[512,384]{1,0:T(8,128)(2,1)} %collective-permute-done.25.refs_2_.refs_3_), channel_id=1, source_target_pairs={{0,2},{1,3},{2,0},{3,1},{4,6},{5,7},{6,4},{7,5},{8,10},{9,11},{10,... | collective-permute-start | bytes 1179656 | tf_op jit(solution)/shard_map/ppermute | solution.py:820
  297.5 25.4 %collective-permute-start.30 = (bf16[512,512]{1,0:T(8,128)(2,1)}, bf16[512,512]{1,0:T(8,128)(2,1)}, u32[]{:S(2)}, u32[]{:S(2)}) collective-permute-start(bf16[512,512]{1,0:T(8,128)(2,1)} %pad_maximum_fusion.7.refs_5_.refs_6_.refs_8_.refs_9_), channel_id=1, source_target_pairs={{0,8},{1,9},{2,6},{3,7},{4,0},{5,1},{6,14},{7,15},{8,16},{9,17},{1... | collective-permute-start | bytes 1572872 | tf_op jit(solution)/shard_map/ppermute | solution.py:820
  319.3 24.1 %collective-permute-start.66 = (bf16[2,112,1472]{2,1,0:T(8,128)(2,1)}, bf16[2,112,1472]{2,1,0:T(8,128)(2,1)}, u32[]{:S(2)}, u32[]{:S(2)}) collective-permute-start(bf16[2,112,1472]{2,1,0:T(8,128)(2,1)} %dynamic-slice_bitcast_fusion), channel_id=1, source_target_pairs={{0,1},{1,0},{2,3},{3,2},{4,5},{5,4},{6,7},{7,6},{8,9},{9,8},{10,11... | collective-permute-start | bytes 1978376 | tf_op jit(solution)/shard_map/ppermute | solution.py:820
  323.0 10.6 %collective-permute-start.31 = (bf16[512,512]{1,0:T(8,128)(2,1)}, bf16[512,512]{1,0:T(8,128)(2,1)}, u32[]{:S(2)}, u32[]{:S(2)}) collective-permute-start(bf16[512,512]{1,0:T(8,128)(2,1)} %collective-permute-done.30.refs_6_.refs_7_.refs_10_.refs_11_), channel_id=1, source_target_pairs={{0,8},{1,9},{2,6},{3,7},{4,0},{5,1},{6,14},{7,15},{8,16},{9,17},{1... | collective-permute-start | bytes 1572872 | tf_op jit(solution)/shard_map/ppermute | solution.py:820
  324.9 10.6 %collective-permute-start.40 = (bf16[512,512]{1,0:T(8,128)(2,1)}, bf16[512,512]{1,0:T(8,128)(2,1)}, u32[]{:S(2)}, u32[]{:S(2)}) collective-permute-start(bf16[512,512]{1,0:T(8,128)(2,1)} %collective-permute-done.30.refs_6_.refs_7_.refs_10_.refs_11_), channel_id=1, source_target_pairs={{0,2},{1,3},{2,0},{3,1},{4,6},{5,7},{6,4},{7,5},{8,10},{9,11},{10,... | collective-permute-start | bytes 1572872 | tf_op jit(solution)/shard_map/ppermute | solution.py:820
  333.5 12.6 %collective-permute-start.27 = (bf16[256,384]{1,0:T(8,128)(2,1)}, bf16[256,384]{1,0:T(8,128)(2,1)}, u32[]{:S(2)}, u32[]{:S(2)}) collective-permute-start(bf16[256,384]{1,0:T(8,128)(2,1)} %slice.317), channel_id=1, source_target_pairs={{0,8},{1,9},{2,6},{3,7},{4,0},{5,1},{6,14},{7,15},{8,16},{9,17},{1... | collective-permute-start | bytes 589832 | tf_op jit(solution)/shard_map/ppermute | solution.py:820
  334.6 18.1 %collective-permute-start.54 = (bf16[2,112,1472]{2,1,0:T(8,128)(2,1)}, bf16[2,112,1472]{2,1,0:T(8,128)(2,1)}, u32[]{:S(2)}, u32[]{:S(2)}) collective-permute-start(bf16[2,112,1472]{2,1,0:T(8,128)(2,1)} %dynamic-slice_bitcast_fusion.2), channel_id=1, source_target_pairs={{0,1},{1,0},{2,3},{3,2},{4,5},{5,4},{6,7},{7,6},{8,9},{9,8},{10,11... | collective-permute-start | bytes 1978376 | tf_op jit(solution)/shard_map/ppermute | solution.py:820
  335.5 19.4 %collective-permute-start.32 = (bf16[512,512]{1,0:T(8,128)(2,1)}, bf16[512,512]{1,0:T(8,128)(2,1)}, u32[]{:S(2)}, u32[]{:S(2)}) collective-permute-start(bf16[512,512]{1,0:T(8,128)(2,1)} %collective-permute-done.31.refs_6_.refs_7_.refs_10_.refs_11_), channel_id=1, source_target_pairs={{0,8},{1,9},{2,6},{3,7},{4,0},{5,1},{6,14},{7,15},{8,16},{9,17},{1... | collective-permute-start | bytes 1572872 | tf_op jit(solution)/shard_map/ppermute | solution.py:820
  343.4 13.7 %collective-permute-start.38 = (bf16[512,512]{1,0:T(8,128)(2,1)}, bf16[512,512]{1,0:T(8,128)(2,1)}, u32[]{:S(2)}, u32[]{:S(2)}) collective-permute-start(bf16[512,512]{1,0:T(8,128)(2,1)} %collective-permute-done.31.refs_6_.refs_7_.refs_10_.refs_11_), channel_id=1, source_target_pairs={{0,2},{1,3},{2,0},{3,1},{4,6},{5,7},{6,4},{7,5},{8,10},{9,11},{10,... | collective-permute-start | bytes 1572872 | tf_op jit(solution)/shard_map/ppermute | solution.py:820
  346.1 21.8 %collective-permute-start.35 = (bf16[512,384]{1,0:T(8,128)(2,1)}, bf16[512,384]{1,0:T(8,128)(2,1)}, u32[]{:S(2)}, u32[]{:S(2)}) collective-permute-start(bf16[512,384]{1,0:T(8,128)(2,1)} %collective-permute-done.26.refs_2_.refs_3_), channel_id=1, source_target_pairs={{0,2},{1,3},{2,0},{3,1},{4,6},{5,7},{6,4},{7,5},{8,10},{9,11},{10,... | collective-permute-start | bytes 1179656 | tf_op jit(solution)/shard_map/ppermute | solution.py:820
  352.7 27.1 %collective-permute-start.28 = (bf16[256,384]{1,0:T(8,128)(2,1)}, bf16[256,384]{1,0:T(8,128)(2,1)}, u32[]{:S(2)}, u32[]{:S(2)}) collective-permute-start(bf16[256,384]{1,0:T(8,128)(2,1)} %collective-permute-done.27.refs_2_), channel_id=1, source_target_pairs={{0,2},{1,3},{2,0},{3,1},{4,6},{5,7},{6,4},{7,5},{8,10},{9,11},{10,... | collective-permute-start | bytes 589832 | tf_op jit(solution)/shard_map/ppermute | solution.py:820
  354.9 68.4 %collective-permute-start.21 = (bf16[2,256,2944]{1,2,0:T(8,128)(2,1)}, bf16[2,256,2944]{1,2,0:T(8,128)(2,1)}, u32[]{:S(2)}, u32[]{:S(2)}) collective-permute-start(bf16[2,256,2944]{1,2,0:T(8,128)(2,1)} %pad_maximum_fusion.2), channel_id=1, source_target_pairs={{0,2},{1,3},{2,0},{3,1},{4,6},{5,7},{6,4},{7,5},{8,10},{9,11},{10,... | collective-permute-start | bytes 9043976 | tf_op jit(solution)/shard_map/ppermute | solution.py:820
  357.1 14.7 %collective-permute-start.36 = (bf16[512,512]{1,0:T(8,128)(2,1)}, bf16[512,512]{1,0:T(8,128)(2,1)}, u32[]{:S(2)}, u32[]{:S(2)}) collective-permute-start(bf16[512,512]{1,0:T(8,128)(2,1)} %collective-permute-done.32.refs_6_.refs_7_.refs_10_.refs_11_), channel_id=1, source_target_pairs={{0,2},{1,3},{2,0},{3,1},{4,6},{5,7},{6,4},{7,5},{8,10},{9,11},{10,... | collective-permute-start | bytes 1572872 | tf_op jit(solution)/shard_map/ppermute | solution.py:820
  357.1 7.9 %collective-permute-start.33 = (bf16[256,512]{1,0:T(8,128)(2,1)}, bf16[256,512]{1,0:T(8,128)(2,1)}, u32[]{:S(2)}, u32[]{:S(2)}) collective-permute-start(bf16[256,512]{1,0:T(8,128)(2,1)} %slice.260), channel_id=1, source_target_pairs={{0,8},{1,9},{2,6},{3,7},{4,0},{5,1},{6,14},{7,15},{8,16},{9,17},{1... | collective-permute-start | bytes 786440 | tf_op jit(solution)/shard_map/ppermute | solution.py:820
  365.1 16.8 %collective-permute-start.34 = (bf16[256,512]{1,0:T(8,128)(2,1)}, bf16[256,512]{1,0:T(8,128)(2,1)}, u32[]{:S(2)}, u32[]{:S(2)}) collective-permute-start(bf16[256,512]{1,0:T(8,128)(2,1)} %collective-permute-done.33.refs_4_.refs_6_), channel_id=1, source_target_pairs={{0,2},{1,3},{2,0},{3,1},{4,6},{5,7},{6,4},{7,5},{8,10},{9,11},{10,... | collective-permute-start | bytes 786440 | tf_op jit(solution)/shard_map/ppermute | solution.py:820
  367.9 53.1 %collective-permute-start.67 = (bf16[2,112,1472]{2,1,0:T(8,128)(2,1)}, bf16[2,112,1472]{2,1,0:T(8,128)(2,1)}, u32[]{:S(2)}, u32[]{:S(2)}) collective-permute-start(bf16[2,112,1472]{2,1,0:T(8,128)(2,1)} %get-tuple-element.123), channel_id=1, source_target_pairs={{0,8},{1,9},{2,10},{3,11},{4,12},{5,13},{6,14},{7,15},{24,16},{25,... | collective-permute-start | bytes 1978376 | tf_op jit(solution)/shard_map/ppermute | solution.py:820
  371.8 59.2 %collective-permute-start.59 = (bf16[448,1472]{1,0:T(8,128)(2,1)}, bf16[448,1472]{1,0:T(8,128)(2,1)}, u32[]{:S(2)}, u32[]{:S(2)}) collective-permute-start(bf16[448,1472]{1,0:T(8,128)(2,1)} %constant_dynamic-slice_fusion.1), channel_id=1, source_target_pairs={{0,4},{1,5},{2,6},{3,7},{4,0},{5,1},{6,2},{7,3},{8,12},{9,13},{10,... | collective-permute-start | bytes 3956744 | tf_op jit(solution)/shard_map/ppermute | solution.py:820
  379.8 47.8 %collective-permute-start.55 = (bf16[2,112,1472]{2,1,0:T(8,128)(2,1)}, bf16[2,112,1472]{2,1,0:T(8,128)(2,1)}, u32[]{:S(2)}, u32[]{:S(2)}) collective-permute-start(bf16[2,112,1472]{2,1,0:T(8,128)(2,1)} %get-tuple-element.118), channel_id=1, source_target_pairs={{0,8},{1,9},{2,10},{3,11},{4,12},{5,13},{6,14},{7,15},{24,16},{25,... | collective-permute-start | bytes 1978376 | tf_op jit(solution)/shard_map/ppermute | solution.py:820
  397.3 5.5 collective-permute-start.43
  422.5 7.1 %collective-permute-start.68 = (bf16[2,112,1472]{2,1,0:T(8,128)(2,1)S(1)}, bf16[2,112,1472]{2,1,0:T(8,128)(2,1)S(1)}, u32[]{:S(2)}, u32[]{:S(2)}) collective-permute-start(bf16[2,112,1472]{2,1,0:T(8,128)(2,1)S(1)} %add_convert_fusion.5), channel_id=1, source_target_pairs={{8,16},{9,17},{10,18},{11,19},{12,20},{13,21},{14,22},{15,23},{16,... | collective-permute-start | bytes 1978376 | tf_op jit(solution)/shard_map/ppermute | solution.py:820
  426.3 36.0 %collective-permute-start.22 = (bf16[256,2944]{0,1:T(8,128)(2,1)S(1)}, bf16[256,2944]{0,1:T(8,128)(2,1)S(1)}, u32[]{:S(2)}, u32[]{:S(2)}) collective-permute-start(bf16[256,2944]{0,1:T(8,128)(2,1)S(1)} %fusion.11), channel_id=1, source_target_pairs={{0,1},{1,0},{2,3},{3,2},{4,5},{5,4},{6,7},{7,6},{8,9},{9,8},{10,11... | collective-permute-start | bytes 4521992 | tf_op jit(solution)/shard_map/ppermute | solution.py:820
  428.9 39.2 %collective-permute-start.56 = (bf16[2,112,1472]{2,1,0:T(8,128)(2,1)S(1)}, bf16[2,112,1472]{2,1,0:T(8,128)(2,1)S(1)}, u32[]{:S(2)}, u32[]{:S(2)}) collective-permute-start(bf16[2,112,1472]{2,1,0:T(8,128)(2,1)S(1)} %add_convert_fusion.11), channel_id=1, source_target_pairs={{8,16},{9,17},{10,18},{11,19},{12,20},{13,21},{14,22},{15,23},{16,... | collective-permute-start | bytes 1978376 | tf_op jit(solution)/shard_map/ppermute | solution.py:820
  429.8 39.8 %collective-permute-start.69 = (bf16[2,112,1472]{2,1,0:T(8,128)(2,1)S(1)}, bf16[2,112,1472]{2,1,0:T(8,128)(2,1)S(1)}, u32[]{:S(2)}, u32[]{:S(2)}) collective-permute-start(bf16[2,112,1472]{2,1,0:T(8,128)(2,1)S(1)} %add_convert_fusion.4), channel_id=1, source_target_pairs={{2,10},{3,11},{6,14},{7,15},{8,0},{9,1},{12,4},{13,5},{18,26},{19,... | collective-permute-start | bytes 1978376 | tf_op jit(solution)/shard_map/ppermute | solution.py:820
  432.8 42.6 %collective-permute-start.60 = (bf16[2,112,1472]{2,1,0:T(8,128)(2,1)S(1)}, bf16[2,112,1472]{2,1,0:T(8,128)(2,1)S(1)}, u32[]{:S(2)}, u32[]{:S(2)}) collective-permute-start(bf16[2,112,1472]{2,1,0:T(8,128)(2,1)S(1)} %dynamic-slice_bitcast_fusion.1), channel_id=1, source_target_pairs={{0,1},{1,0},{2,3},{3,2},{4,5},{5,4},{6,7},{7,6},{8,9},{9,8},{10,11... | collective-permute-start | bytes 1978376 | tf_op jit(solution)/shard_map/ppermute | solution.py:820
  468.0 17.8 %collective-permute-start.48 = (bf16[8,192,736]{2,1,0:T(8,128)(2,1)S(1)}, bf16[8,192,736]{2,1,0:T(8,128)(2,1)S(1)}, u32[]{:S(2)}, u32[]{:S(2)}) collective-permute-start(bf16[8,192,736]{2,1,0:T(8,128)(2,1)S(1)} %fusion.61), channel_id=1, source_target_pairs={{0,2},{1,3},{2,0},{3,1},{4,6},{5,7},{6,4},{7,5},{8,10},{9,11},{10,... | collective-permute-start | bytes 6782984 | tf_op jit(solution)/shard_map/ppermute | solution.py:820
  468.3 12.8 %collective-permute-start.57 = (bf16[2,112,1472]{2,1,0:T(8,128)(2,1)S(1)}, bf16[2,112,1472]{2,1,0:T(8,128)(2,1)S(1)}, u32[]{:S(2)}, u32[]{:S(2)}) collective-permute-start(bf16[2,112,1472]{2,1,0:T(8,128)(2,1)S(1)} %add_convert_fusion.10), channel_id=1, source_target_pairs={{2,10},{3,11},{6,14},{7,15},{8,0},{9,1},{12,4},{13,5},{18,26},{19,... | collective-permute-start | bytes 1978376 | tf_op jit(solution)/shard_map/ppermute | solution.py:820
  469.8 23.8 %collective-permute-start.70 = (bf16[112,1472]{1,0:T(8,128)(2,1)S(1)}, bf16[112,1472]{1,0:T(8,128)(2,1)S(1)}, u32[]{:S(2)}, u32[]{:S(2)}) collective-permute-start(bf16[112,1472]{1,0:T(8,128)(2,1)S(1)} %dynamic-slice_bitcast_fusion.3), channel_id=1, source_target_pairs={{0,2},{1,3},{4,6},{5,7},{10,8},{11,9},{14,12},{15,13},{16,18},{17,... | collective-permute-start | bytes 989192 | tf_op jit(solution)/shard_map/ppermute | solution.py:820
  475.6 17.2 %collective-permute-start.61 = (bf16[2,112,1472]{2,1,0:T(8,128)(2,1)S(1)}, bf16[2,112,1472]{2,1,0:T(8,128)(2,1)S(1)}, u32[]{:S(2)}, u32[]{:S(2)}) collective-permute-start(bf16[2,112,1472]{2,1,0:T(8,128)(2,1)S(1)} %bitcast_select_fusion.2), channel_id=1, source_target_pairs={{0,8},{1,9},{2,10},{3,11},{4,12},{5,13},{6,14},{7,15},{24,16},{25,... | collective-permute-start | bytes 1978376 | tf_op jit(solution)/shard_map/ppermute | solution.py:820
  481.3 36.8 %collective-permute-start.58 = (bf16[112,1472]{1,0:T(8,128)(2,1)S(1)}, bf16[112,1472]{1,0:T(8,128)(2,1)S(1)}, u32[]{:S(2)}, u32[]{:S(2)}) collective-permute-start(bf16[112,1472]{1,0:T(8,128)(2,1)S(1)} %dynamic-slice_bitcast_fusion.5), channel_id=1, source_target_pairs={{0,2},{1,3},{4,6},{5,7},{10,8},{11,9},{14,12},{15,13},{16,18},{17,... | collective-permute-start | bytes 989192 | tf_op jit(solution)/shard_map/ppermute | solution.py:820
  487.6 27.3 %collective-permute-start.49 = (bf16[4,192,736]{2,1,0:T(8,128)(2,1)S(1)}, bf16[4,192,736]{2,1,0:T(8,128)(2,1)S(1)}, u32[]{:S(2)}, u32[]{:S(2)}) collective-permute-start(bf16[4,192,736]{2,1,0:T(8,128)(2,1)S(1)} %fusion.14), channel_id=1, source_target_pairs={{0,1},{1,0},{2,3},{3,2},{4,5},{5,4},{6,7},{7,6},{8,9},{9,8},{10,11... | collective-permute-start | bytes 3391496 | tf_op jit(solution)/shard_map/ppermute | solution.py:820
  492.9 23.6 %collective-permute-start.62 = (bf16[2,112,1472]{2,1,0:T(8,128)(2,1)S(1)}, bf16[2,112,1472]{2,1,0:T(8,128)(2,1)S(1)}, u32[]{:S(2)}, u32[]{:S(2)}) collective-permute-start(bf16[2,112,1472]{2,1,0:T(8,128)(2,1)S(1)} %add_convert_fusion.8), channel_id=1, source_target_pairs={{8,16},{9,17},{10,18},{11,19},{12,20},{13,21},{14,22},{15,23},{16,... | collective-permute-start | bytes 1978376 | tf_op jit(solution)/shard_map/ppermute | solution.py:820
  515.4 13.7 %collective-permute-start.50 = (bf16[4,96,736]{2,1,0:T(8,128)(2,1)S(1)}, bf16[4,96,736]{2,1,0:T(8,128)(2,1)S(1)}, u32[]{:S(2)}, u32[]{:S(2)}) collective-permute-start(bf16[4,96,736]{2,1,0:T(8,128)(2,1)S(1)} %constant_dynamic-slice_fusion.6), channel_id=1, source_target_pairs={{0,4},{1,5},{2,6},{3,7},{4,0},{5,1},{6,2},{7,3},{8,12},{9,13},{10,... | collective-permute-start | bytes 1695752 | tf_op jit(solution)/shard_map/ppermute | solution.py:820
  516.8 12.8 %collective-permute-start.63 = (bf16[2,112,1472]{2,1,0:T(8,128)(2,1)S(1)}, bf16[2,112,1472]{2,1,0:T(8,128)(2,1)S(1)}, u32[]{:S(2)}, u32[]{:S(2)}) collective-permute-start(bf16[2,112,1472]{2,1,0:T(8,128)(2,1)S(1)} %add_convert_fusion.7), channel_id=1, source_target_pairs={{2,10},{3,11},{6,14},{7,15},{8,0},{9,1},{12,4},{13,5},{18,26},{19,... | collective-permute-start | bytes 1978376 | tf_op jit(solution)/shard_map/ppermute | solution.py:820
  529.3 14.1 %collective-permute-start.51 = (bf16[4,48,736]{2,1,0:T(8,128)(2,1)S(1)}, bf16[4,48,736]{2,1,0:T(8,128)(2,1)S(1)}, u32[]{:S(2)}, u32[]{:S(2)}) collective-permute-start(bf16[4,48,736]{2,1,0:T(8,128)(2,1)S(1)} %constant_dynamic-slice_fusion.5), channel_id=1, source_target_pairs={{0,16},{1,17},{2,18},{3,19},{4,20},{5,21},{6,22},{7,23},{8,24},{9,... | collective-permute-start | bytes 847880 | tf_op jit(solution)/shard_map/ppermute | solution.py:820
  529.8 13.8 %collective-permute-start.64 = (bf16[112,1472]{1,0:T(8,128)(2,1)S(1)}, bf16[112,1472]{1,0:T(8,128)(2,1)S(1)}, u32[]{:S(2)}, u32[]{:S(2)}) collective-permute-start(bf16[112,1472]{1,0:T(8,128)(2,1)S(1)} %dynamic-slice_bitcast_fusion.4), channel_id=1, source_target_pairs={{0,2},{1,3},{4,6},{5,7},{10,8},{11,9},{14,12},{15,13},{16,18},{17,... | collective-permute-start | bytes 989192 | tf_op jit(solution)/shard_map/ppermute | solution.py:820
  543.6 5.2 collective-permute-start.52
  (82 other events, 1194.7 us)
